TPU v7x, 32 devices: a whole 2x2x4 slice. The times are simulated.
32 devices in a mesh: dom: 16 (over z, y, core), rep: 2 (over x).
Axes of the slice: x: 2, y: 2, z: 4, core: 2. Of those that a mesh axis runs over, the one named last changes fastest.
Arguments:
- features: bfloat16 [4096, 1024], P('dom'), may hold values from -6 to 6
- tiles: bfloat16 [2, 32, 12, 128, 128], P(None, 'dom'), may hold values from 0 to 2, as said below
- columns: int32 [2, 32, 12], P(None, 'dom'), may hold values from 0 to 31, as said below
- counts: int32 [2, 32], P(None, 'dom'), may hold values from 1 to 12, as said below
- degrees: int32 [2, 4096], P(None, 'dom'), may hold values from 16 to 64
- w_self: bfloat16 [1024, 1024], replicated, may hold values from -0.1875 to 0.1875
- w_in: bfloat16 [1024, 1024], replicated, may hold values from -1 to 1
- w_out: bfloat16 [1024, 1024], replicated, may hold values from -1 to 1
Outputs:
- layer_out: bfloat16 [4096, 1024], P('dom')
Inputs may be any that keep to these rules, and one draw needn't show every extreme that they name: Within one block-row the 12 block-columns are distinct; only the first counts slots are read. `counts`: in each relation some block-row has all 12 slots live. `tiles`: edge weights are zero or positive.
All inputs are finite; a program needn't handle non-finite values.
Results may differ from a plain program's by a relative error of at most 0.0038.
Values may be sent and summed in bfloat16 or wider, within the bound.
No kernel may reach another device: no remote copies, remote signals or barrier semaphores. Data moves between devices by JAX's collectives and lax.ppermute only.
A program may use at most 64 MiB of HBM per device.

v0:
```python
import jax
import jax.numpy as jnp
from jax import lax
from jax.sharding import PartitionSpec as P


def from_behind(block, axis, distance):
    devices = range(lax.axis_size(axis))
    route = [((i - distance) % len(devices), i) for i in devices]
    return lax.ppermute(block, axis, route)


def finish(summed, degree_rows, feature_rows, w_self, w_in, w_out):
    scaled = summed / degree_rows[:, :, None].astype(jnp.float32)
    agg_in = scaled[0].astype(jnp.bfloat16)
    agg_out = scaled[1].astype(jnp.bfloat16)
    hidden = jnp.dot(feature_rows, w_self, preferred_element_type=jnp.float32)
    hidden = hidden + jnp.dot(agg_in, w_in, preferred_element_type=jnp.float32)
    hidden = hidden + jnp.dot(agg_out, w_out, preferred_element_type=jnp.float32)
    return jax.nn.relu(hidden).astype(jnp.bfloat16)


def on_device(features, tiles, columns, counts, degrees, w_self, w_in, w_out):
    node_rows, feat_width = features.shape
    tile_size = tiles.shape[3]
    local_blocks = node_rows // tile_size
    cycle_size = lax.axis_size("dom")
    half_cycle = cycle_size // 2
    position = lax.axis_index("dom")
    replica = lax.axis_index("rep")
    slot_ids = jnp.arange(tiles.shape[2], dtype=jnp.int32)
    block_ids = jnp.arange(local_blocks, dtype=jnp.int32)
    live_slots = slot_ids[None, None, :] < counts[:, :, None]

    def absorb(running, feature_panel, source):
        targets = source * local_blocks + block_ids
        matches = (columns[:, :, None, :] == targets[None, None, :, None]) & live_slots[
            :, :, None, :
        ]
        present = jnp.any(matches, axis=-1)
        picks = jnp.sum(jnp.where(matches, slot_ids, 0), axis=-1)
        chosen = jnp.take_along_axis(tiles, picks[:, :, :, None, None], axis=2)
        chosen = jnp.where(present[:, :, :, None, None], chosen, jnp.zeros_like(chosen))
        panel_blocks = feature_panel.reshape(local_blocks, tile_size, feat_width)
        return running + jnp.einsum(
            "ricab,cbh->riah", chosen, panel_blocks, preferred_element_type=jnp.float32
        )

    running = jnp.zeros((2, local_blocks, tile_size, feat_width), jnp.float32)
    distant = from_behind(features, "dom", half_cycle)
    feature_panel = jnp.where(replica == 0, features, distant)
    anchor = (position - replica * half_cycle) % cycle_size

    def advance(turn, carry):
        sums_now, panel_now = carry
        sums_now = absorb(sums_now, panel_now, (anchor - turn) % cycle_size)
        panel_now = from_behind(panel_now, "dom", 1)
        return (sums_now, panel_now)

    running, feature_panel = lax.fori_loop(0, half_cycle - 1, advance, (running, feature_panel))
    running = absorb(running, feature_panel, (anchor - (half_cycle - 1)) % cycle_size)
    stacked = running.reshape(2, node_rows, feat_width)
    summed = lax.psum(stacked, "rep")
    return finish(summed, degrees, features, w_self, w_in, w_out)


def solution(mesh):
    placed = (
        P("dom", None),
        P(None, "dom", None, None, None),
        P(None, "dom", None),
        P(None, "dom"),
        P(None, "dom"),
        P(),
        P(),
        P(),
    )
    return jax.shard_map(
        on_device, mesh=mesh, in_specs=placed, out_specs=P("dom", None), check_vma=False
    )
```

profile of v0, /device:TPU:0, one launch (start us, length us, event | category | flops | bytes accessed | tf_op | source)
XLA Modules:
  0.0 189.8 jit_solution(7590709612621748421)
XLA Ops:
  6.5 4.1 %collective-permute-start.1 = (bf16[256,1024]{1,0:T(8,128)(2,1)}, bf16[256,1024]{1,0:T(8,128)(2,1)S(1)}, u32[]{:S(2)}, u32[]{:S(2)}) collective-permute-start(bf16[256,1024]{1,0:T(8,128)(2,1)} %param.12), channel_id=1, source_target_pairs={{16,0},{18,2},{20,4},{22,6},{24,8},{26,10},{28,12},{30,14},{0,16},... | collective-permute-start | bytes 1572872 | tf_op jit(solution)/shard_map/ppermute | solution.py:10
  10.7 0.8 iota_compare_fusion.1
  11.4 0.9 fusion.24
  12.3 0.1 reshape.89
  12.4 2.7 %gather_fusion.1 = bf16[8,128,128]{2,1,0:T(8,128)(2,1)} fusion(bf16[2,2,12,128,128]{4,3,2,1,0:T(8,128)(2,1)} %param.13, s32[8]{0:T(128)S(1)} %reshape.89), kind=kCustom, calls=%fused_computation.1.clone | custom fusion | bytes 524384 | tf_op jit(solution)/shard_map/jit(take_along_axis)/gather | solution.py:42
  15.1 0.9 fusion.23
  16.0 18.0 %collective-permute-done.1 = bf16[256,1024]{1,0:T(8,128)(2,1)S(1)} collective-permute-done((bf16[256,1024]{1,0:T(8,128)(2,1)}, bf16[256,1024]{1,0:T(8,128)(2,1)S(1)}, u32[]{:S(2)}, u32[]{:S(2)}) %collective-permute-start.1) | collective-permute-done | bytes 524320 | tf_op jit(solution)/shard_map/ppermute | solution.py:10
  34.0 1.1 broadcast_select_fusion
  35.1 79.8 %while.18 = (s32[]{:T(128)}, f32[2,2,128,1024]{3,2,1,0:T(8,128)}, bf16[256,1024]{1,0:T(8,128)(2,1)S(1)}, s32[2,2,12]{2,1,0:T(2,128)S(1)}, s32[]{:T(128)}, /*inde...) while((s32[]{:T(128)}, f32[2,2,128,1024]{3,2,1,0:T(8,128)}, ...), condition=%wide.region_3.5_spmd.clone, body=%wide.region_0.4_spmd.clone.sunk | while | flops 269747040 | bytes 8651944 | solution.py:60
  35.3 0.1 iota_compare_fusion.3
  35.4 0.2 fusion.38
  35.6 0.2 fusion.39
  35.8 0.1 reshape.102
  35.9 2.0 %gather_fusion = bf16[8,128,128]{2,1,0:T(8,128)(2,1)S(1)} fusion(bf16[2,2,12,128,128]{4,3,2,1,0:T(8,128)(2,1)} %get-tuple-element.347, s32[8]{0:T(128)S(1)} %reshape.102), kind=kCustom, calls=%fused_computation.clone.clone.1 | custom fusion | bytes 524384 | tf_op jit(solution)/shard_map/while/body/eval_jaxpr/jit(take_along_axis)/gather | solution.py:42
  37.9 1.8 bitcast_add_fusion.3
  39.8 6.8 %collective-permute-done = bf16[256,1024]{1,0:T(8,128)(2,1)S(1)} collective-permute-done((bf16[256,1024]{1,0:T(8,128)(2,1)S(1)}, bf16[256,1024]{1,0:T(8,128)(2,1)S(1)}, u32[]{:S(2)}, u32[]{:S(2)}) %collective-permute-start) | collective-permute-done | bytes 524320 | tf_op jit(solution)/shard_map/while/body/eval_jaxpr/ppermute | solution.py:10
  46.8 0.2 fusion.38
  47.0 0.2 fusion.39
  47.2 0.1 reshape.102
  47.3 2.0 %gather_fusion = bf16[8,128,128]{2,1,0:T(8,128)(2,1)S(1)} fusion(bf16[2,2,12,128,128]{4,3,2,1,0:T(8,128)(2,1)} %get-tuple-element.347, s32[8]{0:T(128)S(1)} %reshape.102), kind=kCustom, calls=%fused_computation.clone.clone.1 | custom fusion | bytes 524384 | tf_op jit(solution)/shard_map/while/body/eval_jaxpr/jit(take_along_axis)/gather | solution.py:42
  49.3 3.4 %bitcast_add_fusion.3 = f32[2,2,128,1024]{3,2,1,0:T(8,128)} fusion(f32[2,2,128,1024]{3,2,1,0:T(8,128)} %get-tuple-element.331, bf16[2,128,1024,1,1]{2,1,0,4,3:T(8,128)(2,1)S(1)} %bitcast.71, pred[]{:T(512)S(6)} %compare.6, bf16[2,2,2,128,128]{4,3,2,1,0:T(8,128)(2,1)S(1)} %bitcast.72, pred[2,2,2]{2,1,0:T(4,128)(4,1)S(1)} %and_bitcast_fusion.3, ...), kind=kOutput, calls=%fused_computation.5.clone.1 | convolution fusion | flops 269746176 | bytes 4980753 | tf_op jit(solution)/shard_map/while/body/eval_jaxpr/ricab,cbh->riah/dot_general | solution.py:45
  52.8 5.2 %collective-permute-done = bf16[256,1024]{1,0:T(8,128)(2,1)S(1)} collective-permute-done((bf16[256,1024]{1,0:T(8,128)(2,1)S(1)}, bf16[256,1024]{1,0:T(8,128)(2,1)S(1)}, u32[]{:S(2)}, u32[]{:S(2)}) %collective-permute-start) | collective-permute-done | bytes 524320 | tf_op jit(solution)/shard_map/while/body/eval_jaxpr/ppermute | solution.py:10
  58.2 0.2 fusion.38
  58.4 0.2 fusion.39
  58.6 0.1 reshape.102
  58.7 2.0 %gather_fusion = bf16[8,128,128]{2,1,0:T(8,128)(2,1)S(1)} fusion(bf16[2,2,12,128,128]{4,3,2,1,0:T(8,128)(2,1)} %get-tuple-element.347, s32[8]{0:T(128)S(1)} %reshape.102), kind=kCustom, calls=%fused_computation.clone.clone.1 | custom fusion | bytes 524384 | tf_op jit(solution)/shard_map/while/body/eval_jaxpr/jit(take_along_axis)/gather | solution.py:42
  60.7 3.4 %bitcast_add_fusion.3 = f32[2,2,128,1024]{3,2,1,0:T(8,128)} fusion(f32[2,2,128,1024]{3,2,1,0:T(8,128)} %get-tuple-element.331, bf16[2,128,1024,1,1]{2,1,0,4,3:T(8,128)(2,1)S(1)} %bitcast.71, pred[]{:T(512)S(6)} %compare.6, bf16[2,2,2,128,128]{4,3,2,1,0:T(8,128)(2,1)S(1)} %bitcast.72, pred[2,2,2]{2,1,0:T(4,128)(4,1)S(1)} %and_bitcast_fusion.3, ...), kind=kOutput, calls=%fused_computation.5.clone.1 | convolution fusion | flops 269746176 | bytes 4980753 | tf_op jit(solution)/shard_map/while/body/eval_jaxpr/ricab,cbh->riah/dot_general | solution.py:45
  64.2 5.2 %collective-permute-done = bf16[256,1024]{1,0:T(8,128)(2,1)S(1)} collective-permute-done((bf16[256,1024]{1,0:T(8,128)(2,1)S(1)}, bf16[256,1024]{1,0:T(8,128)(2,1)S(1)}, u32[]{:S(2)}, u32[]{:S(2)}) %collective-permute-start) | collective-permute-done | bytes 524320 | tf_op jit(solution)/shard_map/while/body/eval_jaxpr/ppermute | solution.py:10
  69.6 0.2 fusion.38
  69.8 0.2 fusion.39
  70.0 0.1 reshape.102
  70.1 2.0 %gather_fusion = bf16[8,128,128]{2,1,0:T(8,128)(2,1)S(1)} fusion(bf16[2,2,12,128,128]{4,3,2,1,0:T(8,128)(2,1)} %get-tuple-element.347, s32[8]{0:T(128)S(1)} %reshape.102), kind=kCustom, calls=%fused_computation.clone.clone.1 | custom fusion | bytes 524384 | tf_op jit(solution)/shard_map/while/body/eval_jaxpr/jit(take_along_axis)/gather | solution.py:42
  72.1 3.4 %bitcast_add_fusion.3 = f32[2,2,128,1024]{3,2,1,0:T(8,128)} fusion(f32[2,2,128,1024]{3,2,1,0:T(8,128)} %get-tuple-element.331, bf16[2,128,1024,1,1]{2,1,0,4,3:T(8,128)(2,1)S(1)} %bitcast.71, pred[]{:T(512)S(6)} %compare.6, bf16[2,2,2,128,128]{4,3,2,1,0:T(8,128)(2,1)S(1)} %bitcast.72, pred[2,2,2]{2,1,0:T(4,128)(4,1)S(1)} %and_bitcast_fusion.3, ...), kind=kOutput, calls=%fused_computation.5.clone.1 | convolution fusion | flops 269746176 | bytes 4980753 | tf_op jit(solution)/shard_map/while/body/eval_jaxpr/ricab,cbh->riah/dot_general | solution.py:45
  75.6 5.2 %collective-permute-done = bf16[256,1024]{1,0:T(8,128)(2,1)S(1)} collective-permute-done((bf16[256,1024]{1,0:T(8,128)(2,1)S(1)}, bf16[256,1024]{1,0:T(8,128)(2,1)S(1)}, u32[]{:S(2)}, u32[]{:S(2)}) %collective-permute-start) | collective-permute-done | bytes 524320 | tf_op jit(solution)/shard_map/while/body/eval_jaxpr/ppermute | solution.py:10
  80.9 0.2 fusion.38
  81.2 0.2 fusion.39
  81.4 0.1 reshape.102
  81.5 2.0 %gather_fusion = bf16[8,128,128]{2,1,0:T(8,128)(2,1)S(1)} fusion(bf16[2,2,12,128,128]{4,3,2,1,0:T(8,128)(2,1)} %get-tuple-element.347, s32[8]{0:T(128)S(1)} %reshape.102), kind=kCustom, calls=%fused_computation.clone.clone.1 | custom fusion | bytes 524384 | tf_op jit(solution)/shard_map/while/body/eval_jaxpr/jit(take_along_axis)/gather | solution.py:42
  83.5 3.4 %bitcast_add_fusion.3 = f32[2,2,128,1024]{3,2,1,0:T(8,128)} fusion(f32[2,2,128,1024]{3,2,1,0:T(8,128)} %get-tuple-element.331, bf16[2,128,1024,1,1]{2,1,0,4,3:T(8,128)(2,1)S(1)} %bitcast.71, pred[]{:T(512)S(6)} %compare.6, bf16[2,2,2,128,128]{4,3,2,1,0:T(8,128)(2,1)S(1)} %bitcast.72, pred[2,2,2]{2,1,0:T(4,128)(4,1)S(1)} %and_bitcast_fusion.3, ...), kind=kOutput, calls=%fused_computation.5.clone.1 | convolution fusion | flops 269746176 | bytes 4980753 | tf_op jit(solution)/shard_map/while/body/eval_jaxpr/ricab,cbh->riah/dot_general | solution.py:45
  87.0 5.2 %collective-permute-done = bf16[256,1024]{1,0:T(8,128)(2,1)S(1)} collective-permute-done((bf16[256,1024]{1,0:T(8,128)(2,1)S(1)}, bf16[256,1024]{1,0:T(8,128)(2,1)S(1)}, u32[]{:S(2)}, u32[]{:S(2)}) %collective-permute-start) | collective-permute-done | bytes 524320 | tf_op jit(solution)/shard_map/while/body/eval_jaxpr/ppermute | solution.py:10
  92.3 0.2 fusion.38
  92.6 0.2 fusion.39
  92.8 0.1 reshape.102
  92.9 2.0 %gather_fusion = bf16[8,128,128]{2,1,0:T(8,128)(2,1)S(1)} fusion(bf16[2,2,12,128,128]{4,3,2,1,0:T(8,128)(2,1)} %get-tuple-element.347, s32[8]{0:T(128)S(1)} %reshape.102), kind=kCustom, calls=%fused_computation.clone.clone.1 | custom fusion | bytes 524384 | tf_op jit(solution)/shard_map/while/body/eval_jaxpr/jit(take_along_axis)/gather | solution.py:42
  94.9 3.4 %bitcast_add_fusion.3 = f32[2,2,128,1024]{3,2,1,0:T(8,128)} fusion(f32[2,2,128,1024]{3,2,1,0:T(8,128)} %get-tuple-element.331, bf16[2,128,1024,1,1]{2,1,0,4,3:T(8,128)(2,1)S(1)} %bitcast.71, pred[]{:T(512)S(6)} %compare.6, bf16[2,2,2,128,128]{4,3,2,1,0:T(8,128)(2,1)S(1)} %bitcast.72, pred[2,2,2]{2,1,0:T(4,128)(4,1)S(1)} %and_bitcast_fusion.3, ...), kind=kOutput, calls=%fused_computation.5.clone.1 | convolution fusion | flops 269746176 | bytes 4980753 | tf_op jit(solution)/shard_map/while/body/eval_jaxpr/ricab,cbh->riah/dot_general | solution.py:45
  98.4 5.2 %collective-permute-done = bf16[256,1024]{1,0:T(8,128)(2,1)S(1)} collective-permute-done((bf16[256,1024]{1,0:T(8,128)(2,1)S(1)}, bf16[256,1024]{1,0:T(8,128)(2,1)S(1)}, u32[]{:S(2)}, u32[]{:S(2)}) %collective-permute-start) | collective-permute-done | bytes 524320 | tf_op jit(solution)/shard_map/while/body/eval_jaxpr/ppermute | solution.py:10
  103.7 0.1 iota_compare_fusion.3
  103.7 0.2 fusion.38
  104.0 0.2 fusion.39
  104.2 0.1 reshape.102
  104.3 2.0 %gather_fusion = bf16[8,128,128]{2,1,0:T(8,128)(2,1)S(1)} fusion(bf16[2,2,12,128,128]{4,3,2,1,0:T(8,128)(2,1)} %get-tuple-element.347, s32[8]{0:T(128)S(1)} %reshape.102), kind=kCustom, calls=%fused_computation.clone.clone.1 | custom fusion | bytes 524384 | tf_op jit(solution)/shard_map/while/body/eval_jaxpr/jit(take_along_axis)/gather | solution.py:42
  106.3 3.4 %bitcast_add_fusion.3 = f32[2,2,128,1024]{3,2,1,0:T(8,128)} fusion(f32[2,2,128,1024]{3,2,1,0:T(8,128)} %get-tuple-element.331, bf16[2,128,1024,1,1]{2,1,0,4,3:T(8,128)(2,1)S(1)} %bitcast.71, pred[]{:T(512)S(6)} %compare.6, bf16[2,2,2,128,128]{4,3,2,1,0:T(8,128)(2,1)S(1)} %bitcast.72, pred[2,2,2]{2,1,0:T(4,128)(4,1)S(1)} %and_bitcast_fusion.3, ...), kind=kOutput, calls=%fused_computation.5.clone.1 | convolution fusion | flops 269746176 | bytes 4980753 | tf_op jit(solution)/shard_map/while/body/eval_jaxpr/ricab,cbh->riah/dot_general | solution.py:45
  109.7 5.2 %collective-permute-done = bf16[256,1024]{1,0:T(8,128)(2,1)S(1)} collective-permute-done((bf16[256,1024]{1,0:T(8,128)(2,1)S(1)}, bf16[256,1024]{1,0:T(8,128)(2,1)S(1)}, u32[]{:S(2)}, u32[]{:S(2)}) %collective-permute-start) | collective-permute-done | bytes 524320 | tf_op jit(solution)/shard_map/while/body/eval_jaxpr/ppermute | solution.py:10
  114.9 1.6 fusion.17
  116.5 0.1 copy-done.1
  116.6 1.7 bitcast_add_fusion.1
  118.3 0.7 copy-done.6
  119.0 1.8 fusion.27
  120.8 56.9 %all-reduce.2.cloned.1.call-done = f32[2,256,1024]{2,1,0:T(8,128)} async-done(((f32[2,256,1024]{2,1,0:T(8,128)}), f32[2,256,1024]{2,1,0:T(8,128)}) %all-reduce.2.cloned.1.call-update) | async-done | bytes 2097168 | tf_op jit(solution)/shard_map/psum | solution.py:63
  177.6 2.0 %divide_convert_fusion = bf16[2,256,1024]{2,1,0:T(8,128)(2,1)S(1)} fusion(f32[2,256,1024]{2,1,0:T(8,128)} %all-reduce.2.cloned.1.call-done, f32[2,256]{1,0:T(2,128)S(1)} %convert_element_type.15), kind=kLoop, calls=%fused_computation.23 | loop fusion | flops 1048576 | bytes 3147776 | tf_op jit(solution)/shard_map/convert.1
  179.7 0.2 copy-done.2
  179.9 0.7 convolution_add_fusion.1
  180.6 0.8 copy-done.3
  181.4 1.5 fusion.16
  (57 shorter events, 1.2 us)
Async XLA Ops:
  6.5 112.4 %copy-start = (bf16[1024,1024]{1,0:T(8,128)(2,1)S(1)}, bf16[1024,1024]{1,0:T(8,128)(2,1)}, u32[]{:S(2)}) copy-start(bf16[1024,1024]{1,0:T(8,128)(2,1)} %param.17) | copy-start | bytes 6291460
  6.5 28.6 %copy-start.5 = (s32[2,2]{1,0:T(2,128)S(1)}, s32[2,2]{1,0:T(2,128)}, u32[]{:S(2)}) copy-start(s32[2,2]{1,0:T(2,128)} %param.15) | copy-start | bytes 52
  6.5 28.6 %copy-start.4 = (s32[2,2,12]{2,1,0:T(2,128)S(1)}, s32[2,2,12]{2,1,0:T(2,128)}, u32[]{:S(2)}) copy-start(s32[2,2,12]{2,1,0:T(2,128)} %param.14) | copy-start | bytes 580
  6.5 171.1 %all-reduce.2.cloned.1.call-start = ((), (), s32[]{:S(2)}) async-start(), calls=%async_computation | async-start | bytes 4194304 | tf_op jit(solution)/shard_map/psum | solution.py:63
  6.5 27.5 %collective-permute-start.1 = (bf16[256,1024]{1,0:T(8,128)(2,1)}, bf16[256,1024]{1,0:T(8,128)(2,1)S(1)}, u32[]{:S(2)}, u32[]{:S(2)}) collective-permute-start(bf16[256,1024]{1,0:T(8,128)(2,1)} %param.12), channel_id=1, source_target_pairs={{16,0},{18,2},{20,4},{22,6},{24,8},{26,10},{28,12},{30,14},{0,16},... | collective-permute-start | bytes 1572872 | tf_op jit(solution)/shard_map/ppermute | solution.py:10
  35.2 11.4 %collective-permute-start = (bf16[256,1024]{1,0:T(8,128)(2,1)S(1)}, bf16[256,1024]{1,0:T(8,128)(2,1)S(1)}, u32[]{:S(2)}, u32[]{:S(2)}) collective-permute-start(bf16[256,1024]{1,0:T(8,128)(2,1)S(1)} %copy.18), channel_id=1, source_target_pairs={{30,0},{0,2},{2,4},{4,6},{6,8},{8,10},{10,12},{12,14},{14,16},{16,... | collective-permute-start | bytes 1572872 | tf_op jit(solution)/shard_map/while/body/eval_jaxpr/ppermute | solution.py:10
  46.6 11.4 %collective-permute-start = (bf16[256,1024]{1,0:T(8,128)(2,1)S(1)}, bf16[256,1024]{1,0:T(8,128)(2,1)S(1)}, u32[]{:S(2)}, u32[]{:S(2)}) collective-permute-start(bf16[256,1024]{1,0:T(8,128)(2,1)S(1)} %copy.18), channel_id=1, source_target_pairs={{30,0},{0,2},{2,4},{4,6},{6,8},{8,10},{10,12},{12,14},{14,16},{16,... | collective-permute-start | bytes 1572872 | tf_op jit(solution)/shard_map/while/body/eval_jaxpr/ppermute | solution.py:10
  58.0 11.4 %collective-permute-start = (bf16[256,1024]{1,0:T(8,128)(2,1)S(1)}, bf16[256,1024]{1,0:T(8,128)(2,1)S(1)}, u32[]{:S(2)}, u32[]{:S(2)}) collective-permute-start(bf16[256,1024]{1,0:T(8,128)(2,1)S(1)} %copy.18), channel_id=1, source_target_pairs={{30,0},{0,2},{2,4},{4,6},{6,8},{8,10},{10,12},{12,14},{14,16},{16,... | collective-permute-start | bytes 1572872 | tf_op jit(solution)/shard_map/while/body/eval_jaxpr/ppermute | solution.py:10
  69.4 11.4 %collective-permute-start = (bf16[256,1024]{1,0:T(8,128)(2,1)S(1)}, bf16[256,1024]{1,0:T(8,128)(2,1)S(1)}, u32[]{:S(2)}, u32[]{:S(2)}) collective-permute-start(bf16[256,1024]{1,0:T(8,128)(2,1)S(1)} %copy.18), channel_id=1, source_target_pairs={{30,0},{0,2},{2,4},{4,6},{6,8},{8,10},{10,12},{12,14},{14,16},{16,... | collective-permute-start | bytes 1572872 | tf_op jit(solution)/shard_map/while/body/eval_jaxpr/ppermute | solution.py:10
  80.8 11.4 %collective-permute-start = (bf16[256,1024]{1,0:T(8,128)(2,1)S(1)}, bf16[256,1024]{1,0:T(8,128)(2,1)S(1)}, u32[]{:S(2)}, u32[]{:S(2)}) collective-permute-start(bf16[256,1024]{1,0:T(8,128)(2,1)S(1)} %copy.18), channel_id=1, source_target_pairs={{30,0},{0,2},{2,4},{4,6},{6,8},{8,10},{10,12},{12,14},{14,16},{16,... | collective-permute-start | bytes 1572872 | tf_op jit(solution)/shard_map/while/body/eval_jaxpr/ppermute | solution.py:10
  92.2 11.4 %collective-permute-start = (bf16[256,1024]{1,0:T(8,128)(2,1)S(1)}, bf16[256,1024]{1,0:T(8,128)(2,1)S(1)}, u32[]{:S(2)}, u32[]{:S(2)}) collective-permute-start(bf16[256,1024]{1,0:T(8,128)(2,1)S(1)} %copy.18), channel_id=1, source_target_pairs={{30,0},{0,2},{2,4},{4,6},{6,8},{8,10},{10,12},{12,14},{14,16},{16,... | collective-permute-start | bytes 1572872 | tf_op jit(solution)/shard_map/while/body/eval_jaxpr/ppermute | solution.py:10
  103.6 11.4 %collective-permute-start = (bf16[256,1024]{1,0:T(8,128)(2,1)S(1)}, bf16[256,1024]{1,0:T(8,128)(2,1)S(1)}, u32[]{:S(2)}, u32[]{:S(2)}) collective-permute-start(bf16[256,1024]{1,0:T(8,128)(2,1)S(1)} %copy.18), channel_id=1, source_target_pairs={{30,0},{0,2},{2,4},{4,6},{6,8},{8,10},{10,12},{12,14},{14,16},{16,... | collective-permute-start | bytes 1572872 | tf_op jit(solution)/shard_map/while/body/eval_jaxpr/ppermute | solution.py:10
  114.9 1.7 copy-start.1
  118.3 0.7 copy-start.6
  177.6 2.2 %copy-start.2 = (bf16[1024,1024]{1,0:T(8,128)(2,1)S(1)}, bf16[1024,1024]{1,0:T(8,128)(2,1)}, u32[]{:S(2)}) copy-start(bf16[1024,1024]{1,0:T(8,128)(2,1)} %param.18) | copy-start | bytes 6291460
  179.9 1.6 copy-start.3
Sparse Core Ops, SparseCore 0:
  118.4 59.1 all-reduce.1
where the time goes:
time: 191 us; the launch traced here: 190 us
  waiting for transfers between devices  113 us (59%)
  matrix products  28.1 us (15%)
  local copies, waits for them, and re-layouts  19.5 us (10%)
  between operations  13.5 us (7%)
  other arithmetic  11.1 us (6%)
  starting transfers between devices  4.51 us (2%)
    psum x1, waiting for transfers between devices, on_device(): summed = lax.psum(stacked, 'rep')  56.9 us
    ppermute x8, waiting for transfers between devices, from_behind(): return lax.ppermute(block, axis, route)  55.8 us
    dot_general x8, matrix products, absorb(): jnp.einsum('ricab,cbh->riah', chosen, panel_blocks, preferred_element_typ...  24 us
    gather x16, local copies, waits for them, and re-layouts, absorb(): chosen = jnp.take_along_axis(tiles, picks[:, :, :, None, None], axis=2)  17.5 us
    ppermute x8, starting transfers between devices, from_behind(): return lax.ppermute(block, axis, route)  4.51 us
  transfers between devices with their start and end apart: 9, of which 9 were waited for; matrix products, arithmetic and copies ran while one was open for 25% of the time, Pallas kernels for 0%

commit v1 on v0

v1 whole, which is shorter than its diff:
```python
import functools

import jax
import jax.numpy as jnp
from jax import lax
from jax.experimental import pallas as pl
from jax.experimental.pallas import tpu as pltpu
from jax.sharding import PartitionSpec as P

F32 = jnp.float32
BF16 = jnp.bfloat16


def chip_ring(chips):
    half = chips // 2
    return [2 * o for o in range(half)] + [2 * o + 1 for o in reversed(range(half))]


def ring_route(devices, distance):
    ring = chip_ring(devices // 2)
    size = len(ring)
    route = []
    for place, chip in enumerate(ring):
        target = ring[(place + distance) % size]
        route += [(2 * chip + core, 2 * target + core) for core in range(2)]
    return sorted(route)


def core_route(devices):
    return [(d, d ^ 1) for d in range(devices)]


def chip_at(place, chips):
    place = lax.rem(place + 2 * chips, chips)
    return jnp.where(place < chips // 2, 2 * place, 2 * (chips - 1 - place) + 1)


def place_of(chip, chips):
    side = lax.rem(chip, 2)
    rung = chip // 2
    return jnp.where(side == 0, rung, chips - 1 - rung)


def gather_ring(own, sibling, devices):
    chips = devices // 2
    ahead, behind = ring_route(devices, 1), ring_route(devices, -1)
    pieces = [(own, 0, 0), (sibling, 0, 1)]
    forward = [own, sibling]
    backward = [own, sibling]
    for step in range(1, (chips - 1) // 2 + 1):
        forward[0] = lax.ppermute(forward[0], "dom", ahead)
        backward[0] = lax.ppermute(backward[0], "dom", behind)
        forward[1] = lax.ppermute(forward[1], "dom", ahead)
        backward[1] = lax.ppermute(backward[1], "dom", behind)
        pieces += [(forward[0], -step, 0), (backward[0], step, 0)]
        pieces += [(forward[1], -step, 1), (backward[1], step, 1)]
    if chips % 2 == 0:
        far = chips // 2
        pieces.append((lax.ppermute(forward[0], "dom", ahead), far, 0))
        pieces.append((lax.ppermute(backward[1], "dom", behind), far, 1))
    return pieces


def aggregate_body(origins, slots, chips, *refs):
    count = len(origins)
    columns_own, columns_sib = refs[:2]
    tiles_own, tiles_sib, degrees_own, degrees_sib = refs[2:6]
    piece_refs = refs[6 : 6 + count]
    out_own, out_sib, blocks = refs[6 + count :]
    rows = piece_refs[0].shape[0]
    width = piece_refs[0].shape[1]
    tile = tiles_own.shape[-1]
    position = lax.axis_index("dom")
    core = lax.rem(position, 2)
    place = place_of(position // 2, chips)
    for ref, (offset, other) in zip(piece_refs, origins):
        chip = chip_at(place + offset, chips)
        source = 2 * chip + (1 - core if other else core)
        blocks[pl.ds(pl.multiple_of(source * rows, rows), rows), :] = ref[...]
    local = rows // tile
    for columns, tiles, degrees, out in (
        (columns_own, tiles_own, degrees_own, out_own),
        (columns_sib, tiles_sib, degrees_sib, out_sib),
    ):
        for relation in range(2):
            for row in range(local):
                live_count = columns[relation, row, slots]

                def one(slot, total):
                    live = slot < live_count
                    column = jnp.where(live, columns[relation, row, slot], 0)
                    weights = tiles[relation, row, slot]
                    weights = jnp.where(live, weights, jnp.zeros_like(weights))
                    panel = blocks[pl.ds(pl.multiple_of(column * tile, tile), tile), :]
                    return total + jnp.dot(weights, panel, preferred_element_type=F32)

                total = lax.fori_loop(0, slots, one, jnp.zeros((tile, width), F32), unroll=12)
                degree = degrees[relation : relation + 1, row * tile : (row + 1) * tile].astype(F32)
                degree = jnp.broadcast_to(degree, (tile, tile)).T
                span = slice(row * tile, (row + 1) * tile)
                for start in range(0, width, tile):
                    part = total[:, start : start + tile] / degree
                    out[relation, span, start : start + tile] = part.astype(BF16)


def aggregate(pieces, columns, tiles, degrees, devices):
    rows, width = pieces[0][0].shape
    slots = tiles[0].shape[2]
    origins = tuple((offset, other) for _, offset, other in pieces)
    smem = pl.BlockSpec(memory_space=pltpu.SMEM)
    vmem = pl.BlockSpec(memory_space=pltpu.VMEM)
    out = jax.ShapeDtypeStruct((2, rows, width), BF16)
    return pl.pallas_call(
        functools.partial(aggregate_body, origins, slots, devices // 2),
        out_shape=[out, out],
        in_specs=[smem] * 2 + [vmem] * (4 + len(pieces)),
        out_specs=[vmem] * 2,
        scratch_shapes=[pltpu.VMEM((devices * rows, width), BF16)],
        compiler_params=pltpu.CompilerParams(vmem_limit_bytes=48 * 2**20),
        name="aggregate",
    )(*columns, *tiles, *degrees, *[piece for piece, _, _ in pieces])


def project_body(base, own, core_side, twin, diagonal, w_in, w_out, out):
    rep = lax.axis_index("rep")
    core = lax.rem(lax.axis_index("dom"), 2)
    width = own.shape[2]
    total = base[...]
    for part, quarter in (
        (own, 2 * rep + core),
        (core_side, 2 * rep + 1 - core),
        (twin, 2 * (1 - rep) + core),
        (diagonal, 2 * (1 - rep) + 1 - core),
    ):
        span = pl.ds(pl.multiple_of(quarter * width, width), width)
        total = total + jnp.dot(part[0], w_in[span, :], preferred_element_type=F32)
        total = total + jnp.dot(part[1], w_out[span, :], preferred_element_type=F32)
    out[...] = jnp.maximum(total, 0.0).astype(BF16)


def project(base, parts, w_in, w_out):
    vmem = pl.BlockSpec(memory_space=pltpu.VMEM)
    return pl.pallas_call(
        project_body,
        out_shape=jax.ShapeDtypeStruct(base.shape, BF16),
        in_specs=[vmem] * 7,
        out_specs=vmem,
        compiler_params=pltpu.CompilerParams(vmem_limit_bytes=32 * 2**20),
        name="project",
    )(base, *parts, w_in, w_out)


def on_device(features, tiles, columns, counts, degrees, w_self, w_in, w_out):
    devices = lax.axis_size("dom")
    reps = lax.axis_size("rep")
    position = lax.axis_index("dom")
    rep = lax.axis_index("rep")
    core = lax.rem(position, 2)
    width = features.shape[1] // (2 * reps)
    cores = core_route(devices)

    mine = lax.dynamic_slice_in_dim(features, (2 * rep + core) * width, width, 1)
    theirs = lax.dynamic_slice_in_dim(features, (2 * rep + 1 - core) * width, width, 1)
    sibling = lax.ppermute(theirs, "dom", cores)
    pieces = gather_ring(mine, sibling, devices)

    table = jnp.concatenate([columns, counts[:, :, None]], axis=2)
    table_sib = lax.ppermute(table, "dom", cores)
    tiles_sib = lax.ppermute(tiles, "dom", cores)
    degrees_sib = lax.ppermute(degrees, "dom", cores)
    base = jnp.dot(features, w_self, preferred_element_type=F32)

    own, other = aggregate(
        pieces, (table, table_sib), (tiles, tiles_sib), (degrees, degrees_sib), devices
    )
    core_side = lax.ppermute(other, "dom", cores)
    twin = lax.ppermute(own, "rep", [(r, (r + 1) % reps) for r in range(reps)])
    across = [
        (d * reps + r, (d ^ 1) * reps + (r + 1) % reps) for d in range(devices) for r in range(reps)
    ]
    diagonal = lax.ppermute(other, ("dom", "rep"), across)
    return project(base, (own, core_side, twin, diagonal), w_in, w_out)


def solution(mesh):
    placed = (
        P("dom", None),
        P(None, "dom", None, None, None),
        P(None, "dom", None),
        P(None, "dom"),
        P(None, "dom"),
        P(),
        P(),
        P(),
    )
    return jax.shard_map(
        on_device, mesh=mesh, in_specs=placed, out_specs=P("dom", None), check_vma=False
    )
```

time: 191 us -> 54.2 us (0.28)
  waiting for transfers between devices: 113 us -> 22.4 us
  matrix products: 28.1 us -> 0.71 us
  starting transfers between devices: 4.51 us -> 20.3 us
  local copies, waits for them, and re-layouts: 19.5 us -> 4.04 us
  between operations: 13.5 us -> 0.07 us
  other arithmetic: 11.1 us -> 0.76 us
  Pallas kernels: 0 us -> 5.63 us
    psum x1 -> x0, waiting for transfers between devices: 56.9 us -> none  [on_device(): summed = lax.psum(stacked, 'rep')]
    ppermute x8 -> x21, waiting for transfers between devices: 55.8 us -> 22.4 us  [the longest x1 11.4 us: on_device(): twin = lax.ppermute(own, 'rep', [(r, (r + 1) % reps) for r in range(reps)])]
    dot_general x11 -> x1, matrix products: 28.1 us -> 0.71 us  [on_device(): base = jnp.dot(features, w_self, preferred_element_type=F32)]
    gather x16 -> x0, local copies, waits for them, and re-layouts: 17.5 us -> none  [absorb(): chosen = jnp.take_along_axis(tiles, picks[:, :, :, None, None], axis=2)]
    ppermute x8 -> x21, starting transfers between devices: 4.51 us -> 20.3 us  [the longest x3 5.4 us: gather_ring(): backward[1] = lax.ppermute(backward[1], 'dom', behind)]
    pallas_call x0 -> x2, Pallas kernels: none -> 5.63 us  [the longest x1 3.57 us: aggregate(): pl.pallas_call(functools.partial(aggregate_body, origins, slots, devices...]
    reduce_or x8 -> x0, other arithmetic: 2.45 us -> none  [absorb(): present = jnp.any(matches, axis=-1)]
    reduce_sum x8 -> x0, other arithmetic: 2.42 us -> none  [absorb(): picks = jnp.sum(jnp.where(matches, slot_ids, 0), axis=-1)]
  transfers between devices with their start and end apart: 9 -> 21, of which waited for: 9 -> 9; matrix products, arithmetic and copies ran while one was open for 25% -> 6% of each run, Pallas kernels for 0% -> 0%
where the time goes in v1:
time: 54.2 us; the launch traced here: 53.9 us
  waiting for transfers between devices  22.4 us (41%)
  starting transfers between devices  20.3 us (37%)
  Pallas kernels  5.63 us (10%)
  local copies, waits for them, and re-layouts  4.04 us (7%)
  other arithmetic  0.76 us (1%)
  matrix products  0.71 us (1%)
    ppermute x1, waiting for transfers between devices, on_device(): twin = lax.ppermute(own, 'rep', [(r, (r + 1) % reps) for r in range(reps)])  11.4 us
    ppermute x3, starting transfers between devices, gather_ring(): backward[1] = lax.ppermute(backward[1], 'dom', behind)  5.4 us
    ppermute x3, starting transfers between devices, gather_ring(): backward[0] = lax.ppermute(backward[0], 'dom', behind)  4.73 us
    ppermute x3, waiting for transfers between devices, gather_ring(): forward[0] = lax.ppermute(forward[0], 'dom', ahead)  4.44 us
    pallas_call x1, Pallas kernels, aggregate(): pl.pallas_call(functools.partial(aggregate_body, origins, slots, devices...  3.57 us
    ppermute x3, starting transfers between devices, gather_ring(): forward[0] = lax.ppermute(forward[0], 'dom', ahead)  3.5 us
    ppermute x3, waiting for transfers between devices, gather_ring(): backward[0] = lax.ppermute(backward[0], 'dom', behind)  2.25 us
    unnamed x12, local copies, waits for them, and re-layouts  2.11 us
  transfers between devices with their start and end apart: 21, of which 9 were waited for; matrix products, arithmetic and copies ran while one was open for 6% of the time, Pallas kernels for 0%

profile of v1, /device:TPU:0, one launch (start us, length us, event | category | flops | bytes accessed | tf_op | source)
XLA Modules:
  0.0 53.9 jit_solution(4857188419377864532)
XLA Ops:
  0.0 0.0 copy-start
  0.0 0.5 collective-permute-start.1
  0.5 0.0 copy-start.5
  0.5 1.2 %constant_dynamic-slice_fusion = (bf16[256,256]{1,0:T(8,128)(2,1)S(1)}, bf16[256,256]{1,0:T(8,128)(2,1)S(1)}) fusion(bf16[256,1024]{1,0:T(8,128)(2,1)} %param.8, s32[]{:T(128)S(6)} %select_n.7, s32[]{:T(128)S(6)} %select_n.6), kind=kLoop, calls=%fused_computation.1 | loop fusion | bytes 524296 | tf_op jit(solution)/shard_map/dynamic_slice | solution.py:163
  1.6 0.1 collective-permute-start.3
  1.7 2.9 %collective-permute-start.4 = (bf16[256,256]{1,0:T(8,128)(2,1)S(1)}, bf16[256,256]{1,0:T(8,128)(2,1)S(1)}, u32[]{:S(2)}, u32[]{:S(2)}) collective-permute-start(bf16[256,256]{1,0:T(8,128)(2,1)S(1)} %get-tuple-element.10.refs_6_), channel_id=1, source_target_pairs={{0,8},{2,10},{4,0},{6,2},{8,16},{10,18},{12,4},{14,6},{16,24},{18,... | collective-permute-start | bytes 393224 | tf_op jit(solution)/shard_map/ppermute | solution.py:51
  4.7 0.0 collective-permute-done.3.refs_7_
  4.7 1.9 %collective-permute-start.7 = (bf16[256,256]{1,0:T(8,128)(2,1)S(1)}, bf16[256,256]{1,0:T(8,128)(2,1)S(1)}, u32[]{:S(2)}, u32[]{:S(2)}) collective-permute-start(bf16[256,256]{1,0:T(8,128)(2,1)S(1)} %collective-permute-done.3.refs_7_), channel_id=1, source_target_pairs={{0,4},{2,6},{4,12},{6,14},{8,0},{10,2},{12,20},{14,22},{16,8},{18,... | collective-permute-start | bytes 393224 | tf_op jit(solution)/shard_map/ppermute | solution.py:54
  6.6 0.0 collective-permute-start.2
  6.6 0.8 %copy.9 = s32[2,2,1]{2,1,0:T(2,128)S(1)} copy(s32[2,2,1]{1,0,2:T(2,128)} %bitcast.3) | data formatting | bytes 32 | tf_op jit(solution)/shard_map/broadcast_in_dim | solution.py:167
  7.3 0.8 %pad_add_fusion.refs_0_ = s32[2,2,13]{2,1,0:T(2,128)S(1)} fusion(s32[2,2,1]{2,1,0:T(2,128)S(1)} %copy.9, s32[2,2,12]{2,1,0:T(2,128)} %param.10), kind=kLoop, calls=%fused_computation | loop fusion | flops 52 | bytes 416 | tf_op jit(solution)/shard_map/concatenate | solution.py:167
  8.1 0.5 collective-permute-start
  8.6 0.8 %collective-permute-done.refs_1_ = s32[2,2,13]{2,1,0:T(2,128)S(1)} collective-permute-done((s32[2,2,13]{2,1,0:T(2,128)S(1)}, s32[2,2,13]{2,1,0:T(2,128)S(1)}, u32[]{:S(2)}, u32[]{:S(2)}) %collective-permute-start) | collective-permute-done | bytes 240 | tf_op jit(solution)/shard_map/ppermute | solution.py:168
  9.4 1.6 %collective-permute-start.5 = (bf16[256,256]{1,0:T(8,128)(2,1)S(1)}, bf16[256,256]{1,0:T(8,128)(2,1)S(1)}, u32[]{:S(2)}, u32[]{:S(2)}) collective-permute-start(bf16[256,256]{1,0:T(8,128)(2,1)S(1)} %get-tuple-element.10.refs_6_), channel_id=1, source_target_pairs={{0,4},{2,6},{4,12},{6,14},{8,0},{10,2},{12,20},{14,22},{16,8},{18,... | collective-permute-start | bytes 393224 | tf_op jit(solution)/shard_map/ppermute | solution.py:52
  11.0 0.0 collective-permute-done.2.refs_5_
  11.0 0.5 collective-permute-start.6
  11.5 0.0 collective-permute-done.4.refs_8_
  11.5 0.1 collective-permute-start.8
  11.6 0.0 collective-permute-done.7.refs_11_
  11.6 1.9 %collective-permute-start.11 = (bf16[256,256]{1,0:T(8,128)(2,1)S(1)}, bf16[256,256]{1,0:T(8,128)(2,1)S(1)}, u32[]{:S(2)}, u32[]{:S(2)}) collective-permute-start(bf16[256,256]{1,0:T(8,128)(2,1)S(1)} %collective-permute-done.7.refs_11_), channel_id=1, source_target_pairs={{0,4},{2,6},{4,12},{6,14},{8,0},{10,2},{12,20},{14,22},{16,8},{18,... | collective-permute-start | bytes 393224 | tf_op jit(solution)/shard_map/ppermute | solution.py:54
  13.5 2.2 %collective-permute-done.5.refs_9_ = bf16[256,256]{1,0:T(8,128)(2,1)S(1)} collective-permute-done((bf16[256,256]{1,0:T(8,128)(2,1)S(1)}, bf16[256,256]{1,0:T(8,128)(2,1)S(1)}, u32[]{:S(2)}, u32[]{:S(2)}) %collective-permute-start.5) | collective-permute-done | bytes 131104 | tf_op jit(solution)/shard_map/ppermute | solution.py:52
  15.7 1.6 %collective-permute-start.9 = (bf16[256,256]{1,0:T(8,128)(2,1)S(1)}, bf16[256,256]{1,0:T(8,128)(2,1)S(1)}, u32[]{:S(2)}, u32[]{:S(2)}) collective-permute-start(bf16[256,256]{1,0:T(8,128)(2,1)S(1)} %collective-permute-done.5.refs_9_), channel_id=1, source_target_pairs={{0,4},{2,6},{4,12},{6,14},{8,0},{10,2},{12,20},{14,22},{16,8},{18,... | collective-permute-start | bytes 393224 | tf_op jit(solution)/shard_map/ppermute | solution.py:52
  17.3 0.0 collective-permute-done.6.refs_10_
  17.4 0.4 collective-permute-start.10
  17.8 2.1 %collective-permute-done.8.refs_12_ = bf16[256,256]{1,0:T(8,128)(2,1)S(1)} collective-permute-done((bf16[256,256]{1,0:T(8,128)(2,1)S(1)}, bf16[256,256]{1,0:T(8,128)(2,1)S(1)}, u32[]{:S(2)}, u32[]{:S(2)}) %collective-permute-start.8) | collective-permute-done | bytes 131104 | tf_op jit(solution)/shard_map/ppermute | solution.py:51
  19.9 0.4 collective-permute-start.12
  20.3 0.0 collective-permute-done.11.refs_15_
  20.3 1.6 %collective-permute-start.15 = (bf16[256,256]{1,0:T(8,128)(2,1)S(1)}, bf16[256,256]{1,0:T(8,128)(2,1)S(1)}, u32[]{:S(2)}, u32[]{:S(2)}) collective-permute-start(bf16[256,256]{1,0:T(8,128)(2,1)S(1)} %collective-permute-done.11.refs_15_), channel_id=1, source_target_pairs={{0,4},{2,6},{4,12},{6,14},{8,0},{10,2},{12,20},{14,22},{16,8},{18,... | collective-permute-start | bytes 393224 | tf_op jit(solution)/shard_map/ppermute | solution.py:54
  21.9 0.0 collective-permute-done.9.refs_13_
  21.9 1.6 %collective-permute-start.13 = (bf16[256,256]{1,0:T(8,128)(2,1)S(1)}, bf16[256,256]{1,0:T(8,128)(2,1)S(1)}, u32[]{:S(2)}, u32[]{:S(2)}) collective-permute-start(bf16[256,256]{1,0:T(8,128)(2,1)S(1)} %collective-permute-done.9.refs_13_), channel_id=1, source_target_pairs={{0,4},{2,6},{4,12},{6,14},{8,0},{10,2},{12,20},{14,22},{16,8},{18,... | collective-permute-start | bytes 393224 | tf_op jit(solution)/shard_map/ppermute | solution.py:52
  23.5 0.1 collective-permute-done.10.refs_14_
  23.6 0.4 collective-permute-start.14
  24.0 2.4 %collective-permute-done.12.refs_16_ = bf16[256,256]{1,0:T(8,128)(2,1)S(1)} collective-permute-done((bf16[256,256]{1,0:T(8,128)(2,1)S(1)}, bf16[256,256]{1,0:T(8,128)(2,1)S(1)}, u32[]{:S(2)}, u32[]{:S(2)}) %collective-permute-start.12) | collective-permute-done | bytes 131104 | tf_op jit(solution)/shard_map/ppermute | solution.py:51
  26.4 0.4 collective-permute-start.16
  26.8 0.0 collective-permute-done.15.refs_19_
  26.8 1.6 %collective-permute-start.17 = (bf16[256,256]{1,0:T(8,128)(2,1)S(1)}, bf16[256,256]{1,0:T(8,128)(2,1)S(1)}, u32[]{:S(2)}, u32[]{:S(2)}) collective-permute-start(bf16[256,256]{1,0:T(8,128)(2,1)S(1)} %collective-permute-done.15.refs_19_), channel_id=1, source_target_pairs={{0,4},{2,6},{4,12},{6,14},{8,0},{10,2},{12,20},{14,22},{16,8},{18,... | collective-permute-start | bytes 393224 | tf_op jit(solution)/shard_map/ppermute | solution.py:60
  28.4 0.0 collective-permute-done.13.refs_17_
  28.4 1.0 %collective-permute-done.14.refs_18_ = bf16[256,256]{1,0:T(8,128)(2,1)S(1)} collective-permute-done((bf16[256,256]{1,0:T(8,128)(2,1)S(1)}, bf16[256,256]{1,0:T(8,128)(2,1)S(1)}, u32[]{:S(2)}, u32[]{:S(2)}) %collective-permute-start.14) | collective-permute-done | bytes 131104 | tf_op jit(solution)/shard_map/ppermute | solution.py:53
  29.4 1.9 %collective-permute-done.16.refs_20_ = bf16[256,256]{1,0:T(8,128)(2,1)S(1)} collective-permute-done((bf16[256,256]{1,0:T(8,128)(2,1)S(1)}, bf16[256,256]{1,0:T(8,128)(2,1)S(1)}, u32[]{:S(2)}, u32[]{:S(2)}) %collective-permute-start.16) | collective-permute-done | bytes 131104 | tf_op jit(solution)/shard_map/ppermute | solution.py:59
  31.3 0.5 collective-permute-done.17.refs_21_
  31.8 0.0 collective-permute-done.1.refs_3_
  31.8 0.0 copy-start.3
  31.8 1.4 %copy-done.3 = bf16[2,2,12,128,128]{4,3,2,1,0:T(8,128)(2,1)S(1)} copy-done((bf16[2,2,12,128,128]{4,3,2,1,0:T(8,128)(2,1)S(1)}, bf16[2,2,12,128,128]{4,3,2,1,0:T(8,128)(2,1)}, u32[]{:S(2)}) %copy-start.3) | copy-done | bytes 1572888
  33.2 0.0 copy-start.4
  33.2 0.7 %copy-done.4 = s32[2,256]{1,0:T(2,128)S(1)} copy-done((s32[2,256]{1,0:T(2,128)S(1)}, s32[2,256]{1,0:T(2,128)}, u32[]{:S(2)}) %copy-start.4) | copy-done | bytes 2072
  33.9 0.0 copy-start.2
  33.9 3.6 %aggregate.1 = (bf16[2,256,256]{2,1,0:T(8,128)(2,1)S(1)}, bf16[2,256,256]{2,1,0:T(8,128)(2,1)S(1)}) custom-call(s32[2,2,13]{2,1,0:T(2,128)S(1)} %pad_add_fusion.refs_0_, s32[2,2,13]{2,1,0:T(2,128)S(1)} %collective-permute-done.refs_1_, bf16[2,2,12,128,128]{4,3,2,1,0:T(8,128)(2,1)S(1)} %copy-done.3, ...), custom_call_target="tpu_custom_call" | custom-call | tf_op jit(solution)/shard_map/aggregate/pallas_call | solution.py:113
  37.5 0.0 copy-start.1
  37.5 0.1 collective-permute-start.18
  37.6 1.6 %collective-permute-start.20 = (bf16[2,256,256]{2,1,0:T(8,128)(2,1)S(1)}, bf16[2,256,256]{2,1,0:T(8,128)(2,1)S(1)}, u32[]{:S(2)}, u32[]{:S(2)}) collective-permute-start(bf16[2,256,256]{2,1,0:T(8,128)(2,1)S(1)} %get-tuple-element.8), channel_id=1, source_target_pairs={{0,3},{1,2},{2,1},{3,0},{4,7},{5,6},{6,5},{7,4},{8,11},{9,10},{10,... | collective-permute-start | bytes 786440 | tf_op jit(solution)/shard_map/ppermute | solution.py:181
  39.2 0.5 collective-permute-start.19
  39.7 0.0 copy-done
  39.7 0.0 copy-done.5
  39.7 0.7 %fusion.base = f32[256,1024]{1,0:T(8,128)S(1)} fusion(bf16[256,1024]{1,0:T(8,128)(2,1)S(1)} %copy-done.5, bf16[1024,1024]{1,0:T(8,128)(2,1)S(1)} %copy-done), kind=kOutput, calls=%fused_computation.3 | convolution fusion | flops 536870912 | bytes 3670016 | tf_op jit(solution)/shard_map/dot_general | solution.py:171
  40.4 0.0 collective-permute-done.18.core_side
  40.5 11.4 %collective-permute-done.19.twin = bf16[2,256,256]{2,1,0:T(8,128)(2,1)S(1)} collective-permute-done((bf16[2,256,256]{2,1,0:T(8,128)(2,1)S(1)}, bf16[2,256,256]{2,1,0:T(8,128)(2,1)S(1)}, u32[]{:S(2)}, u32[]{:S(2)}) %collective-permute-start.19) | collective-permute-done | bytes 262176 | tf_op jit(solution)/shard_map/ppermute | solution.py:177
  51.9 0.0 collective-permute-done.20.diagonal
  51.9 0.0 copy-done.2
  51.9 0.0 copy-done.1
  51.9 2.1 %project.1 = bf16[256,1024]{1,0:T(8,128)(2,1)} custom-call(f32[256,1024]{1,0:T(8,128)S(1)} %fusion.base, bf16[2,256,256]{2,1,0:T(8,128)(2,1)S(1)} %get-tuple-element.7.own, bf16[2,256,256]{2,1,0:T(8,128)(2,1)S(1)} %collective-permute-done.18.core_side, bf16[2,256,256]{2,1,0:T(8,128)(2,1)S(1)} %collective-permute-done.19.twin, ...), custom_call_target="tpu_custom_call" | custom-call | tf_op jit(solution)/shard_map/project/pallas_call | solution.py:143
Async XLA Ops:
  0.0 39.7 %copy-start = (bf16[1024,1024]{1,0:T(8,128)(2,1)S(1)}, bf16[1024,1024]{1,0:T(8,128)(2,1)}, u32[]{:S(2)}) copy-start(bf16[1024,1024]{1,0:T(8,128)(2,1)} %param.13) | copy-start | bytes 6291460
  0.0 31.8 %collective-permute-start.1 = (bf16[2,2,12,128,128]{4,3,2,1,0:T(8,128)(2,1)}, bf16[2,2,12,128,128]{4,3,2,1,0:T(8,128)(2,1)}, u32[]{:S(2)}, u32[]{:S(2)}) collective-permute-start(bf16[2,2,12,128,128]{4,3,2,1,0:T(8,128)(2,1)} %refs_2_.1), channel_id=1, source_target_pairs={{0,2},{2,0},{4,6},{6,4},{8,10},{10,8},{12,14},{14,12},{16,18},{18,... | collective-permute-start | bytes 4718600 | tf_op jit(solution)/shard_map/ppermute | solution.py:169
  0.5 39.3 %copy-start.5 = (bf16[256,1024]{1,0:T(8,128)(2,1)S(1)}, bf16[256,1024]{1,0:T(8,128)(2,1)}, u32[]{:S(2)}) copy-start(bf16[256,1024]{1,0:T(8,128)(2,1)} %param.8) | copy-start | bytes 1572868
  1.6 3.0 %collective-permute-start.3 = (bf16[256,256]{1,0:T(8,128)(2,1)S(1)}, bf16[256,256]{1,0:T(8,128)(2,1)S(1)}, u32[]{:S(2)}, u32[]{:S(2)}) collective-permute-start(bf16[256,256]{1,0:T(8,128)(2,1)S(1)} %get-tuple-element.9), channel_id=1, source_target_pairs={{0,2},{2,0},{4,6},{6,4},{8,10},{10,8},{12,14},{14,12},{16,18},{18,... | collective-permute-start | bytes 393224 | tf_op jit(solution)/shard_map/ppermute | solution.py:164
  1.7 9.7 %collective-permute-start.4 = (bf16[256,256]{1,0:T(8,128)(2,1)S(1)}, bf16[256,256]{1,0:T(8,128)(2,1)S(1)}, u32[]{:S(2)}, u32[]{:S(2)}) collective-permute-start(bf16[256,256]{1,0:T(8,128)(2,1)S(1)} %get-tuple-element.10.refs_6_), channel_id=1, source_target_pairs={{0,8},{2,10},{4,0},{6,2},{8,16},{10,18},{12,4},{14,6},{16,24},{18,... | collective-permute-start | bytes 393224 | tf_op jit(solution)/shard_map/ppermute | solution.py:51
  4.7 6.9 %collective-permute-start.7 = (bf16[256,256]{1,0:T(8,128)(2,1)S(1)}, bf16[256,256]{1,0:T(8,128)(2,1)S(1)}, u32[]{:S(2)}, u32[]{:S(2)}) collective-permute-start(bf16[256,256]{1,0:T(8,128)(2,1)S(1)} %collective-permute-done.3.refs_7_), channel_id=1, source_target_pairs={{0,4},{2,6},{4,12},{6,14},{8,0},{10,2},{12,20},{14,22},{16,8},{18,... | collective-permute-start | bytes 393224 | tf_op jit(solution)/shard_map/ppermute | solution.py:54
  6.6 4.4 %collective-permute-start.2 = (s32[2,256]{1,0:T(2,128)}, s32[2,256]{1,0:T(2,128)S(1)}, u32[]{:S(2)}, u32[]{:S(2)}) collective-permute-start(s32[2,256]{1,0:T(2,128)} %refs_4_.1), channel_id=1, source_target_pairs={{0,2},{2,0},{4,6},{6,4},{8,10},{10,8},{12,14},{14,12},{16,18},{18,... | collective-permute-start | bytes 6152 | tf_op jit(solution)/shard_map/ppermute | solution.py:170
  8.1 1.3 %collective-permute-start = (s32[2,2,13]{2,1,0:T(2,128)S(1)}, s32[2,2,13]{2,1,0:T(2,128)S(1)}, u32[]{:S(2)}, u32[]{:S(2)}) collective-permute-start(s32[2,2,13]{2,1,0:T(2,128)S(1)} %pad_add_fusion.refs_0_), channel_id=1, source_target_pairs={{0,2},{2,0},{4,6},{6,4},{8,10},{10,8},{12,14},{14,12},{16,18},{18,... | collective-permute-start | bytes 632 | tf_op jit(solution)/shard_map/ppermute | solution.py:168
  9.4 6.3 %collective-permute-start.5 = (bf16[256,256]{1,0:T(8,128)(2,1)S(1)}, bf16[256,256]{1,0:T(8,128)(2,1)S(1)}, u32[]{:S(2)}, u32[]{:S(2)}) collective-permute-start(bf16[256,256]{1,0:T(8,128)(2,1)S(1)} %get-tuple-element.10.refs_6_), channel_id=1, source_target_pairs={{0,4},{2,6},{4,12},{6,14},{8,0},{10,2},{12,20},{14,22},{16,8},{18,... | collective-permute-start | bytes 393224 | tf_op jit(solution)/shard_map/ppermute | solution.py:52
  11.0 6.4 %collective-permute-start.6 = (bf16[256,256]{1,0:T(8,128)(2,1)S(1)}, bf16[256,256]{1,0:T(8,128)(2,1)S(1)}, u32[]{:S(2)}, u32[]{:S(2)}) collective-permute-start(bf16[256,256]{1,0:T(8,128)(2,1)S(1)} %collective-permute-done.3.refs_7_), channel_id=1, source_target_pairs={{0,8},{2,10},{4,0},{6,2},{8,16},{10,18},{12,4},{14,6},{16,24},{18,... | collective-permute-start | bytes 393224 | tf_op jit(solution)/shard_map/ppermute | solution.py:53
  11.5 8.4 %collective-permute-start.8 = (bf16[256,256]{1,0:T(8,128)(2,1)S(1)}, bf16[256,256]{1,0:T(8,128)(2,1)S(1)}, u32[]{:S(2)}, u32[]{:S(2)}) collective-permute-start(bf16[256,256]{1,0:T(8,128)(2,1)S(1)} %collective-permute-done.4.refs_8_), channel_id=1, source_target_pairs={{0,8},{2,10},{4,0},{6,2},{8,16},{10,18},{12,4},{14,6},{16,24},{18,... | collective-permute-start | bytes 393224 | tf_op jit(solution)/shard_map/ppermute | solution.py:51
  11.6 8.8 %collective-permute-start.11 = (bf16[256,256]{1,0:T(8,128)(2,1)S(1)}, bf16[256,256]{1,0:T(8,128)(2,1)S(1)}, u32[]{:S(2)}, u32[]{:S(2)}) collective-permute-start(bf16[256,256]{1,0:T(8,128)(2,1)S(1)} %collective-permute-done.7.refs_11_), channel_id=1, source_target_pairs={{0,4},{2,6},{4,12},{6,14},{8,0},{10,2},{12,20},{14,22},{16,8},{18,... | collective-permute-start | bytes 393224 | tf_op jit(solution)/shard_map/ppermute | solution.py:54
  15.7 6.2 %collective-permute-start.9 = (bf16[256,256]{1,0:T(8,128)(2,1)S(1)}, bf16[256,256]{1,0:T(8,128)(2,1)S(1)}, u32[]{:S(2)}, u32[]{:S(2)}) collective-permute-start(bf16[256,256]{1,0:T(8,128)(2,1)S(1)} %collective-permute-done.5.refs_9_), channel_id=1, source_target_pairs={{0,4},{2,6},{4,12},{6,14},{8,0},{10,2},{12,20},{14,22},{16,8},{18,... | collective-permute-start | bytes 393224 | tf_op jit(solution)/shard_map/ppermute | solution.py:52
  17.4 6.2 %collective-permute-start.10 = (bf16[256,256]{1,0:T(8,128)(2,1)S(1)}, bf16[256,256]{1,0:T(8,128)(2,1)S(1)}, u32[]{:S(2)}, u32[]{:S(2)}) collective-permute-start(bf16[256,256]{1,0:T(8,128)(2,1)S(1)} %collective-permute-done.6.refs_10_), channel_id=1, source_target_pairs={{0,8},{2,10},{4,0},{6,2},{8,16},{10,18},{12,4},{14,6},{16,24},{18,... | collective-permute-start | bytes 393224 | tf_op jit(solution)/shard_map/ppermute | solution.py:53
  19.9 6.5 %collective-permute-start.12 = (bf16[256,256]{1,0:T(8,128)(2,1)S(1)}, bf16[256,256]{1,0:T(8,128)(2,1)S(1)}, u32[]{:S(2)}, u32[]{:S(2)}) collective-permute-start(bf16[256,256]{1,0:T(8,128)(2,1)S(1)} %collective-permute-done.8.refs_12_), channel_id=1, source_target_pairs={{0,8},{2,10},{4,0},{6,2},{8,16},{10,18},{12,4},{14,6},{16,24},{18,... | collective-permute-start | bytes 393224 | tf_op jit(solution)/shard_map/ppermute | solution.py:51
  20.3 6.5 %collective-permute-start.15 = (bf16[256,256]{1,0:T(8,128)(2,1)S(1)}, bf16[256,256]{1,0:T(8,128)(2,1)S(1)}, u32[]{:S(2)}, u32[]{:S(2)}) collective-permute-start(bf16[256,256]{1,0:T(8,128)(2,1)S(1)} %collective-permute-done.11.refs_15_), channel_id=1, source_target_pairs={{0,4},{2,6},{4,12},{6,14},{8,0},{10,2},{12,20},{14,22},{16,8},{18,... | collective-permute-start | bytes 393224 | tf_op jit(solution)/shard_map/ppermute | solution.py:54
  21.9 6.5 %collective-permute-start.13 = (bf16[256,256]{1,0:T(8,128)(2,1)S(1)}, bf16[256,256]{1,0:T(8,128)(2,1)S(1)}, u32[]{:S(2)}, u32[]{:S(2)}) collective-permute-start(bf16[256,256]{1,0:T(8,128)(2,1)S(1)} %collective-permute-done.9.refs_13_), channel_id=1, source_target_pairs={{0,4},{2,6},{4,12},{6,14},{8,0},{10,2},{12,20},{14,22},{16,8},{18,... | collective-permute-start | bytes 393224 | tf_op jit(solution)/shard_map/ppermute | solution.py:52
  23.6 5.8 %collective-permute-start.14 = (bf16[256,256]{1,0:T(8,128)(2,1)S(1)}, bf16[256,256]{1,0:T(8,128)(2,1)S(1)}, u32[]{:S(2)}, u32[]{:S(2)}) collective-permute-start(bf16[256,256]{1,0:T(8,128)(2,1)S(1)} %collective-permute-done.10.refs_14_), channel_id=1, source_target_pairs={{0,8},{2,10},{4,0},{6,2},{8,16},{10,18},{12,4},{14,6},{16,24},{18,... | collective-permute-start | bytes 393224 | tf_op jit(solution)/shard_map/ppermute | solution.py:53
  26.4 5.0 %collective-permute-start.16 = (bf16[256,256]{1,0:T(8,128)(2,1)S(1)}, bf16[256,256]{1,0:T(8,128)(2,1)S(1)}, u32[]{:S(2)}, u32[]{:S(2)}) collective-permute-start(bf16[256,256]{1,0:T(8,128)(2,1)S(1)} %collective-permute-done.12.refs_16_), channel_id=1, source_target_pairs={{0,8},{2,10},{4,0},{6,2},{8,16},{10,18},{12,4},{14,6},{16,24},{18,... | collective-permute-start | bytes 393224 | tf_op jit(solution)/shard_map/ppermute | solution.py:59
  26.8 5.0 %collective-permute-start.17 = (bf16[256,256]{1,0:T(8,128)(2,1)S(1)}, bf16[256,256]{1,0:T(8,128)(2,1)S(1)}, u32[]{:S(2)}, u32[]{:S(2)}) collective-permute-start(bf16[256,256]{1,0:T(8,128)(2,1)S(1)} %collective-permute-done.15.refs_19_), channel_id=1, source_target_pairs={{0,4},{2,6},{4,12},{6,14},{8,0},{10,2},{12,20},{14,22},{16,8},{18,... | collective-permute-start | bytes 393224 | tf_op jit(solution)/shard_map/ppermute | solution.py:60
  31.8 1.4 %copy-start.3 = (bf16[2,2,12,128,128]{4,3,2,1,0:T(8,128)(2,1)S(1)}, bf16[2,2,12,128,128]{4,3,2,1,0:T(8,128)(2,1)}, u32[]{:S(2)}) copy-start(bf16[2,2,12,128,128]{4,3,2,1,0:T(8,128)(2,1)} %refs_2_.1) | copy-start | bytes 4718596
  33.2 0.7 %copy-start.4 = (s32[2,256]{1,0:T(2,128)S(1)}, s32[2,256]{1,0:T(2,128)}, u32[]{:S(2)}) copy-start(s32[2,256]{1,0:T(2,128)} %refs_4_.1) | copy-start | bytes 6148
  33.9 18.0 %copy-start.2 = (bf16[1024,1024]{1,0:T(8,128)(2,1)S(1)}, bf16[1024,1024]{1,0:T(8,128)(2,1)}, u32[]{:S(2)}) copy-start(bf16[1024,1024]{1,0:T(8,128)(2,1)} %w_out.1) | copy-start | bytes 6291460
  37.5 14.4 %copy-start.1 = (bf16[1024,1024]{1,0:T(8,128)(2,1)S(1)}, bf16[1024,1024]{1,0:T(8,128)(2,1)}, u32[]{:S(2)}) copy-start(bf16[1024,1024]{1,0:T(8,128)(2,1)} %w_in.1) | copy-start | bytes 6291460
  37.5 3.0 %collective-permute-start.18 = (bf16[2,256,256]{2,1,0:T(8,128)(2,1)S(1)}, bf16[2,256,256]{2,1,0:T(8,128)(2,1)S(1)}, u32[]{:S(2)}, u32[]{:S(2)}) collective-permute-start(bf16[2,256,256]{2,1,0:T(8,128)(2,1)S(1)} %get-tuple-element.8), channel_id=1, source_target_pairs={{0,2},{2,0},{4,6},{6,4},{8,10},{10,8},{12,14},{14,12},{16,18},{18,... | collective-permute-start | bytes 786440 | tf_op jit(solution)/shard_map/ppermute | solution.py:176
  37.6 14.3 %collective-permute-start.20 = (bf16[2,256,256]{2,1,0:T(8,128)(2,1)S(1)}, bf16[2,256,256]{2,1,0:T(8,128)(2,1)S(1)}, u32[]{:S(2)}, u32[]{:S(2)}) collective-permute-start(bf16[2,256,256]{2,1,0:T(8,128)(2,1)S(1)} %get-tuple-element.8), channel_id=1, source_target_pairs={{0,3},{1,2},{2,1},{3,0},{4,7},{5,6},{6,5},{7,4},{8,11},{9,10},{10,... | collective-permute-start | bytes 786440 | tf_op jit(solution)/shard_map/ppermute | solution.py:181
  39.2 12.7 %collective-permute-start.19 = (bf16[2,256,256]{2,1,0:T(8,128)(2,1)S(1)}, bf16[2,256,256]{2,1,0:T(8,128)(2,1)S(1)}, u32[]{:S(2)}, u32[]{:S(2)}) collective-permute-start(bf16[2,256,256]{2,1,0:T(8,128)(2,1)S(1)} %get-tuple-element.7.own), channel_id=1, source_target_pairs={{0,1},{1,0},{2,3},{3,2},{4,5},{5,4},{6,7},{7,6},{8,9},{9,8},{10,11... | collective-permute-start | bytes 786440 | tf_op jit(solution)/shard_map/ppermute | solution.py:177

commit v2 on v0

v2 whole, which is shorter than its diff:
```python
import functools

import jax
import jax.numpy as jnp
from jax import lax
from jax.experimental import pallas as pl
from jax.experimental.pallas import tpu as pltpu
from jax.sharding import PartitionSpec as P

F32 = jnp.float32
BF16 = jnp.bfloat16
SMEM = pl.BlockSpec(memory_space=pltpu.SMEM)
VMEM = pl.BlockSpec(memory_space=pltpu.VMEM)
HBM = pl.BlockSpec(memory_space=pltpu.HBM)


def params(mib):
    return pltpu.CompilerParams(vmem_limit_bytes=mib * 2**20)


def chip_ring(chips):
    half = chips // 2
    return [2 * o for o in range(half)] + [2 * o + 1 for o in reversed(range(half))]


def ring_route(devices, distance):
    ring = chip_ring(devices // 2)
    size = len(ring)
    route = []
    for place, chip in enumerate(ring):
        target = ring[(place + distance) % size]
        route += [(2 * chip + core, 2 * target + core) for core in range(2)]
    return sorted(route)


def swapped(route):
    return [(source, target ^ 1) for source, target in route]


def core_route(devices):
    return [(d, d ^ 1) for d in range(devices)]


def chip_at(place, chips):
    place = lax.rem(place + 2 * chips, chips)
    return jnp.where(place < chips // 2, 2 * place, 2 * (chips - 1 - place) + 1)


def place_of(chip, chips):
    side = lax.rem(chip, 2)
    rung = chip // 2
    return jnp.where(side == 0, rung, chips - 1 - rung)


def source_device(offset, other, chips):
    position = lax.axis_index("dom")
    core = lax.rem(position, 2)
    chip = chip_at(place_of(position // 2, chips) + offset, chips)
    return 2 * chip + (1 - core if other else core)


def pack_body(blocks, features, tiles_in, columns_in, counts_in, degrees_in, *refs):
    mine, theirs, tiles, info, columns, counts, degrees, arrived = refs
    rep = lax.axis_index("rep")
    core = lax.rem(lax.axis_index("dom"), 2)
    width = mine.shape[1]

    def quarter(core_of):
        return features.at[:, pl.ds(pl.multiple_of((2 * rep + core_of) * width, width), width)]

    moves = (
        (columns_in, columns),
        (counts_in, counts),
        (degrees_in, degrees),
        (quarter(core), mine),
        (quarter(1 - core), theirs),
        (tiles_in, tiles),
    )
    copies = [
        pltpu.make_async_copy(source, target, arrived.at[index])
        for index, (source, target) in enumerate(moves)
    ]
    for copy in copies:
        copy.start()
    for copy in copies[:3]:
        copy.wait()
    info[...] = jnp.full(info.shape, -1, jnp.int32)
    place = lax.broadcasted_iota(jnp.int32, (1, info.shape[1]), 1)
    _, local, slots = columns.shape
    for relation in range(2):
        for row in range(local):
            live = counts[relation, row]
            slot_of = jnp.full(place.shape, -1, jnp.int32)
            for slot in range(slots):
                target = jnp.where(slot < live, columns[relation, row, slot], -1)
                slot_of = jnp.where(place == target, slot, slot_of)
            index = relation * local + row
            info[index : index + 1, :] = slot_of
    info[2 * local : 2 * local + 2, 0 : degrees.shape[1]] = degrees[...]
    for copy in copies[3:]:
        copy.wait()


def pack(features, tiles, columns, counts, degrees, width, devices):
    rows = features.shape[0]
    blocks = devices * tiles.shape[1]
    piece = jax.ShapeDtypeStruct((rows, width), BF16)
    info = jax.ShapeDtypeStruct((8, max(rows, blocks)), jnp.int32)
    operands = [
        pltpu.with_memory_space_constraint(x, pltpu.HBM)
        for x in (features, tiles, columns, counts, degrees)
    ]
    return pl.pallas_call(
        functools.partial(pack_body, blocks),
        out_shape=[piece, piece, jax.ShapeDtypeStruct(tiles.shape, BF16), info],
        in_specs=[HBM] * 5,
        out_specs=[VMEM] * 4,
        scratch_shapes=[
            pltpu.SMEM(columns.shape, jnp.int32),
            pltpu.SMEM(counts.shape, jnp.int32),
            pltpu.VMEM(degrees.shape, jnp.int32),
            pltpu.SemaphoreType.DMA((6,)),
        ],
        compiler_params=params(24),
        name="pack",
    )(*operands)


def contribution(slot_of, tiles, relation, row, pieces, sources):
    local = tiles.shape[1]
    total = None
    for piece, source in zip(pieces, sources):
        weights = []
        for block in range(local):
            slot = slot_of[relation * local + row, source * local + block]
            one = tiles[relation, row, jnp.maximum(slot, 0)]
            weights.append(jnp.where(slot >= 0, one, jnp.zeros_like(one)))
        part = jnp.dot(
            jnp.concatenate(weights, axis=1), piece[...], preferred_element_type=F32
        )
        total = part if total is None else total + part
    return total


def absorb_body(origins, chips, seeded, *refs):
    slot_of, tiles = refs[0:2], refs[2:4]
    count = len(origins)
    pieces = refs[4 : 4 + count]
    seed = refs[4 + count] if seeded else None
    sums = refs[-1]
    tile = tiles[0].shape[-1]
    sources = [source_device(offset, other, chips) for offset, other in origins]
    for side in range(2):
        for relation in range(2):
            for row in range(tiles[side].shape[1]):
                span = slice(row * tile, (row + 1) * tile)
                part = contribution(slot_of[side], tiles[side], relation, row, pieces, sources)
                if seeded:
                    part = part + seed[side, relation, span, :]
                sums[side, relation, span, :] = part


def absorb(plan, pieces, sums, devices):
    infos, tiles = plan
    rows, width = pieces[0][0].shape
    origins = tuple((offset, other) for _, offset, other in pieces)
    seeds = [] if sums is None else [sums]
    return pl.pallas_call(
        functools.partial(absorb_body, origins, devices // 2, sums is not None),
        out_shape=jax.ShapeDtypeStruct((2, 2, rows, width), F32),
        in_specs=[SMEM] * 2 + [VMEM] * (2 + len(pieces) + len(seeds)),
        out_specs=VMEM,
        compiler_params=params(32),
        cost_estimate=pl.CostEstimate(
            flops=len(pieces) * 8 * rows * rows * width, bytes_accessed=0, transcendentals=0
        ),
        name="absorb",
    )(*infos, *tiles, *[piece for piece, _, _ in pieces], *seeds)


def close_body(origins, chips, side, slot_of, info, tiles, sums, *refs):
    pieces, out = refs[:-1], refs[-1]
    tile = tiles.shape[-1]
    local = tiles.shape[1]
    sources = [source_device(offset, other, chips) for offset, other in origins]
    for relation in range(2):
        for row in range(local):
            span = slice(row * tile, (row + 1) * tile)
            total = sums[side, relation, span, :]
            if pieces:
                total = total + contribution(slot_of, tiles, relation, row, pieces, sources)
            index = 2 * local + relation
            degree = info[index : index + 1, row * tile : (row + 1) * tile].astype(F32)
            degree = jnp.broadcast_to(degree, (tile, tile)).T
            for start in range(0, total.shape[1], tile):
                part = total[:, start : start + tile] / degree
                out[relation, span, start : start + tile] = part.astype(BF16)


def close(plan, pieces, sums, side, devices):
    infos, tiles = plan
    _, _, rows, width = sums.shape
    origins = tuple((offset, other) for _, offset, other in pieces)
    return pl.pallas_call(
        functools.partial(close_body, origins, devices // 2, side),
        out_shape=jax.ShapeDtypeStruct((2, rows, width), BF16),
        in_specs=[SMEM] + [VMEM] * (3 + len(pieces)),
        out_specs=VMEM,
        compiler_params=params(32),
        name="close",
    )(infos[side], infos[side], tiles[side], sums, *[piece for piece, _, _ in pieces])


def project_body(quarters, last, base, w_in, w_out, *refs):
    parts, out = refs[:-1], refs[-1]
    rep = lax.axis_index("rep")
    core = lax.rem(lax.axis_index("dom"), 2)
    total = base[...]
    for part, (far, other) in zip(parts, quarters):
        width = part.shape[2]
        quarter = 2 * (1 - rep if far else rep) + (1 - core if other else core)
        span = pl.ds(pl.multiple_of(quarter * width, width), width)
        total = total + jnp.dot(part[0], w_in[span, :], preferred_element_type=F32)
        total = total + jnp.dot(part[1], w_out[span, :], preferred_element_type=F32)
    out[...] = jnp.maximum(total, 0.0).astype(BF16) if last else total


def project(base, parts, quarters, w_in, w_out, last):
    return pl.pallas_call(
        functools.partial(project_body, quarters, last),
        out_shape=jax.ShapeDtypeStruct(base.shape, BF16 if last else F32),
        in_specs=[VMEM] * (3 + len(parts)),
        out_specs=VMEM,
        compiler_params=params(24),
        cost_estimate=pl.CostEstimate(
            flops=len(parts) * 2**28, bytes_accessed=0, transcendentals=0
        ),
        name="project",
    )(base, w_in, w_out, *parts)


def on_device(features, tiles, columns, counts, degrees, w_self, w_in, w_out):
    devices = lax.axis_size("dom")
    reps = lax.axis_size("rep")
    width = features.shape[1] // (2 * reps)
    chips = devices // 2
    cores = core_route(devices)
    ahead, behind = ring_route(devices, 1), ring_route(devices, -1)

    mine, theirs, tiles, info = pack(features, tiles, columns, counts, degrees, width, devices)

    forward = [mine, theirs]
    backward = [mine, theirs]
    steps = []
    for step in range(1, (chips - 1) // 2 + 1):
        found = []
        for other in range(2):
            swap = other == 1 and step == 1
            forward[other] = lax.ppermute(forward[other], "dom", swapped(ahead) if swap else ahead)
            backward[other] = lax.ppermute(backward[other], "dom", swapped(behind) if swap else behind)
            found += [(forward[other], -step, other), (backward[other], step, other)]
        steps.append(found)
    last = [
        (lax.ppermute(forward[0], "dom", ahead), chips // 2, 0),
        (lax.ppermute(backward[1], "dom", behind), chips // 2, 1),
    ]
    sibling = lax.ppermute(theirs, "dom", cores)
    plan = (
        (info, lax.ppermute(info, "dom", cores)),
        (tiles, lax.ppermute(tiles, "dom", cores)),
    )
    early = [(mine, 0, 0), (sibling, 0, 1)] + [piece for found in steps[:-1] for piece in found]
    sums = absorb(plan, early, None, devices)
    sums = absorb(plan, steps[-1], sums, devices)
    other = close(plan, last, sums, 1, devices)
    own = close(plan, last, sums, 0, devices)

    across = [
        (d * reps + r, (d ^ 1) * reps + (r + 1) % reps) for d in range(devices) for r in range(reps)
    ]
    diagonal = lax.ppermute(other, ("dom", "rep"), across)
    core_side = lax.ppermute(other, "dom", cores)
    twin = lax.ppermute(own, "rep", [(r, (r + 1) % reps) for r in range(reps)])

    hidden = jnp.dot(features, w_self, preferred_element_type=F32)
    hidden = project(hidden, (own, core_side), ((0, 0), (0, 1)), w_in, w_out, False)
    hidden = project(hidden, (diagonal,), ((1, 1),), w_in, w_out, False)
    return project(hidden, (twin,), ((1, 0),), w_in, w_out, True)


def solution(mesh):
    placed = (
        P("dom", None),
        P(None, "dom", None, None, None),
        P(None, "dom", None),
        P(None, "dom"),
        P(None, "dom"),
        P(),
        P(),
        P(),
    )
    return jax.shard_map(
        on_device, mesh=mesh, in_specs=placed, out_specs=P("dom", None), check_vma=False
    )
```

time: 191 us -> 45.5 us (0.24)
  waiting for transfers between devices: 113 us -> 16.8 us
  matrix products: 28.1 us -> 0.7 us
  local copies, waits for them, and re-layouts: 19.5 us -> 0.41 us
  between operations: 13.5 us -> 0.15 us
  starting transfers between devices: 4.51 us -> 17.4 us
  other arithmetic: 11.1 us -> 0 us
  Pallas kernels: 0 us -> 10 us
    psum x1 -> x0, waiting for transfers between devices: 56.9 us -> none  [on_device(): summed = lax.psum(stacked, 'rep')]
    ppermute x8 -> x20, waiting for transfers between devices: 55.8 us -> 16.8 us  [the longest x1 5.59 us: on_device(): twin = lax.ppermute(own, 'rep', [(r, (r + 1) % reps) for r in range(reps)])]
    dot_general x11 -> x1, matrix products: 28.1 us -> 0.7 us  [on_device(): hidden = jnp.dot(features, w_self, preferred_element_type=F32)]
    gather x16 -> x0, local copies, waits for them, and re-layouts: 17.5 us -> none  [absorb(): chosen = jnp.take_along_axis(tiles, picks[:, :, :, None, None], axis=2)]
    ppermute x8 -> x20, starting transfers between devices: 4.51 us -> 17.4 us  [the longest x6 10.8 us: on_device(): lax.ppermute(backward[other], 'dom', swapped(behind) if swap else behind)]
    pallas_call x0 -> x8, Pallas kernels: none -> 10 us  [the longest x2 3.87 us: absorb(): pl.pallas_call(functools.partial(absorb_body, origins, devices // 2, sums...]
    reduce_or x8 -> x0, other arithmetic: 2.45 us -> none  [absorb(): present = jnp.any(matches, axis=-1)]
    reduce_sum x8 -> x0, other arithmetic: 2.42 us -> none  [absorb(): picks = jnp.sum(jnp.where(matches, slot_ids, 0), axis=-1)]
  transfers between devices with their start and end apart: 9 -> 20, of which waited for: 9 -> 13; matrix products, arithmetic and copies ran while one was open for 25% -> 2% of each run, Pallas kernels for 0% -> 13%
where the time goes in v2:
time: 45.5 us; the launch traced here: 45.4 us
  starting transfers between devices  17.4 us (38%)
  waiting for transfers between devices  16.8 us (37%)
  Pallas kernels  10 us (22%)
  matrix products  0.7 us (2%)
    ppermute x6, starting transfers between devices, on_device(): lax.ppermute(backward[other], 'dom', swapped(behind) if swap else behind)  10.8 us
    ppermute x1, waiting for transfers between devices, on_device(): twin = lax.ppermute(own, 'rep', [(r, (r + 1) % reps) for r in range(reps)])  5.59 us
    ppermute x6, waiting for transfers between devices, on_device(): lax.ppermute(forward[other], 'dom', swapped(ahead) if swap else ahead)  4.25 us
    pallas_call x2, Pallas kernels, absorb(): pl.pallas_call(functools.partial(absorb_body, origins, devices // 2, sums...  3.87 us
    ppermute x1, waiting for transfers between devices, on_device(): diagonal = lax.ppermute(other, ('dom', 'rep'), across)  3.18 us
    ppermute x6, waiting for transfers between devices, on_device(): lax.ppermute(backward[other], 'dom', swapped(behind) if swap else behind)  2.56 us
    pallas_call x3, Pallas kernels, project(): pl.pallas_call(functools.partial(project_body, quarters, last), out_shape...  2.39 us
    pallas_call x2, Pallas kernels, close(): pl.pallas_call(functools.partial(close_body, origins, devices // 2, side)...  1.99 us
  transfers between devices with their start and end apart: 20, of which 13 were waited for; matrix products, arithmetic and copies ran while one was open for 2% of the time, Pallas kernels for 13%

profile of v2, /device:TPU:0, one launch (start us, length us, event | category | flops | bytes accessed | tf_op | source)
XLA Modules:
  0.0 45.4 jit_solution(12249415896322003595)
XLA Ops:
  0.0 0.0 copy-start
  0.0 1.8 %pack.1 = (bf16[256,256]{1,0:T(8,128)(2,1)S(1)}, bf16[256,256]{1,0:T(8,128)(2,1)S(1)}, bf16[2,2,12,128,128]{4,3,2,1,0:T(8,128)(2,1)S(1)}, s32[8,256]{1,0:T(8,128)S(1)}) custom-call(bf16[256,1024]{1,0:T(8,128)(2,1)} %features.1, bf16[2,2,12,128,128]{4,3,2,1,0:T(8,128)(2,1)} %tiles_in.1, s32[2,2,12]{2,1,0:T(2,128)} %columns_in.1, s32[2,2]{1,0:T(2,128)} %counts_in.1, ...), custom_call_target="tpu_custom_call" | custom-call | tf_op jit(solution)/shard_map/pack/pallas_call | solution.py:113
  1.8 0.5 %collective-permute-start.1 = (bf16[2,2,12,128,128]{4,3,2,1,0:T(8,128)(2,1)S(1)}, bf16[2,2,12,128,128]{4,3,2,1,0:T(8,128)(2,1)S(1)}, u32[]{:S(2)}, u32[]{:S(2)}) collective-permute-start(bf16[2,2,12,128,128]{4,3,2,1,0:T(8,128)(2,1)S(1)} %get-tuple-element.10.refs_2_.tiles), channel_id=1, source_target_pairs={{0,2},{2,0},{4,6},{6,4},{8,10},{10,8},{12,14},{14,12},{16,18},{18,... | collective-permute-start | bytes 4718600 | tf_op jit(solution)/shard_map/ppermute | solution.py:270
  2.3 2.6 %collective-permute-start.11 = (bf16[256,256]{1,0:T(8,128)(2,1)S(1)}, bf16[256,256]{1,0:T(8,128)(2,1)S(1)}, u32[]{:S(2)}, u32[]{:S(2)}) collective-permute-start(bf16[256,256]{1,0:T(8,128)(2,1)S(1)} %get-tuple-element.12), channel_id=1, source_target_pairs={{0,6},{2,4},{4,14},{6,12},{8,2},{10,0},{12,22},{14,20},{16,10},{18... | collective-permute-start | bytes 393224 | tf_op jit(solution)/shard_map/ppermute | solution.py:260
  4.9 0.1 collective-permute-start.2
  5.0 1.9 %collective-permute-start.5 = (bf16[256,256]{1,0:T(8,128)(2,1)S(1)}, bf16[256,256]{1,0:T(8,128)(2,1)S(1)}, u32[]{:S(2)}, u32[]{:S(2)}) collective-permute-start(bf16[256,256]{1,0:T(8,128)(2,1)S(1)} %get-tuple-element.11.refs_4_), channel_id=1, source_target_pairs={{0,4},{2,6},{4,12},{6,14},{8,0},{10,2},{12,20},{14,22},{16,8},{18,... | collective-permute-start | bytes 393224 | tf_op jit(solution)/shard_map/ppermute | solution.py:260
  6.9 0.0 collective-permute-start
  6.9 1.2 %collective-permute-done.refs_1_.slot_of.info = s32[8,256]{1,0:T(8,128)S(1)} collective-permute-done((s32[8,256]{1,0:T(8,128)S(1)}, s32[8,256]{1,0:T(8,128)S(1)}, u32[]{:S(2)}, u32[]{:S(2)}) %collective-permute-start) | collective-permute-done | bytes 8224 | tf_op jit(solution)/shard_map/ppermute | solution.py:269
  8.1 0.0 collective-permute-start.8
  8.1 0.7 %collective-permute-done.11.refs_9_ = bf16[256,256]{1,0:T(8,128)(2,1)S(1)} collective-permute-done((bf16[256,256]{1,0:T(8,128)(2,1)S(1)}, bf16[256,256]{1,0:T(8,128)(2,1)S(1)}, u32[]{:S(2)}, u32[]{:S(2)}) %collective-permute-start.11) | collective-permute-done | bytes 131104 | tf_op jit(solution)/shard_map/ppermute | solution.py:260
  8.8 0.6 %collective-permute-start.14 = (bf16[256,256]{1,0:T(8,128)(2,1)S(1)}, bf16[256,256]{1,0:T(8,128)(2,1)S(1)}, u32[]{:S(2)}, u32[]{:S(2)}) collective-permute-start(bf16[256,256]{1,0:T(8,128)(2,1)S(1)} %get-tuple-element.12), channel_id=1, source_target_pairs={{0,2},{2,0},{4,6},{6,4},{8,10},{10,8},{12,14},{14,12},{16,18},{18,... | collective-permute-start | bytes 393224 | tf_op jit(solution)/shard_map/ppermute | solution.py:267
  9.4 1.0 %collective-permute-done.2.refs_6_ = bf16[256,256]{1,0:T(8,128)(2,1)S(1)} collective-permute-done((bf16[256,256]{1,0:T(8,128)(2,1)S(1)}, bf16[256,256]{1,0:T(8,128)(2,1)S(1)}, u32[]{:S(2)}, u32[]{:S(2)}) %collective-permute-start.2) | collective-permute-done | bytes 131104 | tf_op jit(solution)/shard_map/ppermute | solution.py:259
  10.4 1.0 %collective-permute-start.3 = (bf16[256,256]{1,0:T(8,128)(2,1)S(1)}, bf16[256,256]{1,0:T(8,128)(2,1)S(1)}, u32[]{:S(2)}, u32[]{:S(2)}) collective-permute-start(bf16[256,256]{1,0:T(8,128)(2,1)S(1)} %collective-permute-done.2.refs_6_), channel_id=1, source_target_pairs={{0,8},{2,10},{4,0},{6,2},{8,16},{10,18},{12,4},{14,6},{16,24},{18,... | collective-permute-start | bytes 393224 | tf_op jit(solution)/shard_map/ppermute | solution.py:259
  11.4 0.4 collective-permute-done.5.refs_7_
  11.8 1.6 %collective-permute-start.12 = (bf16[256,256]{1,0:T(8,128)(2,1)S(1)}, bf16[256,256]{1,0:T(8,128)(2,1)S(1)}, u32[]{:S(2)}, u32[]{:S(2)}) collective-permute-start(bf16[256,256]{1,0:T(8,128)(2,1)S(1)} %collective-permute-done.11.refs_9_), channel_id=1, source_target_pairs={{0,4},{2,6},{4,12},{6,14},{8,0},{10,2},{12,20},{14,22},{16,8},{18,... | collective-permute-start | bytes 393224 | tf_op jit(solution)/shard_map/ppermute | solution.py:260
  13.5 0.2 collective-permute-done.8.refs_8_
  13.7 0.2 collective-permute-start.9
  13.9 0.0 collective-permute-done.14.refs_5_
  13.9 1.8 %collective-permute-start.6 = (bf16[256,256]{1,0:T(8,128)(2,1)S(1)}, bf16[256,256]{1,0:T(8,128)(2,1)S(1)}, u32[]{:S(2)}, u32[]{:S(2)}) collective-permute-start(bf16[256,256]{1,0:T(8,128)(2,1)S(1)} %collective-permute-done.5.refs_7_), channel_id=1, source_target_pairs={{0,4},{2,6},{4,12},{6,14},{8,0},{10,2},{12,20},{14,22},{16,8},{18,... | collective-permute-start | bytes 393224 | tf_op jit(solution)/shard_map/ppermute | solution.py:260
  15.7 1.1 %collective-permute-done.3.refs_10_ = bf16[256,256]{1,0:T(8,128)(2,1)S(1)} collective-permute-done((bf16[256,256]{1,0:T(8,128)(2,1)S(1)}, bf16[256,256]{1,0:T(8,128)(2,1)S(1)}, u32[]{:S(2)}, u32[]{:S(2)}) %collective-permute-start.3) | collective-permute-done | bytes 131104 | tf_op jit(solution)/shard_map/ppermute | solution.py:259
  16.8 0.1 collective-permute-start.4
  16.9 0.6 %collective-permute-done.12.refs_13_ = bf16[256,256]{1,0:T(8,128)(2,1)S(1)} collective-permute-done((bf16[256,256]{1,0:T(8,128)(2,1)S(1)}, bf16[256,256]{1,0:T(8,128)(2,1)S(1)}, u32[]{:S(2)}, u32[]{:S(2)}) %collective-permute-start.12) | collective-permute-done | bytes 131104 | tf_op jit(solution)/shard_map/ppermute | solution.py:260
  17.5 1.3 %collective-permute-start.13 = (bf16[256,256]{1,0:T(8,128)(2,1)S(1)}, bf16[256,256]{1,0:T(8,128)(2,1)S(1)}, u32[]{:S(2)}, u32[]{:S(2)}) collective-permute-start(bf16[256,256]{1,0:T(8,128)(2,1)S(1)} %collective-permute-done.12.refs_13_), channel_id=1, source_target_pairs={{0,4},{2,6},{4,12},{6,14},{8,0},{10,2},{12,20},{14,22},{16,8},{18,... | collective-permute-start | bytes 393224 | tf_op jit(solution)/shard_map/ppermute | solution.py:260
  18.8 1.0 %collective-permute-done.9.refs_12_ = bf16[256,256]{1,0:T(8,128)(2,1)S(1)} collective-permute-done((bf16[256,256]{1,0:T(8,128)(2,1)S(1)}, bf16[256,256]{1,0:T(8,128)(2,1)S(1)}, u32[]{:S(2)}, u32[]{:S(2)}) %collective-permute-start.9) | collective-permute-done | bytes 131104 | tf_op jit(solution)/shard_map/ppermute | solution.py:259
  19.8 0.0 collective-permute-start.10
  19.9 0.5 %collective-permute-done.6.refs_11_ = bf16[256,256]{1,0:T(8,128)(2,1)S(1)} collective-permute-done((bf16[256,256]{1,0:T(8,128)(2,1)S(1)}, bf16[256,256]{1,0:T(8,128)(2,1)S(1)}, u32[]{:S(2)}, u32[]{:S(2)}) %collective-permute-start.6) | collective-permute-done | bytes 131104 | tf_op jit(solution)/shard_map/ppermute | solution.py:260
  20.3 1.5 %collective-permute-start.7 = (bf16[256,256]{1,0:T(8,128)(2,1)S(1)}, bf16[256,256]{1,0:T(8,128)(2,1)S(1)}, u32[]{:S(2)}, u32[]{:S(2)}) collective-permute-start(bf16[256,256]{1,0:T(8,128)(2,1)S(1)} %collective-permute-done.6.refs_11_), channel_id=1, source_target_pairs={{0,4},{2,6},{4,12},{6,14},{8,0},{10,2},{12,20},{14,22},{16,8},{18,... | collective-permute-start | bytes 393224 | tf_op jit(solution)/shard_map/ppermute | solution.py:260
  21.9 1.0 %collective-permute-done.4.refs_4_ = bf16[256,256]{1,0:T(8,128)(2,1)S(1)} collective-permute-done((bf16[256,256]{1,0:T(8,128)(2,1)S(1)}, bf16[256,256]{1,0:T(8,128)(2,1)S(1)}, u32[]{:S(2)}, u32[]{:S(2)}) %collective-permute-start.4) | collective-permute-done | bytes 131104 | tf_op jit(solution)/shard_map/ppermute | solution.py:259
  22.8 0.0 collective-permute-start.15
  22.9 0.4 collective-permute-done.13.refs_7_
  23.2 1.6 %collective-permute-start.16 = (bf16[256,256]{1,0:T(8,128)(2,1)S(1)}, bf16[256,256]{1,0:T(8,128)(2,1)S(1)}, u32[]{:S(2)}, u32[]{:S(2)}) collective-permute-start(bf16[256,256]{1,0:T(8,128)(2,1)S(1)} %collective-permute-done.13.refs_7_), channel_id=1, source_target_pairs={{0,4},{2,6},{4,12},{6,14},{8,0},{10,2},{12,20},{14,22},{16,8},{18,... | collective-permute-start | bytes 393224 | tf_op jit(solution)/shard_map/ppermute | solution.py:265
  24.9 0.0 collective-permute-done.1.refs_3_.tiles
  24.9 2.3 %absorb.2.refs_8_ = f32[2,2,256,256]{3,2,1,0:T(8,128)S(1)} custom-call(s32[8,256]{1,0:T(8,128)S(1)} %get-tuple-element.9.refs_0_.slot_of.info, s32[8,256]{1,0:T(8,128)S(1)} %collective-permute-done.refs_1_.slot_of.info, bf16[2,2,12,128,128]{4,3,2,1,0:T(8,128)(2,1)S(1)} %get-tuple-element.10.refs_2_.tiles, ...), custom_call_target="tpu_custom_call" | custom-call | flops 1342177280 | tf_op jit(solution)/shard_map/absorb/pallas_call | solution.py:168
  27.2 0.0 collective-permute-done.10.refs_6_
  27.2 0.0 collective-permute-done.7.refs_5_
  27.2 1.5 %absorb.3.sums = f32[2,2,256,256]{3,2,1,0:T(8,128)S(1)} custom-call(s32[8,256]{1,0:T(8,128)S(1)} %get-tuple-element.9.refs_0_.slot_of.info, s32[8,256]{1,0:T(8,128)S(1)} %collective-permute-done.refs_1_.slot_of.info, bf16[2,2,12,128,128]{4,3,2,1,0:T(8,128)(2,1)S(1)} %get-tuple-element.10.refs_2_.tiles, ...), custom_call_target="tpu_custom_call" | custom-call | flops 536870912 | tf_op jit(solution)/shard_map/absorb/pallas_call | solution.py:168
  28.8 0.0 collective-permute-done.15.refs_0_
  28.8 0.0 collective-permute-done.16.refs_1_
  28.8 1.0 %close.3 = bf16[2,256,256]{2,1,0:T(8,128)(2,1)S(1)} custom-call(s32[8,256]{1,0:T(8,128)S(1)} %collective-permute-done.refs_1_.slot_of.info, s32[8,256]{1,0:T(8,128)S(1)} %collective-permute-done.refs_1_.slot_of.info, bf16[2,2,12,128,128]{4,3,2,1,0:T(8,128)(2,1)S(1)} %collective-permute-done.1.refs_3_.tiles, f32[2,2,256,256]{3,2,1,0:T(8,128)S(1)} %absorb.3.sums, ...), custom_call_target="tpu_custom_call" | custom-call | tf_op jit(solution)/shard_map/close/pallas_call | solution.py:204
  29.8 0.0 copy-start.3
  29.8 0.1 collective-permute-start.17
  29.9 1.6 %collective-permute-start.18 = (bf16[2,256,256]{2,1,0:T(8,128)(2,1)S(1)}, bf16[2,256,256]{2,1,0:T(8,128)(2,1)S(1)}, u32[]{:S(2)}, u32[]{:S(2)}) collective-permute-start(bf16[2,256,256]{2,1,0:T(8,128)(2,1)S(1)} %close.3), channel_id=1, source_target_pairs={{0,3},{1,2},{2,1},{3,0},{4,7},{5,6},{6,5},{7,4},{8,11},{9,10},{10,... | collective-permute-start | bytes 786440 | tf_op jit(solution)/shard_map/ppermute | solution.py:281
  31.5 0.0 copy-start.2
  31.5 1.0 %close.2.refs_0_ = bf16[2,256,256]{2,1,0:T(8,128)(2,1)S(1)} custom-call(s32[8,256]{1,0:T(8,128)S(1)} %get-tuple-element.9.refs_0_.slot_of.info, s32[8,256]{1,0:T(8,128)S(1)} %get-tuple-element.9.refs_0_.slot_of.info, bf16[2,2,12,128,128]{4,3,2,1,0:T(8,128)(2,1)S(1)} %get-tuple-element.10.refs_2_.tiles, f32[2,2,256,256]{3,2,1,0:T(8,128)S(1)} %absorb.3.sums, ...), custom_call_target="tpu_custom_call" | custom-call | tf_op jit(solution)/shard_map/close/pallas_call | solution.py:204
  32.5 0.0 copy-start.1
  32.5 0.6 %collective-permute-start.19 = (bf16[2,256,256]{2,1,0:T(8,128)(2,1)S(1)}, bf16[2,256,256]{2,1,0:T(8,128)(2,1)S(1)}, u32[]{:S(2)}, u32[]{:S(2)}) collective-permute-start(bf16[2,256,256]{2,1,0:T(8,128)(2,1)S(1)} %close.2.refs_0_), channel_id=1, source_target_pairs={{0,1},{1,0},{2,3},{3,2},{4,5},{5,4},{6,7},{7,6},{8,9},{9,8},{10,11... | collective-permute-start | bytes 786440 | tf_op jit(solution)/shard_map/ppermute | solution.py:283
  33.1 0.0 copy-done
  33.1 0.0 copy-done.3
  33.1 0.7 %fusion.base = f32[256,1024]{1,0:T(8,128)S(1)} fusion(bf16[256,1024]{1,0:T(8,128)(2,1)S(1)} %copy-done.3, bf16[1024,1024]{1,0:T(8,128)(2,1)S(1)} %copy-done), kind=kOutput, calls=%fused_computation | convolution fusion | flops 536870912 | bytes 3670016 | tf_op jit(solution)/shard_map/dot_general | solution.py:285
  33.8 0.0 collective-permute-done.17.refs_1_
  33.8 0.0 copy-done.2
  33.8 0.4 copy-done.1
  34.2 0.7 %project.3.base = f32[256,1024]{1,0:T(8,128)S(1)} custom-call(f32[256,1024]{1,0:T(8,128)S(1)} %fusion.base, bf16[1024,1024]{1,0:T(8,128)(2,1)S(1)} %copy-done.1, bf16[1024,1024]{1,0:T(8,128)(2,1)S(1)} %copy-done.2, bf16[2,256,256]{2,1,0:T(8,128)(2,1)S(1)} %close.2.refs_0_, bf16[2,256,256]{2,1,0:T(8,128)(2,1)S(1)} %collective-permute-done.17.refs_1_), custom_call_target="tpu_custom_call" | custom-call | flops 536870912 | tf_op jit(solution)/shard_map/project/pallas_call | solution.py:229
  35.0 3.2 %collective-permute-done.18.refs_0_ = bf16[2,256,256]{2,1,0:T(8,128)(2,1)S(1)} collective-permute-done((bf16[2,256,256]{2,1,0:T(8,128)(2,1)S(1)}, bf16[2,256,256]{2,1,0:T(8,128)(2,1)S(1)}, u32[]{:S(2)}, u32[]{:S(2)}) %collective-permute-start.18) | collective-permute-done | bytes 262176 | tf_op jit(solution)/shard_map/ppermute | solution.py:281
  38.1 0.4 project.4.base
  38.6 5.6 %collective-permute-done.19.refs_0_ = bf16[2,256,256]{2,1,0:T(8,128)(2,1)S(1)} collective-permute-done((bf16[2,256,256]{2,1,0:T(8,128)(2,1)S(1)}, bf16[2,256,256]{2,1,0:T(8,128)(2,1)S(1)}, u32[]{:S(2)}, u32[]{:S(2)}) %collective-permute-start.19) | collective-permute-done | bytes 262176 | tf_op jit(solution)/shard_map/ppermute | solution.py:283
  44.2 1.2 %project.5 = bf16[256,1024]{1,0:T(8,128)(2,1)} custom-call(f32[256,1024]{1,0:T(8,128)S(1)} %project.4.base, bf16[1024,1024]{1,0:T(8,128)(2,1)S(1)} %copy-done.1, bf16[1024,1024]{1,0:T(8,128)(2,1)S(1)} %copy-done.2, bf16[2,256,256]{2,1,0:T(8,128)(2,1)S(1)} %collective-permute-done.19.refs_0_), custom_call_target="tpu_custom_call" | custom-call | flops 268435456 | tf_op jit(solution)/shard_map/project/pallas_call | solution.py:229
Async XLA Ops:
  0.0 33.1 %copy-start = (bf16[1024,1024]{1,0:T(8,128)(2,1)S(1)}, bf16[1024,1024]{1,0:T(8,128)(2,1)}, u32[]{:S(2)}) copy-start(bf16[1024,1024]{1,0:T(8,128)(2,1)} %param.13) | copy-start | bytes 6291460
  1.8 23.1 %collective-permute-start.1 = (bf16[2,2,12,128,128]{4,3,2,1,0:T(8,128)(2,1)S(1)}, bf16[2,2,12,128,128]{4,3,2,1,0:T(8,128)(2,1)S(1)}, u32[]{:S(2)}, u32[]{:S(2)}) collective-permute-start(bf16[2,2,12,128,128]{4,3,2,1,0:T(8,128)(2,1)S(1)} %get-tuple-element.10.refs_2_.tiles), channel_id=1, source_target_pairs={{0,2},{2,0},{4,6},{6,4},{8,10},{10,8},{12,14},{14,12},{16,18},{18,... | collective-permute-start | bytes 4718600 | tf_op jit(solution)/shard_map/ppermute | solution.py:270
  2.3 6.5 %collective-permute-start.11 = (bf16[256,256]{1,0:T(8,128)(2,1)S(1)}, bf16[256,256]{1,0:T(8,128)(2,1)S(1)}, u32[]{:S(2)}, u32[]{:S(2)}) collective-permute-start(bf16[256,256]{1,0:T(8,128)(2,1)S(1)} %get-tuple-element.12), channel_id=1, source_target_pairs={{0,6},{2,4},{4,14},{6,12},{8,2},{10,0},{12,22},{14,20},{16,10},{18... | collective-permute-start | bytes 393224 | tf_op jit(solution)/shard_map/ppermute | solution.py:260
  4.9 5.5 %collective-permute-start.2 = (bf16[256,256]{1,0:T(8,128)(2,1)S(1)}, bf16[256,256]{1,0:T(8,128)(2,1)S(1)}, u32[]{:S(2)}, u32[]{:S(2)}) collective-permute-start(bf16[256,256]{1,0:T(8,128)(2,1)S(1)} %get-tuple-element.11.refs_4_), channel_id=1, source_target_pairs={{0,8},{2,10},{4,0},{6,2},{8,16},{10,18},{12,4},{14,6},{16,24},{18,... | collective-permute-start | bytes 393224 | tf_op jit(solution)/shard_map/ppermute | solution.py:259
  5.0 6.8 %collective-permute-start.5 = (bf16[256,256]{1,0:T(8,128)(2,1)S(1)}, bf16[256,256]{1,0:T(8,128)(2,1)S(1)}, u32[]{:S(2)}, u32[]{:S(2)}) collective-permute-start(bf16[256,256]{1,0:T(8,128)(2,1)S(1)} %get-tuple-element.11.refs_4_), channel_id=1, source_target_pairs={{0,4},{2,6},{4,12},{6,14},{8,0},{10,2},{12,20},{14,22},{16,8},{18,... | collective-permute-start | bytes 393224 | tf_op jit(solution)/shard_map/ppermute | solution.py:260
  6.9 1.2 %collective-permute-start = (s32[8,256]{1,0:T(8,128)S(1)}, s32[8,256]{1,0:T(8,128)S(1)}, u32[]{:S(2)}, u32[]{:S(2)}) collective-permute-start(s32[8,256]{1,0:T(8,128)S(1)} %get-tuple-element.9.refs_0_.slot_of.info), channel_id=1, source_target_pairs={{0,2},{2,0},{4,6},{6,4},{8,10},{10,8},{12,14},{14,12},{16,18},{18,... | collective-permute-start | bytes 24584 | tf_op jit(solution)/shard_map/ppermute | solution.py:269
  8.1 5.5 %collective-permute-start.8 = (bf16[256,256]{1,0:T(8,128)(2,1)S(1)}, bf16[256,256]{1,0:T(8,128)(2,1)S(1)}, u32[]{:S(2)}, u32[]{:S(2)}) collective-permute-start(bf16[256,256]{1,0:T(8,128)(2,1)S(1)} %get-tuple-element.12), channel_id=1, source_target_pairs={{0,10},{2,8},{4,2},{6,0},{8,18},{10,16},{12,6},{14,4},{16,26},{18,... | collective-permute-start | bytes 393224 | tf_op jit(solution)/shard_map/ppermute | solution.py:259
  8.8 5.1 %collective-permute-start.14 = (bf16[256,256]{1,0:T(8,128)(2,1)S(1)}, bf16[256,256]{1,0:T(8,128)(2,1)S(1)}, u32[]{:S(2)}, u32[]{:S(2)}) collective-permute-start(bf16[256,256]{1,0:T(8,128)(2,1)S(1)} %get-tuple-element.12), channel_id=1, source_target_pairs={{0,2},{2,0},{4,6},{6,4},{8,10},{10,8},{12,14},{14,12},{16,18},{18,... | collective-permute-start | bytes 393224 | tf_op jit(solution)/shard_map/ppermute | solution.py:267
  10.4 6.4 %collective-permute-start.3 = (bf16[256,256]{1,0:T(8,128)(2,1)S(1)}, bf16[256,256]{1,0:T(8,128)(2,1)S(1)}, u32[]{:S(2)}, u32[]{:S(2)}) collective-permute-start(bf16[256,256]{1,0:T(8,128)(2,1)S(1)} %collective-permute-done.2.refs_6_), channel_id=1, source_target_pairs={{0,8},{2,10},{4,0},{6,2},{8,16},{10,18},{12,4},{14,6},{16,24},{18,... | collective-permute-start | bytes 393224 | tf_op jit(solution)/shard_map/ppermute | solution.py:259
  11.8 5.7 %collective-permute-start.12 = (bf16[256,256]{1,0:T(8,128)(2,1)S(1)}, bf16[256,256]{1,0:T(8,128)(2,1)S(1)}, u32[]{:S(2)}, u32[]{:S(2)}) collective-permute-start(bf16[256,256]{1,0:T(8,128)(2,1)S(1)} %collective-permute-done.11.refs_9_), channel_id=1, source_target_pairs={{0,4},{2,6},{4,12},{6,14},{8,0},{10,2},{12,20},{14,22},{16,8},{18,... | collective-permute-start | bytes 393224 | tf_op jit(solution)/shard_map/ppermute | solution.py:260
  13.7 6.2 %collective-permute-start.9 = (bf16[256,256]{1,0:T(8,128)(2,1)S(1)}, bf16[256,256]{1,0:T(8,128)(2,1)S(1)}, u32[]{:S(2)}, u32[]{:S(2)}) collective-permute-start(bf16[256,256]{1,0:T(8,128)(2,1)S(1)} %collective-permute-done.8.refs_8_), channel_id=1, source_target_pairs={{0,8},{2,10},{4,0},{6,2},{8,16},{10,18},{12,4},{14,6},{16,24},{18,... | collective-permute-start | bytes 393224 | tf_op jit(solution)/shard_map/ppermute | solution.py:259
  13.9 6.5 %collective-permute-start.6 = (bf16[256,256]{1,0:T(8,128)(2,1)S(1)}, bf16[256,256]{1,0:T(8,128)(2,1)S(1)}, u32[]{:S(2)}, u32[]{:S(2)}) collective-permute-start(bf16[256,256]{1,0:T(8,128)(2,1)S(1)} %collective-permute-done.5.refs_7_), channel_id=1, source_target_pairs={{0,4},{2,6},{4,12},{6,14},{8,0},{10,2},{12,20},{14,22},{16,8},{18,... | collective-permute-start | bytes 393224 | tf_op jit(solution)/shard_map/ppermute | solution.py:260
  16.8 6.0 %collective-permute-start.4 = (bf16[256,256]{1,0:T(8,128)(2,1)S(1)}, bf16[256,256]{1,0:T(8,128)(2,1)S(1)}, u32[]{:S(2)}, u32[]{:S(2)}) collective-permute-start(bf16[256,256]{1,0:T(8,128)(2,1)S(1)} %collective-permute-done.3.refs_10_), channel_id=1, source_target_pairs={{0,8},{2,10},{4,0},{6,2},{8,16},{10,18},{12,4},{14,6},{16,24},{18,... | collective-permute-start | bytes 393224 | tf_op jit(solution)/shard_map/ppermute | solution.py:259
  17.5 5.7 %collective-permute-start.13 = (bf16[256,256]{1,0:T(8,128)(2,1)S(1)}, bf16[256,256]{1,0:T(8,128)(2,1)S(1)}, u32[]{:S(2)}, u32[]{:S(2)}) collective-permute-start(bf16[256,256]{1,0:T(8,128)(2,1)S(1)} %collective-permute-done.12.refs_13_), channel_id=1, source_target_pairs={{0,4},{2,6},{4,12},{6,14},{8,0},{10,2},{12,20},{14,22},{16,8},{18,... | collective-permute-start | bytes 393224 | tf_op jit(solution)/shard_map/ppermute | solution.py:260
  19.8 7.4 %collective-permute-start.10 = (bf16[256,256]{1,0:T(8,128)(2,1)S(1)}, bf16[256,256]{1,0:T(8,128)(2,1)S(1)}, u32[]{:S(2)}, u32[]{:S(2)}) collective-permute-start(bf16[256,256]{1,0:T(8,128)(2,1)S(1)} %collective-permute-done.9.refs_12_), channel_id=1, source_target_pairs={{0,8},{2,10},{4,0},{6,2},{8,16},{10,18},{12,4},{14,6},{16,24},{18,... | collective-permute-start | bytes 393224 | tf_op jit(solution)/shard_map/ppermute | solution.py:259
  20.3 6.9 %collective-permute-start.7 = (bf16[256,256]{1,0:T(8,128)(2,1)S(1)}, bf16[256,256]{1,0:T(8,128)(2,1)S(1)}, u32[]{:S(2)}, u32[]{:S(2)}) collective-permute-start(bf16[256,256]{1,0:T(8,128)(2,1)S(1)} %collective-permute-done.6.refs_11_), channel_id=1, source_target_pairs={{0,4},{2,6},{4,12},{6,14},{8,0},{10,2},{12,20},{14,22},{16,8},{18,... | collective-permute-start | bytes 393224 | tf_op jit(solution)/shard_map/ppermute | solution.py:260
  22.8 5.9 %collective-permute-start.15 = (bf16[256,256]{1,0:T(8,128)(2,1)S(1)}, bf16[256,256]{1,0:T(8,128)(2,1)S(1)}, u32[]{:S(2)}, u32[]{:S(2)}) collective-permute-start(bf16[256,256]{1,0:T(8,128)(2,1)S(1)} %collective-permute-done.4.refs_4_), channel_id=1, source_target_pairs={{0,8},{2,10},{4,0},{6,2},{8,16},{10,18},{12,4},{14,6},{16,24},{18,... | collective-permute-start | bytes 393224 | tf_op jit(solution)/shard_map/ppermute | solution.py:264
  23.2 5.5 %collective-permute-start.16 = (bf16[256,256]{1,0:T(8,128)(2,1)S(1)}, bf16[256,256]{1,0:T(8,128)(2,1)S(1)}, u32[]{:S(2)}, u32[]{:S(2)}) collective-permute-start(bf16[256,256]{1,0:T(8,128)(2,1)S(1)} %collective-permute-done.13.refs_7_), channel_id=1, source_target_pairs={{0,4},{2,6},{4,12},{6,14},{8,0},{10,2},{12,20},{14,22},{16,8},{18,... | collective-permute-start | bytes 393224 | tf_op jit(solution)/shard_map/ppermute | solution.py:265
  29.8 3.3 %copy-start.3 = (bf16[256,1024]{1,0:T(8,128)(2,1)S(1)}, bf16[256,1024]{1,0:T(8,128)(2,1)}, u32[]{:S(2)}) copy-start(bf16[256,1024]{1,0:T(8,128)(2,1)} %features.1) | copy-start | bytes 1572868
  29.8 4.0 %collective-permute-start.17 = (bf16[2,256,256]{2,1,0:T(8,128)(2,1)S(1)}, bf16[2,256,256]{2,1,0:T(8,128)(2,1)S(1)}, u32[]{:S(2)}, u32[]{:S(2)}) collective-permute-start(bf16[2,256,256]{2,1,0:T(8,128)(2,1)S(1)} %close.3), channel_id=1, source_target_pairs={{0,2},{2,0},{4,6},{6,4},{8,10},{10,8},{12,14},{14,12},{16,18},{18,... | collective-permute-start | bytes 786440 | tf_op jit(solution)/shard_map/ppermute | solution.py:282
  29.9 8.3 %collective-permute-start.18 = (bf16[2,256,256]{2,1,0:T(8,128)(2,1)S(1)}, bf16[2,256,256]{2,1,0:T(8,128)(2,1)S(1)}, u32[]{:S(2)}, u32[]{:S(2)}) collective-permute-start(bf16[2,256,256]{2,1,0:T(8,128)(2,1)S(1)} %close.3), channel_id=1, source_target_pairs={{0,3},{1,2},{2,1},{3,0},{4,7},{5,6},{6,5},{7,4},{8,11},{9,10},{10,... | collective-permute-start | bytes 786440 | tf_op jit(solution)/shard_map/ppermute | solution.py:281
  31.5 2.3 %copy-start.2 = (bf16[1024,1024]{1,0:T(8,128)(2,1)S(1)}, bf16[1024,1024]{1,0:T(8,128)(2,1)}, u32[]{:S(2)}) copy-start(bf16[1024,1024]{1,0:T(8,128)(2,1)} %w_out.5) | copy-start | bytes 6291460
  32.5 1.7 %copy-start.1 = (bf16[1024,1024]{1,0:T(8,128)(2,1)S(1)}, bf16[1024,1024]{1,0:T(8,128)(2,1)}, u32[]{:S(2)}) copy-start(bf16[1024,1024]{1,0:T(8,128)(2,1)} %w_in.5) | copy-start | bytes 6291460
  32.5 11.7 %collective-permute-start.19 = (bf16[2,256,256]{2,1,0:T(8,128)(2,1)S(1)}, bf16[2,256,256]{2,1,0:T(8,128)(2,1)S(1)}, u32[]{:S(2)}, u32[]{:S(2)}) collective-permute-start(bf16[2,256,256]{2,1,0:T(8,128)(2,1)S(1)} %close.2.refs_0_), channel_id=1, source_target_pairs={{0,1},{1,0},{2,3},{3,2},{4,5},{5,4},{6,7},{7,6},{8,9},{9,8},{10,11... | collective-permute-start | bytes 786440 | tf_op jit(solution)/shard_map/ppermute | solution.py:283

commit v3 on v2

--- a/solution.py
+++ b/solution.py
@@ -41,28 +41,22 @@
     return [(d, d ^ 1) for d in range(devices)]
 
 
-def chip_at(place, chips):
-    place = lax.rem(place + 2 * chips, chips)
-    return jnp.where(place < chips // 2, 2 * place, 2 * (chips - 1 - place) + 1)
-
-
 def place_of(chip, chips):
     side = lax.rem(chip, 2)
     rung = chip // 2
     return jnp.where(side == 0, rung, chips - 1 - rung)
 
 
-def source_device(offset, other, chips):
+def lane(offset, other, block, local):
+    return (offset * 2 + other) * local + block
+
+
+def pack_body(chips, features, tiles_in, columns_in, counts_in, degrees_in, *refs):
+    mine, theirs, tiles, info, columns, counts, degrees, arrived = refs
+    rep = lax.axis_index("rep")
     position = lax.axis_index("dom")
     core = lax.rem(position, 2)
-    chip = chip_at(place_of(position // 2, chips) + offset, chips)
-    return 2 * chip + (1 - core if other else core)
-
-
-def pack_body(blocks, features, tiles_in, columns_in, counts_in, degrees_in, *refs):
-    mine, theirs, tiles, info, columns, counts, degrees, arrived = refs
-    rep = lax.axis_index("rep")
-    core = lax.rem(lax.axis_index("dom"), 2)
+    here = place_of(position // 2, chips)
     width = mine.shape[1]
 
     def quarter(core_of):
@@ -92,8 +86,12 @@
             live = counts[relation, row]
             slot_of = jnp.full(place.shape, -1, jnp.int32)
             for slot in range(slots):
-                target = jnp.where(slot < live, columns[relation, row, slot], -1)
-                slot_of = jnp.where(place == target, slot, slot_of)
+                column = columns[relation, row, slot]
+                source = column // local
+                offset = lax.rem(place_of(source // 2, chips) - here + chips, chips)
+                other = lax.rem(lax.rem(source, 2) + core, 2)
+                target = lane(offset, other, lax.rem(column, local), local)
+                slot_of = jnp.where(place == jnp.where(slot < live, target, -1), slot, slot_of)
             index = relation * local + row
             info[index : index + 1, :] = slot_of
     info[2 * local : 2 * local + 2, 0 : degrees.shape[1]] = degrees[...]
@@ -111,7 +109,7 @@
         for x in (features, tiles, columns, counts, degrees)
     ]
     return pl.pallas_call(
-        functools.partial(pack_body, blocks),
+        functools.partial(pack_body, devices // 2),
         out_shape=[piece, piece, jax.ShapeDtypeStruct(tiles.shape, BF16), info],
         in_specs=[HBM] * 5,
         out_specs=[VMEM] * 4,
@@ -126,13 +124,16 @@
     )(*operands)
 
 
-def contribution(slot_of, tiles, relation, row, pieces, sources):
+def contribution(info, tiles, relation, row, side, pieces, origins, chips):
     local = tiles.shape[1]
+    index = relation * local + row
+    slots = info[index : index + 1, :]
     total = None
-    for piece, source in zip(pieces, sources):
+    for piece, (offset, other) in zip(pieces, origins):
         weights = []
         for block in range(local):
-            slot = slot_of[relation * local + row, source * local + block]
+            at = lane(offset % chips, other ^ side, block, local)
+            slot = slots[0, at]
             one = tiles[relation, row, jnp.maximum(slot, 0)]
             weights.append(jnp.where(slot >= 0, one, jnp.zeros_like(one)))
         part = jnp.dot(
@@ -143,18 +144,19 @@
 
 
 def absorb_body(origins, chips, seeded, *refs):
-    slot_of, tiles = refs[0:2], refs[2:4]
+    infos, tiles = refs[0:2], refs[2:4]
     count = len(origins)
     pieces = refs[4 : 4 + count]
     seed = refs[4 + count] if seeded else None
     sums = refs[-1]
     tile = tiles[0].shape[-1]
-    sources = [source_device(offset, other, chips) for offset, other in origins]
     for side in range(2):
         for relation in range(2):
             for row in range(tiles[side].shape[1]):
                 span = slice(row * tile, (row + 1) * tile)
-                part = contribution(slot_of[side], tiles[side], relation, row, pieces, sources)
+                part = contribution(
+                    infos[side], tiles[side], relation, row, side, pieces, origins, chips
+                )
                 if seeded:
                     part = part + seed[side, relation, span, :]
                 sums[side, relation, span, :] = part
@@ -168,7 +170,7 @@
     return pl.pallas_call(
         functools.partial(absorb_body, origins, devices // 2, sums is not None),
         out_shape=jax.ShapeDtypeStruct((2, 2, rows, width), F32),
-        in_specs=[SMEM] * 2 + [VMEM] * (2 + len(pieces) + len(seeds)),
+        in_specs=[VMEM] * (4 + len(pieces) + len(seeds)),
         out_specs=VMEM,
         compiler_params=params(32),
         cost_estimate=pl.CostEstimate(
@@ -178,19 +180,19 @@
     )(*infos, *tiles, *[piece for piece, _, _ in pieces], *seeds)
 
 
-def close_body(origins, chips, side, slot_of, info, tiles, sums, *refs):
+def close_body(origins, chips, side, info, tiles, sums, *refs):
     pieces, out = refs[:-1], refs[-1]
     tile = tiles.shape[-1]
     local = tiles.shape[1]
-    sources = [source_device(offset, other, chips) for offset, other in origins]
     for relation in range(2):
         for row in range(local):
             span = slice(row * tile, (row + 1) * tile)
             total = sums[side, relation, span, :]
-            if pieces:
-                total = total + contribution(slot_of, tiles, relation, row, pieces, sources)
+            total = total + contribution(
+                info, tiles, relation, row, side, pieces, origins, chips
+            )
             index = 2 * local + relation
-            degree = info[index : index + 1, row * tile : (row + 1) * tile].astype(F32)
+            degree = info[index : index + 1, span].astype(F32)
             degree = jnp.broadcast_to(degree, (tile, tile)).T
             for start in range(0, total.shape[1], tile):
                 part = total[:, start : start + tile] / degree
@@ -204,11 +206,11 @@
     return pl.pallas_call(
         functools.partial(close_body, origins, devices // 2, side),
         out_shape=jax.ShapeDtypeStruct((2, rows, width), BF16),
-        in_specs=[SMEM] + [VMEM] * (3 + len(pieces)),
+        in_specs=[VMEM] * (3 + len(pieces)),
         out_specs=VMEM,
         compiler_params=params(32),
         name="close",
-    )(infos[side], infos[side], tiles[side], sums, *[piece for piece, _, _ in pieces])
+    )(infos[side], tiles[side], sums, *[piece for piece, _, _ in pieces])
 
 
 def project_body(quarters, last, base, w_in, w_out, *refs):

time: 45.5 us -> 44.6 us (0.980)
  Pallas kernels: 10 us -> 7.51 us
  waiting for transfers between devices: 16.8 us -> 18.2 us
    pallas_call x2, Pallas kernels: 3.87 us -> 2.47 us  [absorb(): pl.pallas_call(functools.partial(absorb_body, origins, devices // 2, sums...]
    pallas_call x2, Pallas kernels: 1.99 us -> 0.77 us  [close(): pl.pallas_call(functools.partial(close_body, origins, devices // 2, side)...]
  transfers between devices with their start and end apart: 20 -> 20, of which waited for: 13 -> 16; matrix products, arithmetic and copies ran while one was open for 2% -> 2% of each run, Pallas kernels for 13% -> 9%
where the time goes in v3:
time: 44.6 us; the launch traced here: 44.5 us
  waiting for transfers between devices  18.2 us (41%)
  starting transfers between devices  17.4 us (39%)
  Pallas kernels  7.51 us (17%)
  matrix products  0.7 us (2%)
  local copies, waits for them, and re-layouts  0.56 us (1%)
    ppermute x6, starting transfers between devices, on_device(): lax.ppermute(backward[other], 'dom', swapped(behind) if swap else behind)  10.8 us
    ppermute x1, waiting for transfers between devices, on_device(): twin = lax.ppermute(own, 'rep', [(r, (r + 1) % reps) for r in range(reps)])  5.63 us
    ppermute x6, waiting for transfers between devices, on_device(): lax.ppermute(forward[other], 'dom', swapped(ahead) if swap else ahead)  4.25 us
    ppermute x1, waiting for transfers between devices, on_device(): diagonal = lax.ppermute(other, ('dom', 'rep'), across)  3.6 us
    ppermute x6, waiting for transfers between devices, on_device(): lax.ppermute(backward[other], 'dom', swapped(behind) if swap else behind)  2.8 us
    pallas_call x2, Pallas kernels, absorb(): pl.pallas_call(functools.partial(absorb_body, origins, devices // 2, sums...  2.47 us
    pallas_call x3, Pallas kernels, project(): pl.pallas_call(functools.partial(project_body, quarters, last), out_shape...  2.39 us
    pallas_call x1, Pallas kernels, pack(): pl.pallas_call(functools.partial(pack_body, devices // 2), out_shape=[pie...  1.88 us
  transfers between devices with their start and end apart: 20, of which 16 were waited for; matrix products, arithmetic and copies ran while one was open for 2% of the time, Pallas kernels for 9%

profile of v3, /device:TPU:0, one launch (start us, length us, event | category | flops | bytes accessed | tf_op | source)
XLA Modules:
  0.0 44.5 jit_solution(7155255423033252402)
XLA Ops:
  0.0 0.0 copy-start
  0.0 1.9 %pack.1 = (bf16[256,256]{1,0:T(8,128)(2,1)S(1)}, bf16[256,256]{1,0:T(8,128)(2,1)S(1)}, bf16[2,2,12,128,128]{4,3,2,1,0:T(8,128)(2,1)S(1)}, s32[8,256]{1,0:T(8,128)S(1)}) custom-call(bf16[256,1024]{1,0:T(8,128)(2,1)} %features.1, bf16[2,2,12,128,128]{4,3,2,1,0:T(8,128)(2,1)} %tiles_in.1, s32[2,2,12]{2,1,0:T(2,128)} %columns_in.1, s32[2,2]{1,0:T(2,128)} %counts_in.1, ...), custom_call_target="tpu_custom_call" | custom-call | tf_op jit(solution)/shard_map/pack/pallas_call | solution.py:111
  1.9 0.5 %collective-permute-start.1 = (bf16[2,2,12,128,128]{4,3,2,1,0:T(8,128)(2,1)S(1)}, bf16[2,2,12,128,128]{4,3,2,1,0:T(8,128)(2,1)S(1)}, u32[]{:S(2)}, u32[]{:S(2)}) collective-permute-start(bf16[2,2,12,128,128]{4,3,2,1,0:T(8,128)(2,1)S(1)} %get-tuple-element.10.refs_2_.tiles), channel_id=1, source_target_pairs={{0,2},{2,0},{4,6},{6,4},{8,10},{10,8},{12,14},{14,12},{16,18},{18,... | collective-permute-start | bytes 4718600 | tf_op jit(solution)/shard_map/ppermute | solution.py:272
  2.4 2.6 %collective-permute-start.11 = (bf16[256,256]{1,0:T(8,128)(2,1)S(1)}, bf16[256,256]{1,0:T(8,128)(2,1)S(1)}, u32[]{:S(2)}, u32[]{:S(2)}) collective-permute-start(bf16[256,256]{1,0:T(8,128)(2,1)S(1)} %get-tuple-element.12), channel_id=1, source_target_pairs={{0,6},{2,4},{4,14},{6,12},{8,2},{10,0},{12,22},{14,20},{16,10},{18... | collective-permute-start | bytes 393224 | tf_op jit(solution)/shard_map/ppermute | solution.py:262
  5.0 0.1 collective-permute-start.2
  5.1 1.9 %collective-permute-start.5 = (bf16[256,256]{1,0:T(8,128)(2,1)S(1)}, bf16[256,256]{1,0:T(8,128)(2,1)S(1)}, u32[]{:S(2)}, u32[]{:S(2)}) collective-permute-start(bf16[256,256]{1,0:T(8,128)(2,1)S(1)} %get-tuple-element.11.refs_4_), channel_id=1, source_target_pairs={{0,4},{2,6},{4,12},{6,14},{8,0},{10,2},{12,20},{14,22},{16,8},{18,... | collective-permute-start | bytes 393224 | tf_op jit(solution)/shard_map/ppermute | solution.py:262
  7.1 0.0 collective-permute-start
  7.1 1.2 %collective-permute-done.refs_1_.info = s32[8,256]{1,0:T(8,128)S(1)} collective-permute-done((s32[8,256]{1,0:T(8,128)S(1)}, s32[8,256]{1,0:T(8,128)S(1)}, u32[]{:S(2)}, u32[]{:S(2)}) %collective-permute-start) | collective-permute-done | bytes 8224 | tf_op jit(solution)/shard_map/ppermute | solution.py:271
  8.2 0.0 collective-permute-start.8
  8.2 0.7 %collective-permute-done.11.refs_9_ = bf16[256,256]{1,0:T(8,128)(2,1)S(1)} collective-permute-done((bf16[256,256]{1,0:T(8,128)(2,1)S(1)}, bf16[256,256]{1,0:T(8,128)(2,1)S(1)}, u32[]{:S(2)}, u32[]{:S(2)}) %collective-permute-start.11) | collective-permute-done | bytes 131104 | tf_op jit(solution)/shard_map/ppermute | solution.py:262
  8.9 0.6 %collective-permute-start.14 = (bf16[256,256]{1,0:T(8,128)(2,1)S(1)}, bf16[256,256]{1,0:T(8,128)(2,1)S(1)}, u32[]{:S(2)}, u32[]{:S(2)}) collective-permute-start(bf16[256,256]{1,0:T(8,128)(2,1)S(1)} %get-tuple-element.12), channel_id=1, source_target_pairs={{0,2},{2,0},{4,6},{6,4},{8,10},{10,8},{12,14},{14,12},{16,18},{18,... | collective-permute-start | bytes 393224 | tf_op jit(solution)/shard_map/ppermute | solution.py:269
  9.5 1.0 %collective-permute-done.2.refs_6_ = bf16[256,256]{1,0:T(8,128)(2,1)S(1)} collective-permute-done((bf16[256,256]{1,0:T(8,128)(2,1)S(1)}, bf16[256,256]{1,0:T(8,128)(2,1)S(1)}, u32[]{:S(2)}, u32[]{:S(2)}) %collective-permute-start.2) | collective-permute-done | bytes 131104 | tf_op jit(solution)/shard_map/ppermute | solution.py:261
  10.5 1.0 %collective-permute-start.3 = (bf16[256,256]{1,0:T(8,128)(2,1)S(1)}, bf16[256,256]{1,0:T(8,128)(2,1)S(1)}, u32[]{:S(2)}, u32[]{:S(2)}) collective-permute-start(bf16[256,256]{1,0:T(8,128)(2,1)S(1)} %collective-permute-done.2.refs_6_), channel_id=1, source_target_pairs={{0,8},{2,10},{4,0},{6,2},{8,16},{10,18},{12,4},{14,6},{16,24},{18,... | collective-permute-start | bytes 393224 | tf_op jit(solution)/shard_map/ppermute | solution.py:261
  11.5 0.4 collective-permute-done.5.refs_7_
  12.0 1.6 %collective-permute-start.12 = (bf16[256,256]{1,0:T(8,128)(2,1)S(1)}, bf16[256,256]{1,0:T(8,128)(2,1)S(1)}, u32[]{:S(2)}, u32[]{:S(2)}) collective-permute-start(bf16[256,256]{1,0:T(8,128)(2,1)S(1)} %collective-permute-done.11.refs_9_), channel_id=1, source_target_pairs={{0,4},{2,6},{4,12},{6,14},{8,0},{10,2},{12,20},{14,22},{16,8},{18,... | collective-permute-start | bytes 393224 | tf_op jit(solution)/shard_map/ppermute | solution.py:262
  13.6 0.2 collective-permute-done.8.refs_8_
  13.8 0.2 collective-permute-start.9
  14.0 0.0 collective-permute-done.14.refs_5_
  14.0 1.8 %collective-permute-start.6 = (bf16[256,256]{1,0:T(8,128)(2,1)S(1)}, bf16[256,256]{1,0:T(8,128)(2,1)S(1)}, u32[]{:S(2)}, u32[]{:S(2)}) collective-permute-start(bf16[256,256]{1,0:T(8,128)(2,1)S(1)} %collective-permute-done.5.refs_7_), channel_id=1, source_target_pairs={{0,4},{2,6},{4,12},{6,14},{8,0},{10,2},{12,20},{14,22},{16,8},{18,... | collective-permute-start | bytes 393224 | tf_op jit(solution)/shard_map/ppermute | solution.py:262
  15.8 1.1 %collective-permute-done.3.refs_10_ = bf16[256,256]{1,0:T(8,128)(2,1)S(1)} collective-permute-done((bf16[256,256]{1,0:T(8,128)(2,1)S(1)}, bf16[256,256]{1,0:T(8,128)(2,1)S(1)}, u32[]{:S(2)}, u32[]{:S(2)}) %collective-permute-start.3) | collective-permute-done | bytes 131104 | tf_op jit(solution)/shard_map/ppermute | solution.py:261
  16.9 0.1 collective-permute-start.4
  17.0 0.6 %collective-permute-done.12.refs_13_ = bf16[256,256]{1,0:T(8,128)(2,1)S(1)} collective-permute-done((bf16[256,256]{1,0:T(8,128)(2,1)S(1)}, bf16[256,256]{1,0:T(8,128)(2,1)S(1)}, u32[]{:S(2)}, u32[]{:S(2)}) %collective-permute-start.12) | collective-permute-done | bytes 131104 | tf_op jit(solution)/shard_map/ppermute | solution.py:262
  17.6 1.3 %collective-permute-start.13 = (bf16[256,256]{1,0:T(8,128)(2,1)S(1)}, bf16[256,256]{1,0:T(8,128)(2,1)S(1)}, u32[]{:S(2)}, u32[]{:S(2)}) collective-permute-start(bf16[256,256]{1,0:T(8,128)(2,1)S(1)} %collective-permute-done.12.refs_13_), channel_id=1, source_target_pairs={{0,4},{2,6},{4,12},{6,14},{8,0},{10,2},{12,20},{14,22},{16,8},{18,... | collective-permute-start | bytes 393224 | tf_op jit(solution)/shard_map/ppermute | solution.py:262
  18.9 1.0 %collective-permute-done.9.refs_12_ = bf16[256,256]{1,0:T(8,128)(2,1)S(1)} collective-permute-done((bf16[256,256]{1,0:T(8,128)(2,1)S(1)}, bf16[256,256]{1,0:T(8,128)(2,1)S(1)}, u32[]{:S(2)}, u32[]{:S(2)}) %collective-permute-start.9) | collective-permute-done | bytes 131104 | tf_op jit(solution)/shard_map/ppermute | solution.py:261
  19.9 0.0 collective-permute-start.10
  20.0 0.5 %collective-permute-done.6.refs_11_ = bf16[256,256]{1,0:T(8,128)(2,1)S(1)} collective-permute-done((bf16[256,256]{1,0:T(8,128)(2,1)S(1)}, bf16[256,256]{1,0:T(8,128)(2,1)S(1)}, u32[]{:S(2)}, u32[]{:S(2)}) %collective-permute-start.6) | collective-permute-done | bytes 131104 | tf_op jit(solution)/shard_map/ppermute | solution.py:262
  20.5 1.5 %collective-permute-start.7 = (bf16[256,256]{1,0:T(8,128)(2,1)S(1)}, bf16[256,256]{1,0:T(8,128)(2,1)S(1)}, u32[]{:S(2)}, u32[]{:S(2)}) collective-permute-start(bf16[256,256]{1,0:T(8,128)(2,1)S(1)} %collective-permute-done.6.refs_11_), channel_id=1, source_target_pairs={{0,4},{2,6},{4,12},{6,14},{8,0},{10,2},{12,20},{14,22},{16,8},{18,... | collective-permute-start | bytes 393224 | tf_op jit(solution)/shard_map/ppermute | solution.py:262
  22.0 1.0 %collective-permute-done.4.refs_4_ = bf16[256,256]{1,0:T(8,128)(2,1)S(1)} collective-permute-done((bf16[256,256]{1,0:T(8,128)(2,1)S(1)}, bf16[256,256]{1,0:T(8,128)(2,1)S(1)}, u32[]{:S(2)}, u32[]{:S(2)}) %collective-permute-start.4) | collective-permute-done | bytes 131104 | tf_op jit(solution)/shard_map/ppermute | solution.py:261
  22.9 0.0 collective-permute-start.15
  23.0 0.4 collective-permute-done.13.refs_7_
  23.4 1.6 %collective-permute-start.16 = (bf16[256,256]{1,0:T(8,128)(2,1)S(1)}, bf16[256,256]{1,0:T(8,128)(2,1)S(1)}, u32[]{:S(2)}, u32[]{:S(2)}) collective-permute-start(bf16[256,256]{1,0:T(8,128)(2,1)S(1)} %collective-permute-done.13.refs_7_), channel_id=1, source_target_pairs={{0,4},{2,6},{4,12},{6,14},{8,0},{10,2},{12,20},{14,22},{16,8},{18,... | collective-permute-start | bytes 393224 | tf_op jit(solution)/shard_map/ppermute | solution.py:267
  25.0 0.0 collective-permute-done.1.refs_3_.tiles
  25.0 1.7 %absorb.2.refs_8_ = f32[2,2,256,256]{3,2,1,0:T(8,128)S(1)} custom-call(s32[8,256]{1,0:T(8,128)S(1)} %get-tuple-element.9.refs_0_.info, s32[8,256]{1,0:T(8,128)S(1)} %collective-permute-done.refs_1_.info, bf16[2,2,12,128,128]{4,3,2,1,0:T(8,128)(2,1)S(1)} %get-tuple-element.10.refs_2_.tiles, ...), custom_call_target="tpu_custom_call" | custom-call | flops 1342177280 | tf_op jit(solution)/shard_map/absorb/pallas_call | solution.py:170
  26.6 0.0 collective-permute-done.10.refs_6_
  26.7 0.2 collective-permute-done.7.refs_5_
  26.9 0.8 %absorb.3.sums = f32[2,2,256,256]{3,2,1,0:T(8,128)S(1)} custom-call(s32[8,256]{1,0:T(8,128)S(1)} %get-tuple-element.9.refs_0_.info, s32[8,256]{1,0:T(8,128)S(1)} %collective-permute-done.refs_1_.info, bf16[2,2,12,128,128]{4,3,2,1,0:T(8,128)(2,1)S(1)} %get-tuple-element.10.refs_2_.tiles, ...), custom_call_target="tpu_custom_call" | custom-call | flops 536870912 | tf_op jit(solution)/shard_map/absorb/pallas_call | solution.py:170
  27.7 0.4 collective-permute-done.15.refs_0_
  28.1 0.4 collective-permute-done.16.refs_1_
  28.5 0.4 close.3
  28.9 0.0 copy-start.3
  28.9 0.1 collective-permute-start.17
  28.9 1.6 %collective-permute-start.18 = (bf16[2,256,256]{2,1,0:T(8,128)(2,1)S(1)}, bf16[2,256,256]{2,1,0:T(8,128)(2,1)S(1)}, u32[]{:S(2)}, u32[]{:S(2)}) collective-permute-start(bf16[2,256,256]{2,1,0:T(8,128)(2,1)S(1)} %close.3), channel_id=1, source_target_pairs={{0,3},{1,2},{2,1},{3,0},{4,7},{5,6},{6,5},{7,4},{8,11},{9,10},{10,... | collective-permute-start | bytes 786440 | tf_op jit(solution)/shard_map/ppermute | solution.py:283
  30.5 0.0 copy-start.2
  30.5 0.4 close.2.refs_0_
  30.9 0.0 copy-start.1
  30.9 0.6 %collective-permute-start.19 = (bf16[2,256,256]{2,1,0:T(8,128)(2,1)S(1)}, bf16[2,256,256]{2,1,0:T(8,128)(2,1)S(1)}, u32[]{:S(2)}, u32[]{:S(2)}) collective-permute-start(bf16[2,256,256]{2,1,0:T(8,128)(2,1)S(1)} %close.2.refs_0_), channel_id=1, source_target_pairs={{0,1},{1,0},{2,3},{3,2},{4,5},{5,4},{6,7},{7,6},{8,9},{9,8},{10,11... | collective-permute-start | bytes 786440 | tf_op jit(solution)/shard_map/ppermute | solution.py:285
  31.6 0.0 copy-done
  31.6 0.0 copy-done.3
  31.6 0.7 %fusion.base = f32[256,1024]{1,0:T(8,128)S(1)} fusion(bf16[256,1024]{1,0:T(8,128)(2,1)S(1)} %copy-done.3, bf16[1024,1024]{1,0:T(8,128)(2,1)S(1)} %copy-done), kind=kOutput, calls=%fused_computation | convolution fusion | flops 536870912 | bytes 3670016 | tf_op jit(solution)/shard_map/dot_general | solution.py:287
  32.3 0.0 collective-permute-done.17.refs_1_
  32.3 0.0 copy-done.2
  32.3 0.5 %copy-done.1 = bf16[1024,1024]{1,0:T(8,128)(2,1)S(1)} copy-done((bf16[1024,1024]{1,0:T(8,128)(2,1)S(1)}, bf16[1024,1024]{1,0:T(8,128)(2,1)}, u32[]{:S(2)}) %copy-start.1) | copy-done | bytes 2097176
  32.8 0.7 %project.3.base = f32[256,1024]{1,0:T(8,128)S(1)} custom-call(f32[256,1024]{1,0:T(8,128)S(1)} %fusion.base, bf16[1024,1024]{1,0:T(8,128)(2,1)S(1)} %copy-done.1, bf16[1024,1024]{1,0:T(8,128)(2,1)S(1)} %copy-done.2, bf16[2,256,256]{2,1,0:T(8,128)(2,1)S(1)} %close.2.refs_0_, bf16[2,256,256]{2,1,0:T(8,128)(2,1)S(1)} %collective-permute-done.17.refs_1_), custom_call_target="tpu_custom_call" | custom-call | flops 536870912 | tf_op jit(solution)/shard_map/project/pallas_call | solution.py:231
  33.6 3.6 %collective-permute-done.18.refs_0_ = bf16[2,256,256]{2,1,0:T(8,128)(2,1)S(1)} collective-permute-done((bf16[2,256,256]{2,1,0:T(8,128)(2,1)S(1)}, bf16[2,256,256]{2,1,0:T(8,128)(2,1)S(1)}, u32[]{:S(2)}, u32[]{:S(2)}) %collective-permute-start.18) | collective-permute-done | bytes 262176 | tf_op jit(solution)/shard_map/ppermute | solution.py:283
  37.2 0.4 project.4.base
  37.6 5.6 %collective-permute-done.19.refs_0_ = bf16[2,256,256]{2,1,0:T(8,128)(2,1)S(1)} collective-permute-done((bf16[2,256,256]{2,1,0:T(8,128)(2,1)S(1)}, bf16[2,256,256]{2,1,0:T(8,128)(2,1)S(1)}, u32[]{:S(2)}, u32[]{:S(2)}) %collective-permute-start.19) | collective-permute-done | bytes 262176 | tf_op jit(solution)/shard_map/ppermute | solution.py:285
  43.2 1.2 %project.5 = bf16[256,1024]{1,0:T(8,128)(2,1)} custom-call(f32[256,1024]{1,0:T(8,128)S(1)} %project.4.base, bf16[1024,1024]{1,0:T(8,128)(2,1)S(1)} %copy-done.1, bf16[1024,1024]{1,0:T(8,128)(2,1)S(1)} %copy-done.2, bf16[2,256,256]{2,1,0:T(8,128)(2,1)S(1)} %collective-permute-done.19.refs_0_), custom_call_target="tpu_custom_call" | custom-call | flops 268435456 | tf_op jit(solution)/shard_map/project/pallas_call | solution.py:231
Async XLA Ops:
  0.0 31.6 %copy-start = (bf16[1024,1024]{1,0:T(8,128)(2,1)S(1)}, bf16[1024,1024]{1,0:T(8,128)(2,1)}, u32[]{:S(2)}) copy-start(bf16[1024,1024]{1,0:T(8,128)(2,1)} %param.13) | copy-start | bytes 6291460
  1.9 23.1 %collective-permute-start.1 = (bf16[2,2,12,128,128]{4,3,2,1,0:T(8,128)(2,1)S(1)}, bf16[2,2,12,128,128]{4,3,2,1,0:T(8,128)(2,1)S(1)}, u32[]{:S(2)}, u32[]{:S(2)}) collective-permute-start(bf16[2,2,12,128,128]{4,3,2,1,0:T(8,128)(2,1)S(1)} %get-tuple-element.10.refs_2_.tiles), channel_id=1, source_target_pairs={{0,2},{2,0},{4,6},{6,4},{8,10},{10,8},{12,14},{14,12},{16,18},{18,... | collective-permute-start | bytes 4718600 | tf_op jit(solution)/shard_map/ppermute | solution.py:272
  2.4 6.5 %collective-permute-start.11 = (bf16[256,256]{1,0:T(8,128)(2,1)S(1)}, bf16[256,256]{1,0:T(8,128)(2,1)S(1)}, u32[]{:S(2)}, u32[]{:S(2)}) collective-permute-start(bf16[256,256]{1,0:T(8,128)(2,1)S(1)} %get-tuple-element.12), channel_id=1, source_target_pairs={{0,6},{2,4},{4,14},{6,12},{8,2},{10,0},{12,22},{14,20},{16,10},{18... | collective-permute-start | bytes 393224 | tf_op jit(solution)/shard_map/ppermute | solution.py:262
  5.0 5.5 %collective-permute-start.2 = (bf16[256,256]{1,0:T(8,128)(2,1)S(1)}, bf16[256,256]{1,0:T(8,128)(2,1)S(1)}, u32[]{:S(2)}, u32[]{:S(2)}) collective-permute-start(bf16[256,256]{1,0:T(8,128)(2,1)S(1)} %get-tuple-element.11.refs_4_), channel_id=1, source_target_pairs={{0,8},{2,10},{4,0},{6,2},{8,16},{10,18},{12,4},{14,6},{16,24},{18,... | collective-permute-start | bytes 393224 | tf_op jit(solution)/shard_map/ppermute | solution.py:261
  5.1 6.8 %collective-permute-start.5 = (bf16[256,256]{1,0:T(8,128)(2,1)S(1)}, bf16[256,256]{1,0:T(8,128)(2,1)S(1)}, u32[]{:S(2)}, u32[]{:S(2)}) collective-permute-start(bf16[256,256]{1,0:T(8,128)(2,1)S(1)} %get-tuple-element.11.refs_4_), channel_id=1, source_target_pairs={{0,4},{2,6},{4,12},{6,14},{8,0},{10,2},{12,20},{14,22},{16,8},{18,... | collective-permute-start | bytes 393224 | tf_op jit(solution)/shard_map/ppermute | solution.py:262
  7.1 1.2 %collective-permute-start = (s32[8,256]{1,0:T(8,128)S(1)}, s32[8,256]{1,0:T(8,128)S(1)}, u32[]{:S(2)}, u32[]{:S(2)}) collective-permute-start(s32[8,256]{1,0:T(8,128)S(1)} %get-tuple-element.9.refs_0_.info), channel_id=1, source_target_pairs={{0,2},{2,0},{4,6},{6,4},{8,10},{10,8},{12,14},{14,12},{16,18},{18,... | collective-permute-start | bytes 24584 | tf_op jit(solution)/shard_map/ppermute | solution.py:271
  8.2 5.5 %collective-permute-start.8 = (bf16[256,256]{1,0:T(8,128)(2,1)S(1)}, bf16[256,256]{1,0:T(8,128)(2,1)S(1)}, u32[]{:S(2)}, u32[]{:S(2)}) collective-permute-start(bf16[256,256]{1,0:T(8,128)(2,1)S(1)} %get-tuple-element.12), channel_id=1, source_target_pairs={{0,10},{2,8},{4,2},{6,0},{8,18},{10,16},{12,6},{14,4},{16,26},{18,... | collective-permute-start | bytes 393224 | tf_op jit(solution)/shard_map/ppermute | solution.py:261
  8.9 5.1 %collective-permute-start.14 = (bf16[256,256]{1,0:T(8,128)(2,1)S(1)}, bf16[256,256]{1,0:T(8,128)(2,1)S(1)}, u32[]{:S(2)}, u32[]{:S(2)}) collective-permute-start(bf16[256,256]{1,0:T(8,128)(2,1)S(1)} %get-tuple-element.12), channel_id=1, source_target_pairs={{0,2},{2,0},{4,6},{6,4},{8,10},{10,8},{12,14},{14,12},{16,18},{18,... | collective-permute-start | bytes 393224 | tf_op jit(solution)/shard_map/ppermute | solution.py:269
  10.5 6.4 %collective-permute-start.3 = (bf16[256,256]{1,0:T(8,128)(2,1)S(1)}, bf16[256,256]{1,0:T(8,128)(2,1)S(1)}, u32[]{:S(2)}, u32[]{:S(2)}) collective-permute-start(bf16[256,256]{1,0:T(8,128)(2,1)S(1)} %collective-permute-done.2.refs_6_), channel_id=1, source_target_pairs={{0,8},{2,10},{4,0},{6,2},{8,16},{10,18},{12,4},{14,6},{16,24},{18,... | collective-permute-start | bytes 393224 | tf_op jit(solution)/shard_map/ppermute | solution.py:261
  12.0 5.7 %collective-permute-start.12 = (bf16[256,256]{1,0:T(8,128)(2,1)S(1)}, bf16[256,256]{1,0:T(8,128)(2,1)S(1)}, u32[]{:S(2)}, u32[]{:S(2)}) collective-permute-start(bf16[256,256]{1,0:T(8,128)(2,1)S(1)} %collective-permute-done.11.refs_9_), channel_id=1, source_target_pairs={{0,4},{2,6},{4,12},{6,14},{8,0},{10,2},{12,20},{14,22},{16,8},{18,... | collective-permute-start | bytes 393224 | tf_op jit(solution)/shard_map/ppermute | solution.py:262
  13.8 6.2 %collective-permute-start.9 = (bf16[256,256]{1,0:T(8,128)(2,1)S(1)}, bf16[256,256]{1,0:T(8,128)(2,1)S(1)}, u32[]{:S(2)}, u32[]{:S(2)}) collective-permute-start(bf16[256,256]{1,0:T(8,128)(2,1)S(1)} %collective-permute-done.8.refs_8_), channel_id=1, source_target_pairs={{0,8},{2,10},{4,0},{6,2},{8,16},{10,18},{12,4},{14,6},{16,24},{18,... | collective-permute-start | bytes 393224 | tf_op jit(solution)/shard_map/ppermute | solution.py:261
  14.0 6.5 %collective-permute-start.6 = (bf16[256,256]{1,0:T(8,128)(2,1)S(1)}, bf16[256,256]{1,0:T(8,128)(2,1)S(1)}, u32[]{:S(2)}, u32[]{:S(2)}) collective-permute-start(bf16[256,256]{1,0:T(8,128)(2,1)S(1)} %collective-permute-done.5.refs_7_), channel_id=1, source_target_pairs={{0,4},{2,6},{4,12},{6,14},{8,0},{10,2},{12,20},{14,22},{16,8},{18,... | collective-permute-start | bytes 393224 | tf_op jit(solution)/shard_map/ppermute | solution.py:262
  16.9 6.0 %collective-permute-start.4 = (bf16[256,256]{1,0:T(8,128)(2,1)S(1)}, bf16[256,256]{1,0:T(8,128)(2,1)S(1)}, u32[]{:S(2)}, u32[]{:S(2)}) collective-permute-start(bf16[256,256]{1,0:T(8,128)(2,1)S(1)} %collective-permute-done.3.refs_10_), channel_id=1, source_target_pairs={{0,8},{2,10},{4,0},{6,2},{8,16},{10,18},{12,4},{14,6},{16,24},{18,... | collective-permute-start | bytes 393224 | tf_op jit(solution)/shard_map/ppermute | solution.py:261
  17.6 5.7 %collective-permute-start.13 = (bf16[256,256]{1,0:T(8,128)(2,1)S(1)}, bf16[256,256]{1,0:T(8,128)(2,1)S(1)}, u32[]{:S(2)}, u32[]{:S(2)}) collective-permute-start(bf16[256,256]{1,0:T(8,128)(2,1)S(1)} %collective-permute-done.12.refs_13_), channel_id=1, source_target_pairs={{0,4},{2,6},{4,12},{6,14},{8,0},{10,2},{12,20},{14,22},{16,8},{18,... | collective-permute-start | bytes 393224 | tf_op jit(solution)/shard_map/ppermute | solution.py:262
  19.9 6.7 %collective-permute-start.10 = (bf16[256,256]{1,0:T(8,128)(2,1)S(1)}, bf16[256,256]{1,0:T(8,128)(2,1)S(1)}, u32[]{:S(2)}, u32[]{:S(2)}) collective-permute-start(bf16[256,256]{1,0:T(8,128)(2,1)S(1)} %collective-permute-done.9.refs_12_), channel_id=1, source_target_pairs={{0,8},{2,10},{4,0},{6,2},{8,16},{10,18},{12,4},{14,6},{16,24},{18,... | collective-permute-start | bytes 393224 | tf_op jit(solution)/shard_map/ppermute | solution.py:261
  20.5 6.4 %collective-permute-start.7 = (bf16[256,256]{1,0:T(8,128)(2,1)S(1)}, bf16[256,256]{1,0:T(8,128)(2,1)S(1)}, u32[]{:S(2)}, u32[]{:S(2)}) collective-permute-start(bf16[256,256]{1,0:T(8,128)(2,1)S(1)} %collective-permute-done.6.refs_11_), channel_id=1, source_target_pairs={{0,4},{2,6},{4,12},{6,14},{8,0},{10,2},{12,20},{14,22},{16,8},{18,... | collective-permute-start | bytes 393224 | tf_op jit(solution)/shard_map/ppermute | solution.py:262
  22.9 5.1 %collective-permute-start.15 = (bf16[256,256]{1,0:T(8,128)(2,1)S(1)}, bf16[256,256]{1,0:T(8,128)(2,1)S(1)}, u32[]{:S(2)}, u32[]{:S(2)}) collective-permute-start(bf16[256,256]{1,0:T(8,128)(2,1)S(1)} %collective-permute-done.4.refs_4_), channel_id=1, source_target_pairs={{0,8},{2,10},{4,0},{6,2},{8,16},{10,18},{12,4},{14,6},{16,24},{18,... | collective-permute-start | bytes 393224 | tf_op jit(solution)/shard_map/ppermute | solution.py:266
  23.4 5.1 %collective-permute-start.16 = (bf16[256,256]{1,0:T(8,128)(2,1)S(1)}, bf16[256,256]{1,0:T(8,128)(2,1)S(1)}, u32[]{:S(2)}, u32[]{:S(2)}) collective-permute-start(bf16[256,256]{1,0:T(8,128)(2,1)S(1)} %collective-permute-done.13.refs_7_), channel_id=1, source_target_pairs={{0,4},{2,6},{4,12},{6,14},{8,0},{10,2},{12,20},{14,22},{16,8},{18,... | collective-permute-start | bytes 393224 | tf_op jit(solution)/shard_map/ppermute | solution.py:267
  28.9 2.7 %copy-start.3 = (bf16[256,1024]{1,0:T(8,128)(2,1)S(1)}, bf16[256,1024]{1,0:T(8,128)(2,1)}, u32[]{:S(2)}) copy-start(bf16[256,1024]{1,0:T(8,128)(2,1)} %features.1) | copy-start | bytes 1572868
  28.9 3.4 %collective-permute-start.17 = (bf16[2,256,256]{2,1,0:T(8,128)(2,1)S(1)}, bf16[2,256,256]{2,1,0:T(8,128)(2,1)S(1)}, u32[]{:S(2)}, u32[]{:S(2)}) collective-permute-start(bf16[2,256,256]{2,1,0:T(8,128)(2,1)S(1)} %close.3), channel_id=1, source_target_pairs={{0,2},{2,0},{4,6},{6,4},{8,10},{10,8},{12,14},{14,12},{16,18},{18,... | collective-permute-start | bytes 786440 | tf_op jit(solution)/shard_map/ppermute | solution.py:284
  28.9 8.2 %collective-permute-start.18 = (bf16[2,256,256]{2,1,0:T(8,128)(2,1)S(1)}, bf16[2,256,256]{2,1,0:T(8,128)(2,1)S(1)}, u32[]{:S(2)}, u32[]{:S(2)}) collective-permute-start(bf16[2,256,256]{2,1,0:T(8,128)(2,1)S(1)} %close.3), channel_id=1, source_target_pairs={{0,3},{1,2},{2,1},{3,0},{4,7},{5,6},{6,5},{7,4},{8,11},{9,10},{10,... | collective-permute-start | bytes 786440 | tf_op jit(solution)/shard_map/ppermute | solution.py:283
  30.5 1.8 %copy-start.2 = (bf16[1024,1024]{1,0:T(8,128)(2,1)S(1)}, bf16[1024,1024]{1,0:T(8,128)(2,1)}, u32[]{:S(2)}) copy-start(bf16[1024,1024]{1,0:T(8,128)(2,1)} %w_out.5) | copy-start | bytes 6291460
  30.9 1.9 %copy-start.1 = (bf16[1024,1024]{1,0:T(8,128)(2,1)S(1)}, bf16[1024,1024]{1,0:T(8,128)(2,1)}, u32[]{:S(2)}) copy-start(bf16[1024,1024]{1,0:T(8,128)(2,1)} %w_in.5) | copy-start | bytes 6291460
  30.9 12.3 %collective-permute-start.19 = (bf16[2,256,256]{2,1,0:T(8,128)(2,1)S(1)}, bf16[2,256,256]{2,1,0:T(8,128)(2,1)S(1)}, u32[]{:S(2)}, u32[]{:S(2)}) collective-permute-start(bf16[2,256,256]{2,1,0:T(8,128)(2,1)S(1)} %close.2.refs_0_), channel_id=1, source_target_pairs={{0,1},{1,0},{2,3},{3,2},{4,5},{5,4},{6,7},{7,6},{8,9},{9,8},{10,11... | collective-permute-start | bytes 786440 | tf_op jit(solution)/shard_map/ppermute | solution.py:285

commit v4 on v3

v4 whole, which is shorter than its diff:
```python
import functools

import jax
import jax.numpy as jnp
from jax import lax
from jax.experimental import pallas as pl
from jax.experimental.pallas import tpu as pltpu
from jax.sharding import PartitionSpec as P

F32 = jnp.float32
BF16 = jnp.bfloat16
SMEM = pl.BlockSpec(memory_space=pltpu.SMEM)
VMEM = pl.BlockSpec(memory_space=pltpu.VMEM)
HBM = pl.BlockSpec(memory_space=pltpu.HBM)


def params(mib):
    return pltpu.CompilerParams(vmem_limit_bytes=mib * 2**20)


def chip_ring(chips):
    half = chips // 2
    return [2 * o for o in range(half)] + [2 * o + 1 for o in reversed(range(half))]


def ring_route(devices, distance):
    ring = chip_ring(devices // 2)
    size = len(ring)
    route = []
    for place, chip in enumerate(ring):
        target = ring[(place + distance) % size]
        route += [(2 * chip + core, 2 * target + core) for core in range(2)]
    return sorted(route)


def swapped(route):
    return [(source, target ^ 1) for source, target in route]


def core_route(devices):
    return [(d, d ^ 1) for d in range(devices)]


def split(value, size):
    if size & (size - 1) == 0:
        return value >> (size.bit_length() - 1), value & (size - 1)
    return value // size, lax.rem(value, size)


def place_of(chip, chips):
    rung, side = split(chip, 2)
    return jnp.where(side == 0, rung, chips - 1 - rung)


def lane(offset, other, block, local):
    return (offset * 2 + other) * local + block


def pack_body(chips, local, features, bands, tiles, columns_in, counts_in, degrees_in, *refs):
    mine, theirs, bundle, columns, counts, degrees, arrived = refs
    rep = lax.axis_index("rep")
    position = lax.axis_index("dom")
    core = lax.rem(position, 2)
    here = place_of(position // 2, chips)
    width = mine.shape[1]
    tile = tiles.shape[1]
    slots = columns.shape[2]

    def quarter(core_of, start, size):
        return pl.ds(pl.multiple_of((2 * rep + core_of) * width + start, tile), size)

    moves = [
        (columns_in, columns),
        (counts_in, counts),
        (degrees_in, degrees),
        (features.at[:, quarter(core, 0, width)], mine),
        (features.at[:, quarter(1 - core, 0, width)], theirs),
        (tiles, bundle.at[0 : tiles.shape[0]]),
    ]
    index = tiles.shape[0]
    for start in range(0, width, tile):
        panel = bands.at[:, :, quarter(1 - core, start, tile)]
        moves.append((panel, bundle.at[index : index + bands.shape[0]]))
        index += bands.shape[0]
    copies = [
        pltpu.make_async_copy(source, target, arrived.at[number])
        for number, (source, target) in enumerate(moves)
    ]
    for copy in copies:
        copy.start()
    for copy in copies[:3]:
        copy.wait()
    column = jnp.concatenate([columns[relation] for relation in range(2)], axis=0)
    live = jnp.concatenate(
        [counts[relation : relation + 1, row : row + 1] for relation in range(2) for row in range(local)],
        axis=0,
    )
    source, block = split(column, local)
    chip, other = split(source, 2)
    _, offset = split(place_of(chip, chips) - here + chips, chips)
    other = jnp.where(core == 0, other, 1 - other)
    target = lane(offset, other, block, local)
    target = jnp.where(lax.broadcasted_iota(jnp.int32, column.shape, 1) < live, target, -1)
    place = lax.broadcasted_iota(jnp.int32, (2 * local, tile), 1)
    table = jnp.full(place.shape, -1, jnp.int32)
    for slot in range(slots):
        table = jnp.where(place == target[:, slot : slot + 1], slot, table)
    table = [table]
    for relation in range(2):
        for row in range(local):
            table.append(degrees[relation : relation + 1, row * tile : (row + 1) * tile])
    table = jnp.concatenate(table, axis=0).astype(F32)
    bundle[index, 0 : table.shape[0], :] = table.astype(BF16)
    for copy in copies[3:]:
        copy.wait()


def pack(features, tiles, columns, counts, degrees, width, devices):
    rows = features.shape[0]
    _, local, slots, tile, _ = tiles.shape
    assert devices * local <= tile
    panels = (rows // tile) * (width // tile)
    piece = jax.ShapeDtypeStruct((rows, width), BF16)
    bundle = jax.ShapeDtypeStruct((2 * local * slots + panels + 1, tile, tile), BF16)
    operands = [
        pltpu.with_memory_space_constraint(x, pltpu.HBM)
        for x in (
            features,
            features.reshape(rows // tile, tile, features.shape[1]),
            tiles.reshape(2 * local * slots, tile, tile),
            columns,
            counts,
            degrees,
        )
    ]
    return pl.pallas_call(
        functools.partial(pack_body, devices // 2, local),
        out_shape=[piece, piece, bundle],
        in_specs=[HBM] * 6,
        out_specs=[VMEM] * 3,
        scratch_shapes=[
            pltpu.VMEM(columns.shape, jnp.int32),
            pltpu.VMEM(counts.shape, jnp.int32),
            pltpu.VMEM(degrees.shape, jnp.int32),
            pltpu.SemaphoreType.DMA((6 + width // tile,)),
        ],
        compiler_params=params(24),
        name="pack",
    )(*operands)


def table_of(bundle):
    return bundle[bundle.shape[0] - 1, 0:8, :].astype(F32)


def packed_panel(bundle, rows, width):
    tile = bundle.shape[-1]
    across, count = width // tile, rows // tile
    first = bundle.shape[0] - 1 - count * across
    bands = []
    for band in range(count):
        parts = [bundle[first + part * count + band] for part in range(across)]
        bands.append(jnp.concatenate(parts, axis=1))
    return jnp.concatenate(bands, axis=0)


def contribution(table, bundle, local, slots, relation, row, side, panels, origins, chips):
    index = relation * local + row
    total = None
    for panel, (offset, other) in zip(panels, origins):
        weights = []
        for block in range(local):
            slot = table[index, lane(offset % chips, other ^ side, block, local)]
            one = bundle[index * slots + jnp.maximum(slot, 0)]
            weights.append(jnp.where(slot >= 0, one, jnp.zeros_like(one)))
        part = jnp.dot(
            jnp.concatenate(weights, axis=1), panel[...], preferred_element_type=F32
        )
        total = part if total is None else total + part
    return total


def absorb_body(origins, local, slots, chips, seeded, *refs):
    bundles = refs[:2]
    pieces, sums = list(refs[2:-1]), refs[-1]
    seed = pieces.pop() if seeded else None
    rows, width = sums.shape[2:]
    if not seeded:
        pieces.append(packed_panel(bundles[1], rows, width))
    tile = bundles[0].shape[-1]
    for side in range(2):
        table = table_of(bundles[side]).astype(jnp.int32)
        for relation in range(2):
            for row in range(local):
                span = slice(row * tile, (row + 1) * tile)
                part = contribution(
                    table, bundles[side], local, slots, relation, row, side, pieces, origins, chips
                )
                if seeded:
                    part = part + seed[side, relation, span, :]
                sums[side, relation, span, :] = part


def absorb(bundles, shape, pieces, sums, chips):
    local, slots = shape
    rows, width = pieces[0][0].shape
    origins = tuple((offset, other) for _, offset, other in pieces)
    seeds = [] if sums is None else [sums]
    if sums is None:
        origins += ((0, 1),)
    return pl.pallas_call(
        functools.partial(absorb_body, origins, local, slots, chips, sums is not None),
        out_shape=jax.ShapeDtypeStruct((2, 2, rows, width), F32),
        in_specs=[VMEM] * (2 + len(pieces) + len(seeds)),
        out_specs=VMEM,
        compiler_params=params(32),
        cost_estimate=pl.CostEstimate(
            flops=len(pieces) * 8 * rows * rows * width, bytes_accessed=0, transcendentals=0
        ),
        name="absorb",
    )(*bundles, *[piece for piece, _, _ in pieces], *seeds)


def close_body(origins, local, slots, chips, side, bundle, sums, *refs):
    pieces, outs = refs[: len(origins)], refs[len(origins) :]
    band_rows = outs[0].shape[1]
    tile = bundle.shape[-1]
    values = table_of(bundle)
    table = values.astype(jnp.int32)
    for relation in range(2):
        for row in range(local):
            span = slice(row * tile, (row + 1) * tile)
            total = sums[side, relation, span, :]
            total = total + contribution(
                table, bundle, local, slots, relation, row, side, pieces, origins, chips
            )
            index = 2 * local + relation * local + row
            degree = jnp.broadcast_to(values[index : index + 1, :], (tile, tile)).T
            for start in range(0, total.shape[1], tile):
                part = total[:, start : start + tile] / degree
                first = row * tile % band_rows
                out = outs[row * tile // band_rows]
                out[relation, first : first + tile, start : start + tile] = part.astype(BF16)


def close(bundle, shape, pieces, sums, side, chips, bands):
    local, slots = shape
    _, _, rows, width = sums.shape
    origins = tuple((offset, other) for _, offset, other in pieces)
    return pl.pallas_call(
        functools.partial(close_body, origins, local, slots, chips, side),
        out_shape=[jax.ShapeDtypeStruct((2, rows // bands, width), BF16)] * bands,
        in_specs=[VMEM] * (2 + len(pieces)),
        out_specs=[VMEM] * bands,
        compiler_params=params(32),
        name="close",
    )(bundle, sums, *[piece for piece, _, _ in pieces])


def project_body(quarters, bands, base, w_in, w_out, *refs):
    parts, out = list(refs[:-1]), refs[-1]
    rep = lax.axis_index("rep")
    core = lax.rem(lax.axis_index("dom"), 2)
    total = base[...]
    for (far, other), count in zip(quarters, bands):
        part, parts = parts[:count], parts[count:]
        width = part[0].shape[2]
        quarter = 2 * (1 - rep if far else rep) + (1 - core if other else core)
        span = pl.ds(pl.multiple_of(quarter * width, width), width)
        for relation, weights in enumerate((w_in, w_out)):
            rows = jnp.concatenate([band[relation] for band in part], axis=0)
            total = total + jnp.dot(rows, weights[span, :], preferred_element_type=F32)
    out[...] = total


def project(base, parts, quarters, w_in, w_out):
    bands = tuple(len(part) for part in parts)
    flat = [band for part in parts for band in part]
    return pl.pallas_call(
        functools.partial(project_body, quarters, bands),
        out_shape=jax.ShapeDtypeStruct(base.shape, F32),
        in_specs=[VMEM] * (3 + len(flat)),
        out_specs=VMEM,
        compiler_params=params(24),
        cost_estimate=pl.CostEstimate(
            flops=len(parts) * 2**28, bytes_accessed=0, transcendentals=0
        ),
        name="project",
    )(base, w_in, w_out, *flat)


def finish_body(band, quarter, base, w_in, w_out, part, *refs):
    out, staged, sent = refs[-3:]
    far, other = quarter
    rep = lax.axis_index("rep")
    core = lax.rem(lax.axis_index("dom"), 2)
    rows, width = part.shape[1:]
    quarter = 2 * (1 - rep if far else rep) + (1 - core if other else core)
    span = pl.ds(pl.multiple_of(quarter * width, width), width)
    first = band * rows
    total = base[first : first + rows, :]
    total = total + jnp.dot(part[0], w_in[span, :], preferred_element_type=F32)
    total = total + jnp.dot(part[1], w_out[span, :], preferred_element_type=F32)
    staged[...] = jnp.maximum(total, 0.0).astype(BF16)
    copy = pltpu.make_async_copy(staged, out.at[first : first + rows, :], sent)
    copy.start()
    copy.wait()


def finish(base, part, quarter, w_in, w_out, band, out):
    rows = part.shape[1]
    earlier = [] if out is None else [out]
    return pl.pallas_call(
        functools.partial(finish_body, band, quarter),
        out_shape=jax.ShapeDtypeStruct(base.shape, BF16),
        in_specs=[VMEM] * 4 + [HBM] * len(earlier),
        out_specs=HBM,
        scratch_shapes=[pltpu.VMEM((rows, base.shape[1]), BF16), pltpu.SemaphoreType.DMA],
        input_output_aliases={4: 0} if earlier else {},
        compiler_params=params(24),
        cost_estimate=pl.CostEstimate(flops=2**27, bytes_accessed=0, transcendentals=0),
        name="finish",
    )(base, w_in, w_out, part, *earlier)


def on_device(features, tiles, columns, counts, degrees, w_self, w_in, w_out):
    devices = lax.axis_size("dom")
    reps = lax.axis_size("rep")
    width = features.shape[1] // (2 * reps)
    chips = devices // 2
    cores = core_route(devices)
    ahead, behind = ring_route(devices, 1), ring_route(devices, -1)

    mine, theirs, bundle = pack(features, tiles, columns, counts, degrees, width, devices)
    bundles = (bundle, lax.ppermute(bundle, "dom", cores))
    shape = tiles.shape[1:3]

    forward = [mine, theirs]
    backward = [mine, theirs]
    steps = []
    for step in range(1, (chips - 1) // 2 + 1):
        found = []
        forward[1] = lax.ppermute(forward[1], "dom", swapped(ahead) if step == 1 else ahead)
        found.append((forward[1], -step, 1))
        backward[1] = lax.ppermute(backward[1], "dom", swapped(behind) if step == 1 else behind)
        found.append((backward[1], step, 1))
        forward[0] = lax.ppermute(forward[0], "dom", ahead)
        found.append((forward[0], -step, 0))
        backward[0] = lax.ppermute(backward[0], "dom", behind)
        found.append((backward[0], step, 0))
        steps.append(found)
    last = [
        (lax.ppermute(forward[1], "dom", ahead), chips // 2, 1),
        (lax.ppermute(backward[0], "dom", behind), chips // 2, 0),
    ]
    early = [(mine, 0, 0)] + [piece for found in steps[:-1] for piece in found]
    sums = absorb(bundles, shape, early, None, chips)
    sums = absorb(bundles, shape, steps[-1], sums, chips)
    (other,) = close(bundles[1], shape, last, sums, 1, chips, 1)
    owns = close(bundles[0], shape, last, sums, 0, chips, shape[0])

    across = [
        (d * reps + r, (d ^ 1) * reps + (r + 1) % reps) for d in range(devices) for r in range(reps)
    ]
    diagonal = lax.ppermute(other, ("dom", "rep"), across)
    core_side = lax.ppermute(other, "dom", cores)
    facing = [(r, (r + 1) % reps) for r in range(reps)]
    twins = [lax.ppermute(half, "rep", facing) for half in owns]

    hidden = jnp.dot(features, w_self, preferred_element_type=F32)
    hidden = project(hidden, [owns, [core_side]], ((0, 0), (0, 1)), w_in, w_out)
    hidden = project(hidden, [[diagonal]], ((1, 1),), w_in, w_out)
    out = None
    for band, twin in enumerate(twins):
        out = finish(hidden, twin, (1, 0), w_in, w_out, band, out)
    return out


def solution(mesh):
    placed = (
        P("dom", None),
        P(None, "dom", None, None, None),
        P(None, "dom", None),
        P(None, "dom"),
        P(None, "dom"),
        P(),
        P(),
        P(),
    )
    return jax.shard_map(
        on_device, mesh=mesh, in_specs=placed, out_specs=P("dom", None), check_vma=False
    )
```

time: 44.6 us -> 44.6 us (level)
  waiting for transfers between devices: 18.2 us -> 16.5 us
  starting transfers between devices: 17.4 us -> 18.9 us
  Pallas kernels: 7.51 us -> 8.27 us
  local copies, waits for them, and re-layouts: 0.56 us -> 0.02 us
    ppermute x18 -> x17, starting transfers between devices: 15.7 us -> 17.2 us  [the longest x3 6.29 us: on_device(): backward[0] = lax.ppermute(backward[0], 'dom', behind)]
    ppermute x1, waiting for transfers between devices: 3.6 us -> 2.66 us  [on_device(): diagonal = lax.ppermute(other, ('dom', 'rep'), across)]
    ppermute x18 -> x17, waiting for transfers between devices: 14.6 us -> 13.8 us  [the longest x3 4.92 us: on_device(): forward[0] = lax.ppermute(forward[0], 'dom', ahead)]
    pallas_call x8 -> x9, Pallas kernels: 7.51 us -> 8.27 us  [the longest x2 2.46 us: absorb(): pl.pallas_call(functools.partial(absorb_body, origins, local, slots, chip...]
    unnamed x8, local copies, waits for them, and re-layouts: 0.56 us -> 0.02 us
  transfers between devices with their start and end apart: 20 -> 19, of which waited for: 16 -> 11; matrix products, arithmetic and copies ran while one was open for 2% -> 2% of each run, Pallas kernels for 9% -> 11%
where the time goes in v4:
time: 44.6 us; the launch traced here: 44.5 us
  starting transfers between devices  18.9 us (42%)
  waiting for transfers between devices  16.5 us (37%)
  Pallas kernels  8.27 us (19%)
  matrix products  0.7 us (2%)
    ppermute x3, starting transfers between devices, on_device(): backward[0] = lax.ppermute(backward[0], 'dom', behind)  6.29 us
    ppermute x3, waiting for transfers between devices, on_device(): forward[0] = lax.ppermute(forward[0], 'dom', ahead)  4.92 us
    ppermute x2, waiting for transfers between devices, on_device(): twins = [lax.ppermute(half, 'rep', facing) for half in owns]  4.56 us
    ppermute x3, starting transfers between devices, on_device(): lax.ppermute(backward[1], 'dom', swapped(behind) if step == 1 else behind)  3.91 us
    ppermute x1, waiting for transfers between devices, on_device(): diagonal = lax.ppermute(other, ('dom', 'rep'), across)  2.66 us
    pallas_call x2, Pallas kernels, absorb(): pl.pallas_call(functools.partial(absorb_body, origins, local, slots, chip...  2.46 us
    ppermute x3, waiting for transfers between devices, on_device(): backward[0] = lax.ppermute(backward[0], 'dom', behind)  2.31 us
    ppermute x2, starting transfers between devices, on_device(): twins = [lax.ppermute(half, 'rep', facing) for half in owns]  2.09 us
  transfers between devices with their start and end apart: 19, of which 11 were waited for; matrix products, arithmetic and copies ran while one was open for 2% of the time, Pallas kernels for 11%

profile of v4, /device:TPU:0, one launch (start us, length us, event | category | flops | bytes accessed | tf_op | source)
XLA Modules:
  0.0 44.5 jit_solution(11426552155753516183)
XLA Ops:
  0.0 0.0 copy-start
  0.0 1.8 %pack.1 = (bf16[256,256]{1,0:T(8,128)(2,1)S(1)}, bf16[256,256]{1,0:T(8,128)(2,1)S(1)}, bf16[53,128,128]{2,1,0:T(8,128)(2,1)S(1)}) custom-call(bf16[256,1024]{1,0:T(8,128)(2,1)} %features.1, bf16[2,128,1024]{2,1,0:T(8,128)(2,1)} %bitcast.4, bf16[48,128,128]{2,1,0:T(8,128)(2,1)} %bitcast.5, s32[2,2,12]{2,1,0:T(2,128)} %columns_in.1, s32[2,2]{1,0:T(2,128)} %counts_in.1, ...), custom_call_target="tpu_custom_call" | custom-call | tf_op jit(solution)/shard_map/pack/pallas_call | solution.py:136
  1.8 0.5 %collective-permute-start = (bf16[53,128,128]{2,1,0:T(8,128)(2,1)S(1)}, bf16[53,128,128]{2,1,0:T(8,128)(2,1)S(1)}, u32[]{:S(2)}, u32[]{:S(2)}) collective-permute-start(bf16[53,128,128]{2,1,0:T(8,128)(2,1)S(1)} %get-tuple-element.10.refs_0_.bundle), channel_id=1, source_target_pairs={{0,2},{2,0},{4,6},{6,4},{8,10},{10,8},{12,14},{14,12},{16,18},{18,... | collective-permute-start | bytes 5210120 | tf_op jit(solution)/shard_map/ppermute | solution.py:335
  2.3 2.6 %collective-permute-start.10 = (bf16[256,256]{1,0:T(8,128)(2,1)S(1)}, bf16[256,256]{1,0:T(8,128)(2,1)S(1)}, u32[]{:S(2)}, u32[]{:S(2)}) collective-permute-start(bf16[256,256]{1,0:T(8,128)(2,1)S(1)} %get-tuple-element.12.refs_2_), channel_id=1, source_target_pairs={{0,4},{2,6},{4,12},{6,14},{8,0},{10,2},{12,20},{14,22},{16,8},{18,... | collective-permute-start | bytes 393224 | tf_op jit(solution)/shard_map/ppermute | solution.py:349
  4.9 0.1 collective-permute-start.1
  5.0 1.7 %collective-permute-start.7 = (bf16[256,256]{1,0:T(8,128)(2,1)S(1)}, bf16[256,256]{1,0:T(8,128)(2,1)S(1)}, u32[]{:S(2)}, u32[]{:S(2)}) collective-permute-start(bf16[256,256]{1,0:T(8,128)(2,1)S(1)} %get-tuple-element.12.refs_2_), channel_id=1, source_target_pairs={{0,8},{2,10},{4,0},{6,2},{8,16},{10,18},{12,4},{14,6},{16,24},{18,... | collective-permute-start | bytes 393224 | tf_op jit(solution)/shard_map/ppermute | solution.py:347
  6.8 0.0 collective-permute-start.4
  6.8 2.3 %collective-permute-done.10.refs_6_ = bf16[256,256]{1,0:T(8,128)(2,1)S(1)} collective-permute-done((bf16[256,256]{1,0:T(8,128)(2,1)S(1)}, bf16[256,256]{1,0:T(8,128)(2,1)S(1)}, u32[]{:S(2)}, u32[]{:S(2)}) %collective-permute-start.10) | collective-permute-done | bytes 131104 | tf_op jit(solution)/shard_map/ppermute | solution.py:349
  9.1 2.1 %collective-permute-start.11 = (bf16[256,256]{1,0:T(8,128)(2,1)S(1)}, bf16[256,256]{1,0:T(8,128)(2,1)S(1)}, u32[]{:S(2)}, u32[]{:S(2)}) collective-permute-start(bf16[256,256]{1,0:T(8,128)(2,1)S(1)} %collective-permute-done.10.refs_6_), channel_id=1, source_target_pairs={{0,4},{2,6},{4,12},{6,14},{8,0},{10,2},{12,20},{14,22},{16,8},{18,... | collective-permute-start | bytes 393224 | tf_op jit(solution)/shard_map/ppermute | solution.py:349
  11.2 0.0 collective-permute-done.1.refs_3_
  11.2 0.0 collective-permute-start.2
  11.2 2.3 %collective-permute-done.7.refs_5_ = bf16[256,256]{1,0:T(8,128)(2,1)S(1)} collective-permute-done((bf16[256,256]{1,0:T(8,128)(2,1)S(1)}, bf16[256,256]{1,0:T(8,128)(2,1)S(1)}, u32[]{:S(2)}, u32[]{:S(2)}) %collective-permute-start.7) | collective-permute-done | bytes 131104 | tf_op jit(solution)/shard_map/ppermute | solution.py:347
  13.5 0.1 collective-permute-start.8
  13.7 0.0 collective-permute-done.4.refs_4_
  13.7 1.9 %collective-permute-start.5 = (bf16[256,256]{1,0:T(8,128)(2,1)S(1)}, bf16[256,256]{1,0:T(8,128)(2,1)S(1)}, u32[]{:S(2)}, u32[]{:S(2)}) collective-permute-start(bf16[256,256]{1,0:T(8,128)(2,1)S(1)} %collective-permute-done.4.refs_4_), channel_id=1, source_target_pairs={{0,4},{2,6},{4,12},{6,14},{8,0},{10,2},{12,20},{14,22},{16,8},{18,... | collective-permute-start | bytes 393224 | tf_op jit(solution)/shard_map/ppermute | solution.py:345
  15.6 0.0 collective-permute-done.11.refs_10_
  15.6 1.6 %collective-permute-start.12 = (bf16[256,256]{1,0:T(8,128)(2,1)S(1)}, bf16[256,256]{1,0:T(8,128)(2,1)S(1)}, u32[]{:S(2)}, u32[]{:S(2)}) collective-permute-start(bf16[256,256]{1,0:T(8,128)(2,1)S(1)} %collective-permute-done.11.refs_10_), channel_id=1, source_target_pairs={{0,4},{2,6},{4,12},{6,14},{8,0},{10,2},{12,20},{14,22},{16,8},{18,... | collective-permute-start | bytes 393224 | tf_op jit(solution)/shard_map/ppermute | solution.py:349
  17.1 0.1 collective-permute-done.2.refs_7_
  17.2 0.3 collective-permute-start.3
  17.6 2.5 %collective-permute-done.8.refs_9_ = bf16[256,256]{1,0:T(8,128)(2,1)S(1)} collective-permute-done((bf16[256,256]{1,0:T(8,128)(2,1)S(1)}, bf16[256,256]{1,0:T(8,128)(2,1)S(1)}, u32[]{:S(2)}, u32[]{:S(2)}) %collective-permute-start.8) | collective-permute-done | bytes 131104 | tf_op jit(solution)/shard_map/ppermute | solution.py:347
  20.1 0.0 collective-permute-start.9
  20.1 0.0 collective-permute-done.5.refs_8_
  20.1 2.0 %collective-permute-start.6 = (bf16[256,256]{1,0:T(8,128)(2,1)S(1)}, bf16[256,256]{1,0:T(8,128)(2,1)S(1)}, u32[]{:S(2)}, u32[]{:S(2)}) collective-permute-start(bf16[256,256]{1,0:T(8,128)(2,1)S(1)} %collective-permute-done.5.refs_8_), channel_id=1, source_target_pairs={{0,4},{2,6},{4,12},{6,14},{8,0},{10,2},{12,20},{14,22},{16,8},{18,... | collective-permute-start | bytes 393224 | tf_op jit(solution)/shard_map/ppermute | solution.py:345
  22.1 0.0 collective-permute-done.12.refs_5_
  22.1 1.6 %collective-permute-start.14 = (bf16[256,256]{1,0:T(8,128)(2,1)S(1)}, bf16[256,256]{1,0:T(8,128)(2,1)S(1)}, u32[]{:S(2)}, u32[]{:S(2)}) collective-permute-start(bf16[256,256]{1,0:T(8,128)(2,1)S(1)} %collective-permute-done.12.refs_5_), channel_id=1, source_target_pairs={{0,4},{2,6},{4,12},{6,14},{8,0},{10,2},{12,20},{14,22},{16,8},{18,... | collective-permute-start | bytes 393224 | tf_op jit(solution)/shard_map/ppermute | solution.py:354
  23.7 0.0 collective-permute-done.3.refs_2_
  23.7 0.5 %collective-permute-start.13 = (bf16[256,256]{1,0:T(8,128)(2,1)S(1)}, bf16[256,256]{1,0:T(8,128)(2,1)S(1)}, u32[]{:S(2)}, u32[]{:S(2)}) collective-permute-start(bf16[256,256]{1,0:T(8,128)(2,1)S(1)} %collective-permute-done.3.refs_2_), channel_id=1, source_target_pairs={{0,8},{2,10},{4,0},{6,2},{8,16},{10,18},{12,4},{14,6},{16,24},{18,... | collective-permute-start | bytes 393224 | tf_op jit(solution)/shard_map/ppermute | solution.py:353
  24.1 0.0 collective-permute-done.refs_1_.bundle
  24.1 1.6 %absorb.2.refs_6_ = f32[2,2,256,256]{3,2,1,0:T(8,128)S(1)} custom-call(bf16[53,128,128]{2,1,0:T(8,128)(2,1)S(1)} %get-tuple-element.10.refs_0_.bundle, bf16[53,128,128]{2,1,0:T(8,128)(2,1)S(1)} %collective-permute-done.refs_1_.bundle, bf16[256,256]{1,0:T(8,128)(2,1)S(1)} %get-tuple-element.12.refs_2_, bf16[256,256]{1,0:T(8,128)(2,1)S(1)} %collective-permute-done.1.refs_3_, ...), custom_call_target="tpu_custom_call" | custom-call | flops 1207959552 | tf_op jit(solution)/shard_map/absorb/pallas_call | solution.py:211
  25.8 0.2 collective-permute-done.9.refs_4_
  25.9 0.2 collective-permute-done.6.refs_3_
  26.1 0.8 %absorb.3.sums = f32[2,2,256,256]{3,2,1,0:T(8,128)S(1)} custom-call(bf16[53,128,128]{2,1,0:T(8,128)(2,1)S(1)} %get-tuple-element.10.refs_0_.bundle, bf16[53,128,128]{2,1,0:T(8,128)(2,1)S(1)} %collective-permute-done.refs_1_.bundle, bf16[256,256]{1,0:T(8,128)(2,1)S(1)} %collective-permute-done.3.refs_2_, bf16[256,256]{1,0:T(8,128)(2,1)S(1)} %collective-permute-done.6.refs_3_, ...), custom_call_target="tpu_custom_call" | custom-call | flops 536870912 | tf_op jit(solution)/shard_map/absorb/pallas_call | solution.py:211
  26.9 0.6 %collective-permute-done.14.refs_1_ = bf16[256,256]{1,0:T(8,128)(2,1)S(1)} collective-permute-done((bf16[256,256]{1,0:T(8,128)(2,1)S(1)}, bf16[256,256]{1,0:T(8,128)(2,1)S(1)}, u32[]{:S(2)}, u32[]{:S(2)}) %collective-permute-start.14) | collective-permute-done | bytes 131104 | tf_op jit(solution)/shard_map/ppermute | solution.py:354
  27.5 1.1 %collective-permute-done.13.refs_0_ = bf16[256,256]{1,0:T(8,128)(2,1)S(1)} collective-permute-done((bf16[256,256]{1,0:T(8,128)(2,1)S(1)}, bf16[256,256]{1,0:T(8,128)(2,1)S(1)}, u32[]{:S(2)}, u32[]{:S(2)}) %collective-permute-start.13) | collective-permute-done | bytes 131104 | tf_op jit(solution)/shard_map/ppermute | solution.py:353
  28.6 0.4 close.3
  29.0 0.0 copy-start.3
  29.1 0.1 collective-permute-start.15
  29.1 1.6 %collective-permute-start.16 = (bf16[2,256,256]{2,1,0:T(8,128)(2,1)S(1)}, bf16[2,256,256]{2,1,0:T(8,128)(2,1)S(1)}, u32[]{:S(2)}, u32[]{:S(2)}) collective-permute-start(bf16[2,256,256]{2,1,0:T(8,128)(2,1)S(1)} %close.3), channel_id=1, source_target_pairs={{0,3},{1,2},{2,1},{3,0},{4,7},{5,6},{6,5},{7,4},{8,11},{9,10},{10,... | collective-permute-start | bytes 786440 | tf_op jit(solution)/shard_map/ppermute | solution.py:365
  30.7 0.0 copy-start.2
  30.7 0.4 close.2
  31.1 0.0 copy-start.1
  31.2 0.6 %collective-permute-start.18 = (bf16[2,128,256]{2,1,0:T(8,128)(2,1)S(1)}, bf16[2,128,256]{2,1,0:T(8,128)(2,1)S(1)}, u32[]{:S(2)}, u32[]{:S(2)}) collective-permute-start(bf16[2,128,256]{2,1,0:T(8,128)(2,1)S(1)} %get-tuple-element.13.refs_0_), channel_id=1, source_target_pairs={{0,1},{1,0},{2,3},{3,2},{4,5},{5,4},{6,7},{7,6},{8,9},{9,8},{10,11... | collective-permute-start | bytes 393224 | tf_op jit(solution)/shard_map/ppermute | solution.py:368
  31.8 1.5 %collective-permute-start.17 = (bf16[2,128,256]{2,1,0:T(8,128)(2,1)S(1)}, bf16[2,128,256]{2,1,0:T(8,128)(2,1)S(1)}, u32[]{:S(2)}, u32[]{:S(2)}) collective-permute-start(bf16[2,128,256]{2,1,0:T(8,128)(2,1)S(1)} %get-tuple-element.14.refs_1_), channel_id=1, source_target_pairs={{0,1},{1,0},{2,3},{3,2},{4,5},{5,4},{6,7},{7,6},{8,9},{9,8},{10,11... | collective-permute-start | bytes 393224 | tf_op jit(solution)/shard_map/ppermute | solution.py:368
  33.2 0.0 copy-done
  33.3 0.0 copy-done.3
  33.3 0.7 %fusion.base = f32[256,1024]{1,0:T(8,128)S(1)} fusion(bf16[256,1024]{1,0:T(8,128)(2,1)S(1)} %copy-done.3, bf16[1024,1024]{1,0:T(8,128)(2,1)S(1)} %copy-done), kind=kOutput, calls=%fused_computation | convolution fusion | flops 536870912 | bytes 3670016 | tf_op jit(solution)/shard_map/dot_general | solution.py:370
  34.0 0.0 collective-permute-done.15.refs_2_
  34.0 0.0 copy-done.2
  34.0 0.0 copy-done.1
  34.0 0.7 %project.2.base = f32[256,1024]{1,0:T(8,128)S(1)} custom-call(f32[256,1024]{1,0:T(8,128)S(1)} %fusion.base, bf16[1024,1024]{1,0:T(8,128)(2,1)S(1)} %copy-done.1, bf16[1024,1024]{1,0:T(8,128)(2,1)S(1)} %copy-done.2, bf16[2,128,256]{2,1,0:T(8,128)(2,1)S(1)} %get-tuple-element.13.refs_0_, bf16[2,128,256]{2,1,0:T(8,128)(2,1)S(1)} %get-tuple-element.14.refs_1_, ...), custom_call_target="tpu_custom_call" | custom-call | flops 536870912 | tf_op jit(solution)/shard_map/project/pallas_call | solution.py:279
  34.7 2.7 %collective-permute-done.16.refs_0_ = bf16[2,256,256]{2,1,0:T(8,128)(2,1)S(1)} collective-permute-done((bf16[2,256,256]{2,1,0:T(8,128)(2,1)S(1)}, bf16[2,256,256]{2,1,0:T(8,128)(2,1)S(1)}, u32[]{:S(2)}, u32[]{:S(2)}) %collective-permute-start.16) | collective-permute-done | bytes 262176 | tf_op jit(solution)/shard_map/ppermute | solution.py:365
  37.4 0.4 project.3.base
  37.8 3.4 %collective-permute-done.18.part = bf16[2,128,256]{2,1,0:T(8,128)(2,1)S(1)} collective-permute-done((bf16[2,128,256]{2,1,0:T(8,128)(2,1)S(1)}, bf16[2,128,256]{2,1,0:T(8,128)(2,1)S(1)}, u32[]{:S(2)}, u32[]{:S(2)}) %collective-permute-start.18) | collective-permute-done | bytes 131104 | tf_op jit(solution)/shard_map/ppermute | solution.py:368
  41.2 1.0 %finish.2.refs_0_ = bf16[256,1024]{1,0:T(8,128)(2,1)} custom-call(f32[256,1024]{1,0:T(8,128)S(1)} %project.3.base, bf16[1024,1024]{1,0:T(8,128)(2,1)S(1)} %copy-done.1, bf16[1024,1024]{1,0:T(8,128)(2,1)S(1)} %copy-done.2, bf16[2,128,256]{2,1,0:T(8,128)(2,1)S(1)} %collective-permute-done.18.part), custom_call_target="tpu_custom_call" | custom-call | flops 134217728 | tf_op jit(solution)/shard_map/finish/pallas_call | solution.py:313
  42.2 1.2 %collective-permute-done.17.part = bf16[2,128,256]{2,1,0:T(8,128)(2,1)S(1)} collective-permute-done((bf16[2,128,256]{2,1,0:T(8,128)(2,1)S(1)}, bf16[2,128,256]{2,1,0:T(8,128)(2,1)S(1)}, u32[]{:S(2)}, u32[]{:S(2)}) %collective-permute-start.17) | collective-permute-done | bytes 131104 | tf_op jit(solution)/shard_map/ppermute | solution.py:368
  43.4 1.0 %finish.3 = bf16[256,1024]{1,0:T(8,128)(2,1)} custom-call(f32[256,1024]{1,0:T(8,128)S(1)} %project.3.base, bf16[1024,1024]{1,0:T(8,128)(2,1)S(1)} %copy-done.1, bf16[1024,1024]{1,0:T(8,128)(2,1)S(1)} %copy-done.2, bf16[2,128,256]{2,1,0:T(8,128)(2,1)S(1)} %collective-permute-done.17.part, bf16[256,1024]{1,0:T(8,128)(2,1)} %finish.2.refs_0_), custom_call_target="tpu_custom_call", output_to_operand_aliasing={{}: (4, {})} | custom-call | flops 134217728 | tf_op jit(solution)/shard_map/finish/pallas_call | solution.py:313
Async XLA Ops:
  0.0 33.3 %copy-start = (bf16[1024,1024]{1,0:T(8,128)(2,1)S(1)}, bf16[1024,1024]{1,0:T(8,128)(2,1)}, u32[]{:S(2)}) copy-start(bf16[1024,1024]{1,0:T(8,128)(2,1)} %param.13) | copy-start | bytes 6291460
  1.8 22.3 %collective-permute-start = (bf16[53,128,128]{2,1,0:T(8,128)(2,1)S(1)}, bf16[53,128,128]{2,1,0:T(8,128)(2,1)S(1)}, u32[]{:S(2)}, u32[]{:S(2)}) collective-permute-start(bf16[53,128,128]{2,1,0:T(8,128)(2,1)S(1)} %get-tuple-element.10.refs_0_.bundle), channel_id=1, source_target_pairs={{0,2},{2,0},{4,6},{6,4},{8,10},{10,8},{12,14},{14,12},{16,18},{18,... | collective-permute-start | bytes 5210120 | tf_op jit(solution)/shard_map/ppermute | solution.py:335
  2.3 6.7 %collective-permute-start.10 = (bf16[256,256]{1,0:T(8,128)(2,1)S(1)}, bf16[256,256]{1,0:T(8,128)(2,1)S(1)}, u32[]{:S(2)}, u32[]{:S(2)}) collective-permute-start(bf16[256,256]{1,0:T(8,128)(2,1)S(1)} %get-tuple-element.12.refs_2_), channel_id=1, source_target_pairs={{0,4},{2,6},{4,12},{6,14},{8,0},{10,2},{12,20},{14,22},{16,8},{18,... | collective-permute-start | bytes 393224 | tf_op jit(solution)/shard_map/ppermute | solution.py:349
  4.9 6.3 %collective-permute-start.1 = (bf16[256,256]{1,0:T(8,128)(2,1)S(1)}, bf16[256,256]{1,0:T(8,128)(2,1)S(1)}, u32[]{:S(2)}, u32[]{:S(2)}) collective-permute-start(bf16[256,256]{1,0:T(8,128)(2,1)S(1)} %get-tuple-element.11), channel_id=1, source_target_pairs={{0,10},{2,8},{4,2},{6,0},{8,18},{10,16},{12,6},{14,4},{16,26},{18,... | collective-permute-start | bytes 393224 | tf_op jit(solution)/shard_map/ppermute | solution.py:343
  5.0 8.5 %collective-permute-start.7 = (bf16[256,256]{1,0:T(8,128)(2,1)S(1)}, bf16[256,256]{1,0:T(8,128)(2,1)S(1)}, u32[]{:S(2)}, u32[]{:S(2)}) collective-permute-start(bf16[256,256]{1,0:T(8,128)(2,1)S(1)} %get-tuple-element.12.refs_2_), channel_id=1, source_target_pairs={{0,8},{2,10},{4,0},{6,2},{8,16},{10,18},{12,4},{14,6},{16,24},{18,... | collective-permute-start | bytes 393224 | tf_op jit(solution)/shard_map/ppermute | solution.py:347
  6.8 6.9 %collective-permute-start.4 = (bf16[256,256]{1,0:T(8,128)(2,1)S(1)}, bf16[256,256]{1,0:T(8,128)(2,1)S(1)}, u32[]{:S(2)}, u32[]{:S(2)}) collective-permute-start(bf16[256,256]{1,0:T(8,128)(2,1)S(1)} %get-tuple-element.11), channel_id=1, source_target_pairs={{0,6},{2,4},{4,14},{6,12},{8,2},{10,0},{12,22},{14,20},{16,10},{18... | collective-permute-start | bytes 393224 | tf_op jit(solution)/shard_map/ppermute | solution.py:345
  9.1 6.5 %collective-permute-start.11 = (bf16[256,256]{1,0:T(8,128)(2,1)S(1)}, bf16[256,256]{1,0:T(8,128)(2,1)S(1)}, u32[]{:S(2)}, u32[]{:S(2)}) collective-permute-start(bf16[256,256]{1,0:T(8,128)(2,1)S(1)} %collective-permute-done.10.refs_6_), channel_id=1, source_target_pairs={{0,4},{2,6},{4,12},{6,14},{8,0},{10,2},{12,20},{14,22},{16,8},{18,... | collective-permute-start | bytes 393224 | tf_op jit(solution)/shard_map/ppermute | solution.py:349
  11.2 6.0 %collective-permute-start.2 = (bf16[256,256]{1,0:T(8,128)(2,1)S(1)}, bf16[256,256]{1,0:T(8,128)(2,1)S(1)}, u32[]{:S(2)}, u32[]{:S(2)}) collective-permute-start(bf16[256,256]{1,0:T(8,128)(2,1)S(1)} %collective-permute-done.1.refs_3_), channel_id=1, source_target_pairs={{0,8},{2,10},{4,0},{6,2},{8,16},{10,18},{12,4},{14,6},{16,24},{18,... | collective-permute-start | bytes 393224 | tf_op jit(solution)/shard_map/ppermute | solution.py:343
  13.5 6.5 %collective-permute-start.8 = (bf16[256,256]{1,0:T(8,128)(2,1)S(1)}, bf16[256,256]{1,0:T(8,128)(2,1)S(1)}, u32[]{:S(2)}, u32[]{:S(2)}) collective-permute-start(bf16[256,256]{1,0:T(8,128)(2,1)S(1)} %collective-permute-done.7.refs_5_), channel_id=1, source_target_pairs={{0,8},{2,10},{4,0},{6,2},{8,16},{10,18},{12,4},{14,6},{16,24},{18,... | collective-permute-start | bytes 393224 | tf_op jit(solution)/shard_map/ppermute | solution.py:347
  13.7 6.4 %collective-permute-start.5 = (bf16[256,256]{1,0:T(8,128)(2,1)S(1)}, bf16[256,256]{1,0:T(8,128)(2,1)S(1)}, u32[]{:S(2)}, u32[]{:S(2)}) collective-permute-start(bf16[256,256]{1,0:T(8,128)(2,1)S(1)} %collective-permute-done.4.refs_4_), channel_id=1, source_target_pairs={{0,4},{2,6},{4,12},{6,14},{8,0},{10,2},{12,20},{14,22},{16,8},{18,... | collective-permute-start | bytes 393224 | tf_op jit(solution)/shard_map/ppermute | solution.py:345
  15.6 6.5 %collective-permute-start.12 = (bf16[256,256]{1,0:T(8,128)(2,1)S(1)}, bf16[256,256]{1,0:T(8,128)(2,1)S(1)}, u32[]{:S(2)}, u32[]{:S(2)}) collective-permute-start(bf16[256,256]{1,0:T(8,128)(2,1)S(1)} %collective-permute-done.11.refs_10_), channel_id=1, source_target_pairs={{0,4},{2,6},{4,12},{6,14},{8,0},{10,2},{12,20},{14,22},{16,8},{18,... | collective-permute-start | bytes 393224 | tf_op jit(solution)/shard_map/ppermute | solution.py:349
  17.2 6.4 %collective-permute-start.3 = (bf16[256,256]{1,0:T(8,128)(2,1)S(1)}, bf16[256,256]{1,0:T(8,128)(2,1)S(1)}, u32[]{:S(2)}, u32[]{:S(2)}) collective-permute-start(bf16[256,256]{1,0:T(8,128)(2,1)S(1)} %collective-permute-done.2.refs_7_), channel_id=1, source_target_pairs={{0,8},{2,10},{4,0},{6,2},{8,16},{10,18},{12,4},{14,6},{16,24},{18,... | collective-permute-start | bytes 393224 | tf_op jit(solution)/shard_map/ppermute | solution.py:343
  20.1 5.9 %collective-permute-start.9 = (bf16[256,256]{1,0:T(8,128)(2,1)S(1)}, bf16[256,256]{1,0:T(8,128)(2,1)S(1)}, u32[]{:S(2)}, u32[]{:S(2)}) collective-permute-start(bf16[256,256]{1,0:T(8,128)(2,1)S(1)} %collective-permute-done.8.refs_9_), channel_id=1, source_target_pairs={{0,8},{2,10},{4,0},{6,2},{8,16},{10,18},{12,4},{14,6},{16,24},{18,... | collective-permute-start | bytes 393224 | tf_op jit(solution)/shard_map/ppermute | solution.py:347
  20.1 6.0 %collective-permute-start.6 = (bf16[256,256]{1,0:T(8,128)(2,1)S(1)}, bf16[256,256]{1,0:T(8,128)(2,1)S(1)}, u32[]{:S(2)}, u32[]{:S(2)}) collective-permute-start(bf16[256,256]{1,0:T(8,128)(2,1)S(1)} %collective-permute-done.5.refs_8_), channel_id=1, source_target_pairs={{0,4},{2,6},{4,12},{6,14},{8,0},{10,2},{12,20},{14,22},{16,8},{18,... | collective-permute-start | bytes 393224 | tf_op jit(solution)/shard_map/ppermute | solution.py:345
  22.1 5.4 %collective-permute-start.14 = (bf16[256,256]{1,0:T(8,128)(2,1)S(1)}, bf16[256,256]{1,0:T(8,128)(2,1)S(1)}, u32[]{:S(2)}, u32[]{:S(2)}) collective-permute-start(bf16[256,256]{1,0:T(8,128)(2,1)S(1)} %collective-permute-done.12.refs_5_), channel_id=1, source_target_pairs={{0,4},{2,6},{4,12},{6,14},{8,0},{10,2},{12,20},{14,22},{16,8},{18,... | collective-permute-start | bytes 393224 | tf_op jit(solution)/shard_map/ppermute | solution.py:354
  23.7 5.0 %collective-permute-start.13 = (bf16[256,256]{1,0:T(8,128)(2,1)S(1)}, bf16[256,256]{1,0:T(8,128)(2,1)S(1)}, u32[]{:S(2)}, u32[]{:S(2)}) collective-permute-start(bf16[256,256]{1,0:T(8,128)(2,1)S(1)} %collective-permute-done.3.refs_2_), channel_id=1, source_target_pairs={{0,8},{2,10},{4,0},{6,2},{8,16},{10,18},{12,4},{14,6},{16,24},{18,... | collective-permute-start | bytes 393224 | tf_op jit(solution)/shard_map/ppermute | solution.py:353
  29.0 4.2 %copy-start.3 = (bf16[256,1024]{1,0:T(8,128)(2,1)S(1)}, bf16[256,1024]{1,0:T(8,128)(2,1)}, u32[]{:S(2)}) copy-start(bf16[256,1024]{1,0:T(8,128)(2,1)} %features.1) | copy-start | bytes 1572868
  29.1 4.9 %collective-permute-start.15 = (bf16[2,256,256]{2,1,0:T(8,128)(2,1)S(1)}, bf16[2,256,256]{2,1,0:T(8,128)(2,1)S(1)}, u32[]{:S(2)}, u32[]{:S(2)}) collective-permute-start(bf16[2,256,256]{2,1,0:T(8,128)(2,1)S(1)} %close.3), channel_id=1, source_target_pairs={{0,2},{2,0},{4,6},{6,4},{8,10},{10,8},{12,14},{14,12},{16,18},{18,... | collective-permute-start | bytes 786440 | tf_op jit(solution)/shard_map/ppermute | solution.py:366
  29.1 8.2 %collective-permute-start.16 = (bf16[2,256,256]{2,1,0:T(8,128)(2,1)S(1)}, bf16[2,256,256]{2,1,0:T(8,128)(2,1)S(1)}, u32[]{:S(2)}, u32[]{:S(2)}) collective-permute-start(bf16[2,256,256]{2,1,0:T(8,128)(2,1)S(1)} %close.3), channel_id=1, source_target_pairs={{0,3},{1,2},{2,1},{3,0},{4,7},{5,6},{6,5},{7,4},{8,11},{9,10},{10,... | collective-permute-start | bytes 786440 | tf_op jit(solution)/shard_map/ppermute | solution.py:365
  30.7 3.2 %copy-start.2 = (bf16[1024,1024]{1,0:T(8,128)(2,1)S(1)}, bf16[1024,1024]{1,0:T(8,128)(2,1)}, u32[]{:S(2)}) copy-start(bf16[1024,1024]{1,0:T(8,128)(2,1)} %w_out.7) | copy-start | bytes 6291460
  31.1 2.8 %copy-start.1 = (bf16[1024,1024]{1,0:T(8,128)(2,1)S(1)}, bf16[1024,1024]{1,0:T(8,128)(2,1)}, u32[]{:S(2)}) copy-start(bf16[1024,1024]{1,0:T(8,128)(2,1)} %w_in.7) | copy-start | bytes 6291460
  31.2 10.0 %collective-permute-start.18 = (bf16[2,128,256]{2,1,0:T(8,128)(2,1)S(1)}, bf16[2,128,256]{2,1,0:T(8,128)(2,1)S(1)}, u32[]{:S(2)}, u32[]{:S(2)}) collective-permute-start(bf16[2,128,256]{2,1,0:T(8,128)(2,1)S(1)} %get-tuple-element.13.refs_0_), channel_id=1, source_target_pairs={{0,1},{1,0},{2,3},{3,2},{4,5},{5,4},{6,7},{7,6},{8,9},{9,8},{10,11... | collective-permute-start | bytes 393224 | tf_op jit(solution)/shard_map/ppermute | solution.py:368
  31.8 11.7 %collective-permute-start.17 = (bf16[2,128,256]{2,1,0:T(8,128)(2,1)S(1)}, bf16[2,128,256]{2,1,0:T(8,128)(2,1)S(1)}, u32[]{:S(2)}, u32[]{:S(2)}) collective-permute-start(bf16[2,128,256]{2,1,0:T(8,128)(2,1)S(1)} %get-tuple-element.14.refs_1_), channel_id=1, source_target_pairs={{0,1},{1,0},{2,3},{3,2},{4,5},{5,4},{6,7},{7,6},{8,9},{9,8},{10,11... | collective-permute-start | bytes 393224 | tf_op jit(solution)/shard_map/ppermute | solution.py:368

commit v5 on v4

--- a/solution.py
+++ b/solution.py
@@ -357,15 +357,14 @@
     sums = absorb(bundles, shape, early, None, chips)
     sums = absorb(bundles, shape, steps[-1], sums, chips)
     (other,) = close(bundles[1], shape, last, sums, 1, chips, 1)
-    owns = close(bundles[0], shape, last, sums, 0, chips, shape[0])
-
-    across = [
-        (d * reps + r, (d ^ 1) * reps + (r + 1) % reps) for d in range(devices) for r in range(reps)
-    ]
-    diagonal = lax.ppermute(other, ("dom", "rep"), across)
+    owns = close(bundles[0], shape, last, sums, 0, chips, 1)
+
+    facing = [(r, (r + 1) % reps) for r in range(reps)]
+    passing = lax.ppermute(other, "rep", facing)
+    twins = [lax.ppermute(half, "rep", facing) for half in owns]
+    other, passing = lax.optimization_barrier((other, passing))
     core_side = lax.ppermute(other, "dom", cores)
-    facing = [(r, (r + 1) % reps) for r in range(reps)]
-    twins = [lax.ppermute(half, "rep", facing) for half in owns]
+    diagonal = lax.ppermute(passing, "dom", cores)
 
     hidden = jnp.dot(features, w_self, preferred_element_type=F32)
     hidden = project(hidden, [owns, [core_side]], ((0, 0), (0, 1)), w_in, w_out)

time: 44.6 us -> 42.2 us (0.946)
  starting transfers between devices: 18.9 us -> 17.8 us
  Pallas kernels: 8.27 us -> 7.46 us
  waiting for transfers between devices: 16.5 us -> 16 us
    ppermute x2 -> x1, waiting for transfers between devices: 4.56 us -> 0.08 us  [on_device(): twins = [lax.ppermute(half, 'rep', facing) for half in owns]]
    ppermute x1 -> x2, waiting for transfers between devices: 2.66 us -> 6.41 us  [the longest x1 6.41 us: on_device(): passing = lax.ppermute(other, 'rep', facing)]
    ppermute x2 -> x1, starting transfers between devices: 2.09 us -> 0.6 us  [on_device(): twins = [lax.ppermute(half, 'rep', facing) for half in owns]]
    pallas_call x2 -> x1, Pallas kernels: 2.06 us -> 1.24 us  [finish(): pl.pallas_call(functools.partial(finish_body, band, quarter), out_shape=j...]
    ppermute x1 -> x2, starting transfers between devices: 1.61 us -> 2.06 us  [the longest x1 1.56 us: on_device(): passing = lax.ppermute(other, 'rep', facing)]
  transfers between devices with their start and end apart: 19 -> 19, of which waited for: 11 -> 11; matrix products, arithmetic and copies ran while one was open for 2% -> 2% of each run, Pallas kernels for 11% -> 10%
where the time goes in v5:
time: 42.2 us; the launch traced here: 42.1 us
  starting transfers between devices  17.8 us (42%)
  waiting for transfers between devices  16 us (38%)
  Pallas kernels  7.46 us (18%)
  matrix products  0.7 us (2%)
    ppermute x1, waiting for transfers between devices, on_device(): passing = lax.ppermute(other, 'rep', facing)  6.41 us
    ppermute x3, starting transfers between devices, on_device(): backward[0] = lax.ppermute(backward[0], 'dom', behind)  6.29 us
    ppermute x3, waiting for transfers between devices, on_device(): forward[0] = lax.ppermute(forward[0], 'dom', ahead)  4.92 us
    ppermute x3, starting transfers between devices, on_device(): lax.ppermute(backward[1], 'dom', swapped(behind) if step == 1 else behind)  3.91 us
    pallas_call x2, Pallas kernels, absorb(): pl.pallas_call(functools.partial(absorb_body, origins, local, slots, chip...  2.46 us
    ppermute x3, waiting for transfers between devices, on_device(): backward[0] = lax.ppermute(backward[0], 'dom', behind)  2.31 us
    ppermute x3, starting transfers between devices, on_device(): forward[0] = lax.ppermute(forward[0], 'dom', ahead)  1.89 us
    pallas_call x1, Pallas kernels, pack(): pl.pallas_call(functools.partial(pack_body, devices // 2, local), out_sha...  1.81 us
  transfers between devices with their start and end apart: 19, of which 11 were waited for; matrix products, arithmetic and copies ran while one was open for 2% of the time, Pallas kernels for 10%

profile of v5, /device:TPU:0, one launch (start us, length us, event | category | flops | bytes accessed | tf_op | source)
XLA Modules:
  0.0 42.1 jit_solution(12900719280051805306)
XLA Ops:
  0.0 0.0 copy-start
  0.0 1.8 %pack.1 = (bf16[256,256]{1,0:T(8,128)(2,1)S(1)}, bf16[256,256]{1,0:T(8,128)(2,1)S(1)}, bf16[53,128,128]{2,1,0:T(8,128)(2,1)S(1)}) custom-call(bf16[256,1024]{1,0:T(8,128)(2,1)} %features.1, bf16[2,128,1024]{2,1,0:T(8,128)(2,1)} %bitcast.4, bf16[48,128,128]{2,1,0:T(8,128)(2,1)} %bitcast.5, s32[2,2,12]{2,1,0:T(2,128)} %columns_in.1, s32[2,2]{1,0:T(2,128)} %counts_in.1, ...), custom_call_target="tpu_custom_call" | custom-call | tf_op jit(solution)/shard_map/pack/pallas_call | solution.py:136
  1.8 0.5 %collective-permute-start = (bf16[53,128,128]{2,1,0:T(8,128)(2,1)S(1)}, bf16[53,128,128]{2,1,0:T(8,128)(2,1)S(1)}, u32[]{:S(2)}, u32[]{:S(2)}) collective-permute-start(bf16[53,128,128]{2,1,0:T(8,128)(2,1)S(1)} %get-tuple-element.10.refs_0_.bundle), channel_id=1, source_target_pairs={{0,2},{2,0},{4,6},{6,4},{8,10},{10,8},{12,14},{14,12},{16,18},{18,... | collective-permute-start | bytes 5210120 | tf_op jit(solution)/shard_map/ppermute | solution.py:335
  2.3 2.6 %collective-permute-start.10 = (bf16[256,256]{1,0:T(8,128)(2,1)S(1)}, bf16[256,256]{1,0:T(8,128)(2,1)S(1)}, u32[]{:S(2)}, u32[]{:S(2)}) collective-permute-start(bf16[256,256]{1,0:T(8,128)(2,1)S(1)} %get-tuple-element.12.refs_2_), channel_id=1, source_target_pairs={{0,4},{2,6},{4,12},{6,14},{8,0},{10,2},{12,20},{14,22},{16,8},{18,... | collective-permute-start | bytes 393224 | tf_op jit(solution)/shard_map/ppermute | solution.py:349
  4.9 0.1 collective-permute-start.1
  5.0 1.7 %collective-permute-start.7 = (bf16[256,256]{1,0:T(8,128)(2,1)S(1)}, bf16[256,256]{1,0:T(8,128)(2,1)S(1)}, u32[]{:S(2)}, u32[]{:S(2)}) collective-permute-start(bf16[256,256]{1,0:T(8,128)(2,1)S(1)} %get-tuple-element.12.refs_2_), channel_id=1, source_target_pairs={{0,8},{2,10},{4,0},{6,2},{8,16},{10,18},{12,4},{14,6},{16,24},{18,... | collective-permute-start | bytes 393224 | tf_op jit(solution)/shard_map/ppermute | solution.py:347
  6.8 0.0 collective-permute-start.4
  6.8 2.3 %collective-permute-done.10.refs_6_ = bf16[256,256]{1,0:T(8,128)(2,1)S(1)} collective-permute-done((bf16[256,256]{1,0:T(8,128)(2,1)S(1)}, bf16[256,256]{1,0:T(8,128)(2,1)S(1)}, u32[]{:S(2)}, u32[]{:S(2)}) %collective-permute-start.10) | collective-permute-done | bytes 131104 | tf_op jit(solution)/shard_map/ppermute | solution.py:349
  9.1 2.1 %collective-permute-start.11 = (bf16[256,256]{1,0:T(8,128)(2,1)S(1)}, bf16[256,256]{1,0:T(8,128)(2,1)S(1)}, u32[]{:S(2)}, u32[]{:S(2)}) collective-permute-start(bf16[256,256]{1,0:T(8,128)(2,1)S(1)} %collective-permute-done.10.refs_6_), channel_id=1, source_target_pairs={{0,4},{2,6},{4,12},{6,14},{8,0},{10,2},{12,20},{14,22},{16,8},{18,... | collective-permute-start | bytes 393224 | tf_op jit(solution)/shard_map/ppermute | solution.py:349
  11.2 0.0 collective-permute-done.1.refs_3_
  11.2 0.0 collective-permute-start.2
  11.2 2.3 %collective-permute-done.7.refs_5_ = bf16[256,256]{1,0:T(8,128)(2,1)S(1)} collective-permute-done((bf16[256,256]{1,0:T(8,128)(2,1)S(1)}, bf16[256,256]{1,0:T(8,128)(2,1)S(1)}, u32[]{:S(2)}, u32[]{:S(2)}) %collective-permute-start.7) | collective-permute-done | bytes 131104 | tf_op jit(solution)/shard_map/ppermute | solution.py:347
  13.5 0.1 collective-permute-start.8
  13.7 0.0 collective-permute-done.4.refs_4_
  13.7 1.9 %collective-permute-start.5 = (bf16[256,256]{1,0:T(8,128)(2,1)S(1)}, bf16[256,256]{1,0:T(8,128)(2,1)S(1)}, u32[]{:S(2)}, u32[]{:S(2)}) collective-permute-start(bf16[256,256]{1,0:T(8,128)(2,1)S(1)} %collective-permute-done.4.refs_4_), channel_id=1, source_target_pairs={{0,4},{2,6},{4,12},{6,14},{8,0},{10,2},{12,20},{14,22},{16,8},{18,... | collective-permute-start | bytes 393224 | tf_op jit(solution)/shard_map/ppermute | solution.py:345
  15.6 0.0 collective-permute-done.11.refs_10_
  15.6 1.6 %collective-permute-start.12 = (bf16[256,256]{1,0:T(8,128)(2,1)S(1)}, bf16[256,256]{1,0:T(8,128)(2,1)S(1)}, u32[]{:S(2)}, u32[]{:S(2)}) collective-permute-start(bf16[256,256]{1,0:T(8,128)(2,1)S(1)} %collective-permute-done.11.refs_10_), channel_id=1, source_target_pairs={{0,4},{2,6},{4,12},{6,14},{8,0},{10,2},{12,20},{14,22},{16,8},{18,... | collective-permute-start | bytes 393224 | tf_op jit(solution)/shard_map/ppermute | solution.py:349
  17.1 0.1 collective-permute-done.2.refs_7_
  17.2 0.3 collective-permute-start.3
  17.6 2.5 %collective-permute-done.8.refs_9_ = bf16[256,256]{1,0:T(8,128)(2,1)S(1)} collective-permute-done((bf16[256,256]{1,0:T(8,128)(2,1)S(1)}, bf16[256,256]{1,0:T(8,128)(2,1)S(1)}, u32[]{:S(2)}, u32[]{:S(2)}) %collective-permute-start.8) | collective-permute-done | bytes 131104 | tf_op jit(solution)/shard_map/ppermute | solution.py:347
  20.1 0.0 collective-permute-start.9
  20.1 0.0 collective-permute-done.5.refs_8_
  20.1 2.0 %collective-permute-start.6 = (bf16[256,256]{1,0:T(8,128)(2,1)S(1)}, bf16[256,256]{1,0:T(8,128)(2,1)S(1)}, u32[]{:S(2)}, u32[]{:S(2)}) collective-permute-start(bf16[256,256]{1,0:T(8,128)(2,1)S(1)} %collective-permute-done.5.refs_8_), channel_id=1, source_target_pairs={{0,4},{2,6},{4,12},{6,14},{8,0},{10,2},{12,20},{14,22},{16,8},{18,... | collective-permute-start | bytes 393224 | tf_op jit(solution)/shard_map/ppermute | solution.py:345
  22.1 0.0 collective-permute-done.12.refs_5_
  22.1 1.6 %collective-permute-start.14 = (bf16[256,256]{1,0:T(8,128)(2,1)S(1)}, bf16[256,256]{1,0:T(8,128)(2,1)S(1)}, u32[]{:S(2)}, u32[]{:S(2)}) collective-permute-start(bf16[256,256]{1,0:T(8,128)(2,1)S(1)} %collective-permute-done.12.refs_5_), channel_id=1, source_target_pairs={{0,4},{2,6},{4,12},{6,14},{8,0},{10,2},{12,20},{14,22},{16,8},{18,... | collective-permute-start | bytes 393224 | tf_op jit(solution)/shard_map/ppermute | solution.py:354
  23.7 0.0 collective-permute-done.3.refs_2_
  23.7 0.5 %collective-permute-start.13 = (bf16[256,256]{1,0:T(8,128)(2,1)S(1)}, bf16[256,256]{1,0:T(8,128)(2,1)S(1)}, u32[]{:S(2)}, u32[]{:S(2)}) collective-permute-start(bf16[256,256]{1,0:T(8,128)(2,1)S(1)} %collective-permute-done.3.refs_2_), channel_id=1, source_target_pairs={{0,8},{2,10},{4,0},{6,2},{8,16},{10,18},{12,4},{14,6},{16,24},{18,... | collective-permute-start | bytes 393224 | tf_op jit(solution)/shard_map/ppermute | solution.py:353
  24.1 0.0 collective-permute-done.refs_1_.bundle
  24.1 1.6 %absorb.2.refs_6_ = f32[2,2,256,256]{3,2,1,0:T(8,128)S(1)} custom-call(bf16[53,128,128]{2,1,0:T(8,128)(2,1)S(1)} %get-tuple-element.10.refs_0_.bundle, bf16[53,128,128]{2,1,0:T(8,128)(2,1)S(1)} %collective-permute-done.refs_1_.bundle, bf16[256,256]{1,0:T(8,128)(2,1)S(1)} %get-tuple-element.12.refs_2_, bf16[256,256]{1,0:T(8,128)(2,1)S(1)} %collective-permute-done.1.refs_3_, ...), custom_call_target="tpu_custom_call" | custom-call | flops 1207959552 | tf_op jit(solution)/shard_map/absorb/pallas_call | solution.py:211
  25.8 0.2 collective-permute-done.9.refs_4_
  25.9 0.2 collective-permute-done.6.refs_3_
  26.1 0.8 %absorb.3.sums = f32[2,2,256,256]{3,2,1,0:T(8,128)S(1)} custom-call(bf16[53,128,128]{2,1,0:T(8,128)(2,1)S(1)} %get-tuple-element.10.refs_0_.bundle, bf16[53,128,128]{2,1,0:T(8,128)(2,1)S(1)} %collective-permute-done.refs_1_.bundle, bf16[256,256]{1,0:T(8,128)(2,1)S(1)} %collective-permute-done.3.refs_2_, bf16[256,256]{1,0:T(8,128)(2,1)S(1)} %collective-permute-done.6.refs_3_, ...), custom_call_target="tpu_custom_call" | custom-call | flops 536870912 | tf_op jit(solution)/shard_map/absorb/pallas_call | solution.py:211
  26.9 0.6 %collective-permute-done.14.refs_1_ = bf16[256,256]{1,0:T(8,128)(2,1)S(1)} collective-permute-done((bf16[256,256]{1,0:T(8,128)(2,1)S(1)}, bf16[256,256]{1,0:T(8,128)(2,1)S(1)}, u32[]{:S(2)}, u32[]{:S(2)}) %collective-permute-start.14) | collective-permute-done | bytes 131104 | tf_op jit(solution)/shard_map/ppermute | solution.py:354
  27.5 1.1 %collective-permute-done.13.refs_0_ = bf16[256,256]{1,0:T(8,128)(2,1)S(1)} collective-permute-done((bf16[256,256]{1,0:T(8,128)(2,1)S(1)}, bf16[256,256]{1,0:T(8,128)(2,1)S(1)}, u32[]{:S(2)}, u32[]{:S(2)}) %collective-permute-start.13) | collective-permute-done | bytes 131104 | tf_op jit(solution)/shard_map/ppermute | solution.py:353
  28.6 0.4 close.3
  29.0 0.0 copy-start.3
  29.1 1.6 %collective-permute-start.15 = (bf16[2,256,256]{2,1,0:T(8,128)(2,1)S(1)}, bf16[2,256,256]{2,1,0:T(8,128)(2,1)S(1)}, u32[]{:S(2)}, u32[]{:S(2)}) collective-permute-start(bf16[2,256,256]{2,1,0:T(8,128)(2,1)S(1)} %close.3), channel_id=1, source_target_pairs={{0,1},{1,0},{2,3},{3,2},{4,5},{5,4},{6,7},{7,6},{8,9},{9,8},{10,11... | collective-permute-start | bytes 786440 | tf_op jit(solution)/shard_map/ppermute | solution.py:363
  30.6 0.0 copy-start.2
  30.6 0.4 close.2.refs_0_
  31.0 0.0 copy-start.1
  31.0 0.6 %collective-permute-start.18 = (bf16[2,256,256]{2,1,0:T(8,128)(2,1)S(1)}, bf16[2,256,256]{2,1,0:T(8,128)(2,1)S(1)}, u32[]{:S(2)}, u32[]{:S(2)}) collective-permute-start(bf16[2,256,256]{2,1,0:T(8,128)(2,1)S(1)} %close.2.refs_0_), channel_id=1, source_target_pairs={{0,1},{1,0},{2,3},{3,2},{4,5},{5,4},{6,7},{7,6},{8,9},{9,8},{10,11... | collective-permute-start | bytes 786440 | tf_op jit(solution)/shard_map/ppermute | solution.py:364
  31.6 6.4 %collective-permute-done.15 = bf16[2,256,256]{2,1,0:T(8,128)(2,1)S(1)} collective-permute-done((bf16[2,256,256]{2,1,0:T(8,128)(2,1)S(1)}, bf16[2,256,256]{2,1,0:T(8,128)(2,1)S(1)}, u32[]{:S(2)}, u32[]{:S(2)}) %collective-permute-start.15) | collective-permute-done | bytes 262176 | tf_op jit(solution)/shard_map/ppermute | solution.py:363
  38.0 0.0 collective-permute-start.16
  38.0 0.5 %collective-permute-start.17 = (bf16[2,256,256]{2,1,0:T(8,128)(2,1)S(1)}, bf16[2,256,256]{2,1,0:T(8,128)(2,1)S(1)}, u32[]{:S(2)}, u32[]{:S(2)}) collective-permute-start(bf16[2,256,256]{2,1,0:T(8,128)(2,1)S(1)} %collective-permute-done.15), channel_id=1, source_target_pairs={{0,2},{2,0},{4,6},{6,4},{8,10},{10,8},{12,14},{14,12},{16,18},{18,... | collective-permute-start | bytes 786440 | tf_op jit(solution)/shard_map/ppermute | solution.py:367
  38.6 0.0 copy-done
  38.6 0.0 copy-done.3
  38.6 0.7 %fusion.base = f32[256,1024]{1,0:T(8,128)S(1)} fusion(bf16[256,1024]{1,0:T(8,128)(2,1)S(1)} %copy-done.3, bf16[1024,1024]{1,0:T(8,128)(2,1)S(1)} %copy-done), kind=kOutput, calls=%fused_computation | convolution fusion | flops 536870912 | bytes 3670016 | tf_op jit(solution)/shard_map/dot_general | solution.py:369
  39.3 0.3 collective-permute-done.16.refs_1_
  39.6 0.0 copy-done.2
  39.6 0.0 copy-done.1
  39.6 0.7 %project.2.base = f32[256,1024]{1,0:T(8,128)S(1)} custom-call(f32[256,1024]{1,0:T(8,128)S(1)} %fusion.base, bf16[1024,1024]{1,0:T(8,128)(2,1)S(1)} %copy-done.1, bf16[1024,1024]{1,0:T(8,128)(2,1)S(1)} %copy-done.2, bf16[2,256,256]{2,1,0:T(8,128)(2,1)S(1)} %close.2.refs_0_, bf16[2,256,256]{2,1,0:T(8,128)(2,1)S(1)} %collective-permute-done.16.refs_1_), custom_call_target="tpu_custom_call" | custom-call | flops 536870912 | tf_op jit(solution)/shard_map/project/pallas_call | solution.py:279
  40.3 0.0 collective-permute-done.17.refs_0_
  40.3 0.5 %project.3.base = f32[256,1024]{1,0:T(8,128)S(1)} custom-call(f32[256,1024]{1,0:T(8,128)S(1)} %project.2.base, bf16[1024,1024]{1,0:T(8,128)(2,1)S(1)} %copy-done.1, bf16[1024,1024]{1,0:T(8,128)(2,1)S(1)} %copy-done.2, bf16[2,256,256]{2,1,0:T(8,128)(2,1)S(1)} %collective-permute-done.17.refs_0_), custom_call_target="tpu_custom_call" | custom-call | flops 268435456 | tf_op jit(solution)/shard_map/project/pallas_call | solution.py:279
  40.8 0.1 collective-permute-done.18.part
  40.9 1.2 %finish.1 = bf16[256,1024]{1,0:T(8,128)(2,1)} custom-call(f32[256,1024]{1,0:T(8,128)S(1)} %project.3.base, bf16[1024,1024]{1,0:T(8,128)(2,1)S(1)} %copy-done.1, bf16[1024,1024]{1,0:T(8,128)(2,1)S(1)} %copy-done.2, bf16[2,256,256]{2,1,0:T(8,128)(2,1)S(1)} %collective-permute-done.18.part), custom_call_target="tpu_custom_call" | custom-call | flops 134217728 | tf_op jit(solution)/shard_map/finish/pallas_call | solution.py:313
Async XLA Ops:
  0.0 38.6 %copy-start = (bf16[1024,1024]{1,0:T(8,128)(2,1)S(1)}, bf16[1024,1024]{1,0:T(8,128)(2,1)}, u32[]{:S(2)}) copy-start(bf16[1024,1024]{1,0:T(8,128)(2,1)} %param.13) | copy-start | bytes 6291460
  1.8 22.3 %collective-permute-start = (bf16[53,128,128]{2,1,0:T(8,128)(2,1)S(1)}, bf16[53,128,128]{2,1,0:T(8,128)(2,1)S(1)}, u32[]{:S(2)}, u32[]{:S(2)}) collective-permute-start(bf16[53,128,128]{2,1,0:T(8,128)(2,1)S(1)} %get-tuple-element.10.refs_0_.bundle), channel_id=1, source_target_pairs={{0,2},{2,0},{4,6},{6,4},{8,10},{10,8},{12,14},{14,12},{16,18},{18,... | collective-permute-start | bytes 5210120 | tf_op jit(solution)/shard_map/ppermute | solution.py:335
  2.3 6.7 %collective-permute-start.10 = (bf16[256,256]{1,0:T(8,128)(2,1)S(1)}, bf16[256,256]{1,0:T(8,128)(2,1)S(1)}, u32[]{:S(2)}, u32[]{:S(2)}) collective-permute-start(bf16[256,256]{1,0:T(8,128)(2,1)S(1)} %get-tuple-element.12.refs_2_), channel_id=1, source_target_pairs={{0,4},{2,6},{4,12},{6,14},{8,0},{10,2},{12,20},{14,22},{16,8},{18,... | collective-permute-start | bytes 393224 | tf_op jit(solution)/shard_map/ppermute | solution.py:349
  4.9 6.3 %collective-permute-start.1 = (bf16[256,256]{1,0:T(8,128)(2,1)S(1)}, bf16[256,256]{1,0:T(8,128)(2,1)S(1)}, u32[]{:S(2)}, u32[]{:S(2)}) collective-permute-start(bf16[256,256]{1,0:T(8,128)(2,1)S(1)} %get-tuple-element.11), channel_id=1, source_target_pairs={{0,10},{2,8},{4,2},{6,0},{8,18},{10,16},{12,6},{14,4},{16,26},{18,... | collective-permute-start | bytes 393224 | tf_op jit(solution)/shard_map/ppermute | solution.py:343
  5.0 8.5 %collective-permute-start.7 = (bf16[256,256]{1,0:T(8,128)(2,1)S(1)}, bf16[256,256]{1,0:T(8,128)(2,1)S(1)}, u32[]{:S(2)}, u32[]{:S(2)}) collective-permute-start(bf16[256,256]{1,0:T(8,128)(2,1)S(1)} %get-tuple-element.12.refs_2_), channel_id=1, source_target_pairs={{0,8},{2,10},{4,0},{6,2},{8,16},{10,18},{12,4},{14,6},{16,24},{18,... | collective-permute-start | bytes 393224 | tf_op jit(solution)/shard_map/ppermute | solution.py:347
  6.8 6.9 %collective-permute-start.4 = (bf16[256,256]{1,0:T(8,128)(2,1)S(1)}, bf16[256,256]{1,0:T(8,128)(2,1)S(1)}, u32[]{:S(2)}, u32[]{:S(2)}) collective-permute-start(bf16[256,256]{1,0:T(8,128)(2,1)S(1)} %get-tuple-element.11), channel_id=1, source_target_pairs={{0,6},{2,4},{4,14},{6,12},{8,2},{10,0},{12,22},{14,20},{16,10},{18... | collective-permute-start | bytes 393224 | tf_op jit(solution)/shard_map/ppermute | solution.py:345
  9.1 6.5 %collective-permute-start.11 = (bf16[256,256]{1,0:T(8,128)(2,1)S(1)}, bf16[256,256]{1,0:T(8,128)(2,1)S(1)}, u32[]{:S(2)}, u32[]{:S(2)}) collective-permute-start(bf16[256,256]{1,0:T(8,128)(2,1)S(1)} %collective-permute-done.10.refs_6_), channel_id=1, source_target_pairs={{0,4},{2,6},{4,12},{6,14},{8,0},{10,2},{12,20},{14,22},{16,8},{18,... | collective-permute-start | bytes 393224 | tf_op jit(solution)/shard_map/ppermute | solution.py:349
  11.2 6.0 %collective-permute-start.2 = (bf16[256,256]{1,0:T(8,128)(2,1)S(1)}, bf16[256,256]{1,0:T(8,128)(2,1)S(1)}, u32[]{:S(2)}, u32[]{:S(2)}) collective-permute-start(bf16[256,256]{1,0:T(8,128)(2,1)S(1)} %collective-permute-done.1.refs_3_), channel_id=1, source_target_pairs={{0,8},{2,10},{4,0},{6,2},{8,16},{10,18},{12,4},{14,6},{16,24},{18,... | collective-permute-start | bytes 393224 | tf_op jit(solution)/shard_map/ppermute | solution.py:343
  13.5 6.5 %collective-permute-start.8 = (bf16[256,256]{1,0:T(8,128)(2,1)S(1)}, bf16[256,256]{1,0:T(8,128)(2,1)S(1)}, u32[]{:S(2)}, u32[]{:S(2)}) collective-permute-start(bf16[256,256]{1,0:T(8,128)(2,1)S(1)} %collective-permute-done.7.refs_5_), channel_id=1, source_target_pairs={{0,8},{2,10},{4,0},{6,2},{8,16},{10,18},{12,4},{14,6},{16,24},{18,... | collective-permute-start | bytes 393224 | tf_op jit(solution)/shard_map/ppermute | solution.py:347
  13.7 6.4 %collective-permute-start.5 = (bf16[256,256]{1,0:T(8,128)(2,1)S(1)}, bf16[256,256]{1,0:T(8,128)(2,1)S(1)}, u32[]{:S(2)}, u32[]{:S(2)}) collective-permute-start(bf16[256,256]{1,0:T(8,128)(2,1)S(1)} %collective-permute-done.4.refs_4_), channel_id=1, source_target_pairs={{0,4},{2,6},{4,12},{6,14},{8,0},{10,2},{12,20},{14,22},{16,8},{18,... | collective-permute-start | bytes 393224 | tf_op jit(solution)/shard_map/ppermute | solution.py:345
  15.6 6.5 %collective-permute-start.12 = (bf16[256,256]{1,0:T(8,128)(2,1)S(1)}, bf16[256,256]{1,0:T(8,128)(2,1)S(1)}, u32[]{:S(2)}, u32[]{:S(2)}) collective-permute-start(bf16[256,256]{1,0:T(8,128)(2,1)S(1)} %collective-permute-done.11.refs_10_), channel_id=1, source_target_pairs={{0,4},{2,6},{4,12},{6,14},{8,0},{10,2},{12,20},{14,22},{16,8},{18,... | collective-permute-start | bytes 393224 | tf_op jit(solution)/shard_map/ppermute | solution.py:349
  17.2 6.4 %collective-permute-start.3 = (bf16[256,256]{1,0:T(8,128)(2,1)S(1)}, bf16[256,256]{1,0:T(8,128)(2,1)S(1)}, u32[]{:S(2)}, u32[]{:S(2)}) collective-permute-start(bf16[256,256]{1,0:T(8,128)(2,1)S(1)} %collective-permute-done.2.refs_7_), channel_id=1, source_target_pairs={{0,8},{2,10},{4,0},{6,2},{8,16},{10,18},{12,4},{14,6},{16,24},{18,... | collective-permute-start | bytes 393224 | tf_op jit(solution)/shard_map/ppermute | solution.py:343
  20.1 5.9 %collective-permute-start.9 = (bf16[256,256]{1,0:T(8,128)(2,1)S(1)}, bf16[256,256]{1,0:T(8,128)(2,1)S(1)}, u32[]{:S(2)}, u32[]{:S(2)}) collective-permute-start(bf16[256,256]{1,0:T(8,128)(2,1)S(1)} %collective-permute-done.8.refs_9_), channel_id=1, source_target_pairs={{0,8},{2,10},{4,0},{6,2},{8,16},{10,18},{12,4},{14,6},{16,24},{18,... | collective-permute-start | bytes 393224 | tf_op jit(solution)/shard_map/ppermute | solution.py:347
  20.1 6.0 %collective-permute-start.6 = (bf16[256,256]{1,0:T(8,128)(2,1)S(1)}, bf16[256,256]{1,0:T(8,128)(2,1)S(1)}, u32[]{:S(2)}, u32[]{:S(2)}) collective-permute-start(bf16[256,256]{1,0:T(8,128)(2,1)S(1)} %collective-permute-done.5.refs_8_), channel_id=1, source_target_pairs={{0,4},{2,6},{4,12},{6,14},{8,0},{10,2},{12,20},{14,22},{16,8},{18,... | collective-permute-start | bytes 393224 | tf_op jit(solution)/shard_map/ppermute | solution.py:345
  22.1 5.4 %collective-permute-start.14 = (bf16[256,256]{1,0:T(8,128)(2,1)S(1)}, bf16[256,256]{1,0:T(8,128)(2,1)S(1)}, u32[]{:S(2)}, u32[]{:S(2)}) collective-permute-start(bf16[256,256]{1,0:T(8,128)(2,1)S(1)} %collective-permute-done.12.refs_5_), channel_id=1, source_target_pairs={{0,4},{2,6},{4,12},{6,14},{8,0},{10,2},{12,20},{14,22},{16,8},{18,... | collective-permute-start | bytes 393224 | tf_op jit(solution)/shard_map/ppermute | solution.py:354
  23.7 5.0 %collective-permute-start.13 = (bf16[256,256]{1,0:T(8,128)(2,1)S(1)}, bf16[256,256]{1,0:T(8,128)(2,1)S(1)}, u32[]{:S(2)}, u32[]{:S(2)}) collective-permute-start(bf16[256,256]{1,0:T(8,128)(2,1)S(1)} %collective-permute-done.3.refs_2_), channel_id=1, source_target_pairs={{0,8},{2,10},{4,0},{6,2},{8,16},{10,18},{12,4},{14,6},{16,24},{18,... | collective-permute-start | bytes 393224 | tf_op jit(solution)/shard_map/ppermute | solution.py:353
  29.0 9.5 %copy-start.3 = (bf16[256,1024]{1,0:T(8,128)(2,1)S(1)}, bf16[256,1024]{1,0:T(8,128)(2,1)}, u32[]{:S(2)}) copy-start(bf16[256,1024]{1,0:T(8,128)(2,1)} %features.1) | copy-start | bytes 1572868
  29.1 9.0 %collective-permute-start.15 = (bf16[2,256,256]{2,1,0:T(8,128)(2,1)S(1)}, bf16[2,256,256]{2,1,0:T(8,128)(2,1)S(1)}, u32[]{:S(2)}, u32[]{:S(2)}) collective-permute-start(bf16[2,256,256]{2,1,0:T(8,128)(2,1)S(1)} %close.3), channel_id=1, source_target_pairs={{0,1},{1,0},{2,3},{3,2},{4,5},{5,4},{6,7},{7,6},{8,9},{9,8},{10,11... | collective-permute-start | bytes 786440 | tf_op jit(solution)/shard_map/ppermute | solution.py:363
  30.6 9.0 %copy-start.2 = (bf16[1024,1024]{1,0:T(8,128)(2,1)S(1)}, bf16[1024,1024]{1,0:T(8,128)(2,1)}, u32[]{:S(2)}) copy-start(bf16[1024,1024]{1,0:T(8,128)(2,1)} %w_out.5) | copy-start | bytes 6291460
  31.0 8.6 %copy-start.1 = (bf16[1024,1024]{1,0:T(8,128)(2,1)S(1)}, bf16[1024,1024]{1,0:T(8,128)(2,1)}, u32[]{:S(2)}) copy-start(bf16[1024,1024]{1,0:T(8,128)(2,1)} %w_in.5) | copy-start | bytes 6291460
  31.0 9.8 %collective-permute-start.18 = (bf16[2,256,256]{2,1,0:T(8,128)(2,1)S(1)}, bf16[2,256,256]{2,1,0:T(8,128)(2,1)S(1)}, u32[]{:S(2)}, u32[]{:S(2)}) collective-permute-start(bf16[2,256,256]{2,1,0:T(8,128)(2,1)S(1)} %close.2.refs_0_), channel_id=1, source_target_pairs={{0,1},{1,0},{2,3},{3,2},{4,5},{5,4},{6,7},{7,6},{8,9},{9,8},{10,11... | collective-permute-start | bytes 786440 | tf_op jit(solution)/shard_map/ppermute | solution.py:364
  38.0 1.5 %collective-permute-start.16 = (bf16[2,256,256]{2,1,0:T(8,128)(2,1)S(1)}, bf16[2,256,256]{2,1,0:T(8,128)(2,1)S(1)}, u32[]{:S(2)}, u32[]{:S(2)}) collective-permute-start(bf16[2,256,256]{2,1,0:T(8,128)(2,1)S(1)} %close.3), channel_id=1, source_target_pairs={{0,2},{2,0},{4,6},{6,4},{8,10},{10,8},{12,14},{14,12},{16,18},{18,... | collective-permute-start | bytes 786440 | tf_op jit(solution)/shard_map/ppermute | solution.py:366
  38.0 2.3 %collective-permute-start.17 = (bf16[2,256,256]{2,1,0:T(8,128)(2,1)S(1)}, bf16[2,256,256]{2,1,0:T(8,128)(2,1)S(1)}, u32[]{:S(2)}, u32[]{:S(2)}) collective-permute-start(bf16[2,256,256]{2,1,0:T(8,128)(2,1)S(1)} %collective-permute-done.15), channel_id=1, source_target_pairs={{0,2},{2,0},{4,6},{6,4},{8,10},{10,8},{12,14},{14,12},{16,18},{18,... | collective-permute-start | bytes 786440 | tf_op jit(solution)/shard_map/ppermute | solution.py:367

commit v6 on v5

--- a/solution.py
+++ b/solution.py
@@ -353,9 +353,8 @@
         (lax.ppermute(forward[1], "dom", ahead), chips // 2, 1),
         (lax.ppermute(backward[0], "dom", behind), chips // 2, 0),
     ]
-    early = [(mine, 0, 0)] + [piece for found in steps[:-1] for piece in found]
+    early = [(mine, 0, 0)] + [piece for found in steps for piece in found]
     sums = absorb(bundles, shape, early, None, chips)
-    sums = absorb(bundles, shape, steps[-1], sums, chips)
     (other,) = close(bundles[1], shape, last, sums, 1, chips, 1)
     owns = close(bundles[0], shape, last, sums, 0, chips, 1)
 
@@ -367,8 +366,8 @@
     diagonal = lax.ppermute(passing, "dom", cores)
 
     hidden = jnp.dot(features, w_self, preferred_element_type=F32)
-    hidden = project(hidden, [owns, [core_side]], ((0, 0), (0, 1)), w_in, w_out)
-    hidden = project(hidden, [[diagonal]], ((1, 1),), w_in, w_out)
+    hidden = project(hidden, [owns], ((0, 0),), w_in, w_out)
+    hidden = project(hidden, [[core_side], [diagonal]], ((0, 1), (1, 1)), w_in, w_out)
     out = None
     for band, twin in enumerate(twins):
         out = finish(hidden, twin, (1, 0), w_in, w_out, band, out)

time: 42.2 us -> 42.2 us (level)
    ppermute x3, waiting for transfers between devices: 4.92 us -> 6.57 us  [on_device(): forward[0] = lax.ppermute(forward[0], 'dom', ahead)]
    ppermute x1, waiting for transfers between devices: 1.13 us -> 0.25 us  [on_device(): lax.ppermute(forward[1], 'dom', ahead)]
    ppermute x1, waiting for transfers between devices: 0.58 us -> 0.01 us  [on_device(): lax.ppermute(backward[0], 'dom', behind)]
    pallas_call x2 -> x1, Pallas kernels: 2.46 us -> 2.26 us  [absorb(): pl.pallas_call(functools.partial(absorb_body, origins, local, slots, chip...]
  transfers between devices with their start and end apart: 19 -> 19, of which waited for: 11 -> 10; matrix products, arithmetic and copies ran while one was open for 2% -> 2% of each run, Pallas kernels for 10% -> 9%
where the time goes in v6:
time: 42.2 us; the launch traced here: 42.1 us
  starting transfers between devices  17.8 us (42%)
  waiting for transfers between devices  16.2 us (38%)
  Pallas kernels  7.26 us (17%)
  matrix products  0.7 us (2%)
    ppermute x3, waiting for transfers between devices, on_device(): forward[0] = lax.ppermute(forward[0], 'dom', ahead)  6.57 us
    ppermute x1, waiting for transfers between devices, on_device(): passing = lax.ppermute(other, 'rep', facing)  6.41 us
    ppermute x3, starting transfers between devices, on_device(): backward[0] = lax.ppermute(backward[0], 'dom', behind)  6.29 us
    ppermute x3, starting transfers between devices, on_device(): lax.ppermute(backward[1], 'dom', swapped(behind) if step == 1 else behind)  3.91 us
    ppermute x3, waiting for transfers between devices, on_device(): backward[0] = lax.ppermute(backward[0], 'dom', behind)  2.31 us
    pallas_call x1, Pallas kernels, absorb(): pl.pallas_call(functools.partial(absorb_body, origins, local, slots, chip...  2.26 us
    ppermute x3, starting transfers between devices, on_device(): forward[0] = lax.ppermute(forward[0], 'dom', ahead)  1.89 us
    pallas_call x1, Pallas kernels, pack(): pl.pallas_call(functools.partial(pack_body, devices // 2, local), out_sha...  1.81 us
  transfers between devices with their start and end apart: 19, of which 10 were waited for; matrix products, arithmetic and copies ran while one was open for 2% of the time, Pallas kernels for 9%

profile of v6, /device:TPU:0, one launch (start us, length us, event | category | flops | bytes accessed | tf_op | source)
XLA Modules:
  0.0 42.1 jit_solution(3750679074528003689)
XLA Ops:
  0.0 0.0 copy-start
  0.0 1.8 %pack.1 = (bf16[256,256]{1,0:T(8,128)(2,1)S(1)}, bf16[256,256]{1,0:T(8,128)(2,1)S(1)}, bf16[53,128,128]{2,1,0:T(8,128)(2,1)S(1)}) custom-call(bf16[256,1024]{1,0:T(8,128)(2,1)} %features.1, bf16[2,128,1024]{2,1,0:T(8,128)(2,1)} %bitcast.4, bf16[48,128,128]{2,1,0:T(8,128)(2,1)} %bitcast.5, s32[2,2,12]{2,1,0:T(2,128)} %columns_in.1, s32[2,2]{1,0:T(2,128)} %counts_in.1, ...), custom_call_target="tpu_custom_call" | custom-call | tf_op jit(solution)/shard_map/pack/pallas_call | solution.py:136
  1.8 0.5 %collective-permute-start = (bf16[53,128,128]{2,1,0:T(8,128)(2,1)S(1)}, bf16[53,128,128]{2,1,0:T(8,128)(2,1)S(1)}, u32[]{:S(2)}, u32[]{:S(2)}) collective-permute-start(bf16[53,128,128]{2,1,0:T(8,128)(2,1)S(1)} %get-tuple-element.10.refs_0_.bundle), channel_id=1, source_target_pairs={{0,2},{2,0},{4,6},{6,4},{8,10},{10,8},{12,14},{14,12},{16,18},{18,... | collective-permute-start | bytes 5210120 | tf_op jit(solution)/shard_map/ppermute | solution.py:335
  2.3 2.6 %collective-permute-start.4 = (bf16[256,256]{1,0:T(8,128)(2,1)S(1)}, bf16[256,256]{1,0:T(8,128)(2,1)S(1)}, u32[]{:S(2)}, u32[]{:S(2)}) collective-permute-start(bf16[256,256]{1,0:T(8,128)(2,1)S(1)} %get-tuple-element.11.refs_2_), channel_id=1, source_target_pairs={{0,4},{2,6},{4,12},{6,14},{8,0},{10,2},{12,20},{14,22},{16,8},{18,... | collective-permute-start | bytes 393224 | tf_op jit(solution)/shard_map/ppermute | solution.py:349
  4.9 0.1 collective-permute-start.1
  5.0 1.7 %collective-permute-start.3 = (bf16[256,256]{1,0:T(8,128)(2,1)S(1)}, bf16[256,256]{1,0:T(8,128)(2,1)S(1)}, u32[]{:S(2)}, u32[]{:S(2)}) collective-permute-start(bf16[256,256]{1,0:T(8,128)(2,1)S(1)} %get-tuple-element.11.refs_2_), channel_id=1, source_target_pairs={{0,8},{2,10},{4,0},{6,2},{8,16},{10,18},{12,4},{14,6},{16,24},{18,... | collective-permute-start | bytes 393224 | tf_op jit(solution)/shard_map/ppermute | solution.py:347
  6.8 0.0 collective-permute-start.2
  6.8 2.3 %collective-permute-done.4.refs_6_ = bf16[256,256]{1,0:T(8,128)(2,1)S(1)} collective-permute-done((bf16[256,256]{1,0:T(8,128)(2,1)S(1)}, bf16[256,256]{1,0:T(8,128)(2,1)S(1)}, u32[]{:S(2)}, u32[]{:S(2)}) %collective-permute-start.4) | collective-permute-done | bytes 131104 | tf_op jit(solution)/shard_map/ppermute | solution.py:349
  9.1 2.1 %collective-permute-start.8 = (bf16[256,256]{1,0:T(8,128)(2,1)S(1)}, bf16[256,256]{1,0:T(8,128)(2,1)S(1)}, u32[]{:S(2)}, u32[]{:S(2)}) collective-permute-start(bf16[256,256]{1,0:T(8,128)(2,1)S(1)} %collective-permute-done.4.refs_6_), channel_id=1, source_target_pairs={{0,4},{2,6},{4,12},{6,14},{8,0},{10,2},{12,20},{14,22},{16,8},{18,... | collective-permute-start | bytes 393224 | tf_op jit(solution)/shard_map/ppermute | solution.py:349
  11.2 0.0 collective-permute-done.1.refs_3_
  11.2 0.0 collective-permute-start.5
  11.2 2.3 %collective-permute-done.3.refs_5_ = bf16[256,256]{1,0:T(8,128)(2,1)S(1)} collective-permute-done((bf16[256,256]{1,0:T(8,128)(2,1)S(1)}, bf16[256,256]{1,0:T(8,128)(2,1)S(1)}, u32[]{:S(2)}, u32[]{:S(2)}) %collective-permute-start.3) | collective-permute-done | bytes 131104 | tf_op jit(solution)/shard_map/ppermute | solution.py:347
  13.5 0.1 collective-permute-start.7
  13.7 0.0 collective-permute-done.2.refs_4_
  13.7 1.9 %collective-permute-start.6 = (bf16[256,256]{1,0:T(8,128)(2,1)S(1)}, bf16[256,256]{1,0:T(8,128)(2,1)S(1)}, u32[]{:S(2)}, u32[]{:S(2)}) collective-permute-start(bf16[256,256]{1,0:T(8,128)(2,1)S(1)} %collective-permute-done.2.refs_4_), channel_id=1, source_target_pairs={{0,4},{2,6},{4,12},{6,14},{8,0},{10,2},{12,20},{14,22},{16,8},{18,... | collective-permute-start | bytes 393224 | tf_op jit(solution)/shard_map/ppermute | solution.py:345
  15.6 0.0 collective-permute-done.8.refs_10_
  15.6 1.6 %collective-permute-start.12 = (bf16[256,256]{1,0:T(8,128)(2,1)S(1)}, bf16[256,256]{1,0:T(8,128)(2,1)S(1)}, u32[]{:S(2)}, u32[]{:S(2)}) collective-permute-start(bf16[256,256]{1,0:T(8,128)(2,1)S(1)} %collective-permute-done.8.refs_10_), channel_id=1, source_target_pairs={{0,4},{2,6},{4,12},{6,14},{8,0},{10,2},{12,20},{14,22},{16,8},{18,... | collective-permute-start | bytes 393224 | tf_op jit(solution)/shard_map/ppermute | solution.py:349
  17.1 0.1 collective-permute-done.5.refs_7_
  17.2 0.3 collective-permute-start.9
  17.6 2.5 %collective-permute-done.7.refs_9_ = bf16[256,256]{1,0:T(8,128)(2,1)S(1)} collective-permute-done((bf16[256,256]{1,0:T(8,128)(2,1)S(1)}, bf16[256,256]{1,0:T(8,128)(2,1)S(1)}, u32[]{:S(2)}, u32[]{:S(2)}) %collective-permute-start.7) | collective-permute-done | bytes 131104 | tf_op jit(solution)/shard_map/ppermute | solution.py:347
  20.1 0.0 collective-permute-start.11
  20.1 0.0 collective-permute-done.6.refs_8_
  20.1 2.0 %collective-permute-start.10 = (bf16[256,256]{1,0:T(8,128)(2,1)S(1)}, bf16[256,256]{1,0:T(8,128)(2,1)S(1)}, u32[]{:S(2)}, u32[]{:S(2)}) collective-permute-start(bf16[256,256]{1,0:T(8,128)(2,1)S(1)} %collective-permute-done.6.refs_8_), channel_id=1, source_target_pairs={{0,4},{2,6},{4,12},{6,14},{8,0},{10,2},{12,20},{14,22},{16,8},{18,... | collective-permute-start | bytes 393224 | tf_op jit(solution)/shard_map/ppermute | solution.py:345
  22.1 0.0 collective-permute-done.12.refs_14_
  22.1 1.6 %collective-permute-start.14 = (bf16[256,256]{1,0:T(8,128)(2,1)S(1)}, bf16[256,256]{1,0:T(8,128)(2,1)S(1)}, u32[]{:S(2)}, u32[]{:S(2)}) collective-permute-start(bf16[256,256]{1,0:T(8,128)(2,1)S(1)} %collective-permute-done.12.refs_14_), channel_id=1, source_target_pairs={{0,4},{2,6},{4,12},{6,14},{8,0},{10,2},{12,20},{14,22},{16,8},{18,... | collective-permute-start | bytes 393224 | tf_op jit(solution)/shard_map/ppermute | solution.py:354
  23.7 0.0 collective-permute-done.9.refs_11_
  23.7 0.5 %collective-permute-start.13 = (bf16[256,256]{1,0:T(8,128)(2,1)S(1)}, bf16[256,256]{1,0:T(8,128)(2,1)S(1)}, u32[]{:S(2)}, u32[]{:S(2)}) collective-permute-start(bf16[256,256]{1,0:T(8,128)(2,1)S(1)} %collective-permute-done.9.refs_11_), channel_id=1, source_target_pairs={{0,8},{2,10},{4,0},{6,2},{8,16},{10,18},{12,4},{14,6},{16,24},{18,... | collective-permute-start | bytes 393224 | tf_op jit(solution)/shard_map/ppermute | solution.py:353
  24.1 1.8 %collective-permute-done.11.refs_13_ = bf16[256,256]{1,0:T(8,128)(2,1)S(1)} collective-permute-done((bf16[256,256]{1,0:T(8,128)(2,1)S(1)}, bf16[256,256]{1,0:T(8,128)(2,1)S(1)}, u32[]{:S(2)}, u32[]{:S(2)}) %collective-permute-start.11) | collective-permute-done | bytes 131104 | tf_op jit(solution)/shard_map/ppermute | solution.py:347
  25.9 0.2 collective-permute-done.10.refs_12_
  26.1 0.0 collective-permute-done.refs_1_.bundle
  26.1 2.3 %absorb.1.sums = f32[2,2,256,256]{3,2,1,0:T(8,128)S(1)} custom-call(bf16[53,128,128]{2,1,0:T(8,128)(2,1)S(1)} %get-tuple-element.10.refs_0_.bundle, bf16[53,128,128]{2,1,0:T(8,128)(2,1)S(1)} %collective-permute-done.refs_1_.bundle, bf16[256,256]{1,0:T(8,128)(2,1)S(1)} %get-tuple-element.11.refs_2_, bf16[256,256]{1,0:T(8,128)(2,1)S(1)} %collective-permute-done.1.refs_3_, ...), custom_call_target="tpu_custom_call" | custom-call | flops 1744830464 | tf_op jit(solution)/shard_map/absorb/pallas_call | solution.py:211
  28.4 0.0 collective-permute-done.14.refs_1_
  28.4 0.2 collective-permute-done.13.refs_0_
  28.6 0.4 close.3
  29.0 0.0 copy-start.3
  29.1 1.6 %collective-permute-start.15 = (bf16[2,256,256]{2,1,0:T(8,128)(2,1)S(1)}, bf16[2,256,256]{2,1,0:T(8,128)(2,1)S(1)}, u32[]{:S(2)}, u32[]{:S(2)}) collective-permute-start(bf16[2,256,256]{2,1,0:T(8,128)(2,1)S(1)} %close.3), channel_id=1, source_target_pairs={{0,1},{1,0},{2,3},{3,2},{4,5},{5,4},{6,7},{7,6},{8,9},{9,8},{10,11... | collective-permute-start | bytes 786440 | tf_op jit(solution)/shard_map/ppermute | solution.py:362
  30.6 0.0 copy-start.2
  30.6 0.4 close.2.refs_0_
  31.0 0.0 copy-start.1
  31.0 0.6 %collective-permute-start.18 = (bf16[2,256,256]{2,1,0:T(8,128)(2,1)S(1)}, bf16[2,256,256]{2,1,0:T(8,128)(2,1)S(1)}, u32[]{:S(2)}, u32[]{:S(2)}) collective-permute-start(bf16[2,256,256]{2,1,0:T(8,128)(2,1)S(1)} %close.2.refs_0_), channel_id=1, source_target_pairs={{0,1},{1,0},{2,3},{3,2},{4,5},{5,4},{6,7},{7,6},{8,9},{9,8},{10,11... | collective-permute-start | bytes 786440 | tf_op jit(solution)/shard_map/ppermute | solution.py:363
  31.6 6.4 %collective-permute-done.15 = bf16[2,256,256]{2,1,0:T(8,128)(2,1)S(1)} collective-permute-done((bf16[2,256,256]{2,1,0:T(8,128)(2,1)S(1)}, bf16[2,256,256]{2,1,0:T(8,128)(2,1)S(1)}, u32[]{:S(2)}, u32[]{:S(2)}) %collective-permute-start.15) | collective-permute-done | bytes 262176 | tf_op jit(solution)/shard_map/ppermute | solution.py:362
  38.0 0.0 collective-permute-start.16
  38.0 0.5 %collective-permute-start.17 = (bf16[2,256,256]{2,1,0:T(8,128)(2,1)S(1)}, bf16[2,256,256]{2,1,0:T(8,128)(2,1)S(1)}, u32[]{:S(2)}, u32[]{:S(2)}) collective-permute-start(bf16[2,256,256]{2,1,0:T(8,128)(2,1)S(1)} %collective-permute-done.15), channel_id=1, source_target_pairs={{0,2},{2,0},{4,6},{6,4},{8,10},{10,8},{12,14},{14,12},{16,18},{18,... | collective-permute-start | bytes 786440 | tf_op jit(solution)/shard_map/ppermute | solution.py:366
  38.6 0.0 copy-done
  38.6 0.0 copy-done.3
  38.6 0.7 %fusion.base = f32[256,1024]{1,0:T(8,128)S(1)} fusion(bf16[256,1024]{1,0:T(8,128)(2,1)S(1)} %copy-done.3, bf16[1024,1024]{1,0:T(8,128)(2,1)S(1)} %copy-done), kind=kOutput, calls=%fused_computation | convolution fusion | flops 536870912 | bytes 3670016 | tf_op jit(solution)/shard_map/dot_general | solution.py:368
  39.3 0.0 copy-done.2
  39.3 0.0 copy-done.1
  39.3 0.5 %project.2.base = f32[256,1024]{1,0:T(8,128)S(1)} custom-call(f32[256,1024]{1,0:T(8,128)S(1)} %fusion.base, bf16[1024,1024]{1,0:T(8,128)(2,1)S(1)} %copy-done.1, bf16[1024,1024]{1,0:T(8,128)(2,1)S(1)} %copy-done.2, bf16[2,256,256]{2,1,0:T(8,128)(2,1)S(1)} %close.2.refs_0_), custom_call_target="tpu_custom_call" | custom-call | flops 268435456 | tf_op jit(solution)/shard_map/project/pallas_call | solution.py:279
  39.7 0.0 collective-permute-done.16.refs_0_
  39.8 0.2 collective-permute-done.17.refs_1_
  40.0 0.7 %project.3.base = f32[256,1024]{1,0:T(8,128)S(1)} custom-call(f32[256,1024]{1,0:T(8,128)S(1)} %project.2.base, bf16[1024,1024]{1,0:T(8,128)(2,1)S(1)} %copy-done.1, bf16[1024,1024]{1,0:T(8,128)(2,1)S(1)} %copy-done.2, bf16[2,256,256]{2,1,0:T(8,128)(2,1)S(1)} %collective-permute-done.16.refs_0_, bf16[2,256,256]{2,1,0:T(8,128)(2,1)S(1)} %collective-permute-done.17.refs_1_), custom_call_target="tpu_custom_call" | custom-call | flops 536870912 | tf_op jit(solution)/shard_map/project/pallas_call | solution.py:279
  40.7 0.2 collective-permute-done.18.part
  40.9 1.2 %finish.1 = bf16[256,1024]{1,0:T(8,128)(2,1)} custom-call(f32[256,1024]{1,0:T(8,128)S(1)} %project.3.base, bf16[1024,1024]{1,0:T(8,128)(2,1)S(1)} %copy-done.1, bf16[1024,1024]{1,0:T(8,128)(2,1)S(1)} %copy-done.2, bf16[2,256,256]{2,1,0:T(8,128)(2,1)S(1)} %collective-permute-done.18.part), custom_call_target="tpu_custom_call" | custom-call | flops 134217728 | tf_op jit(solution)/shard_map/finish/pallas_call | solution.py:313
Async XLA Ops:
  0.0 38.6 %copy-start = (bf16[1024,1024]{1,0:T(8,128)(2,1)S(1)}, bf16[1024,1024]{1,0:T(8,128)(2,1)}, u32[]{:S(2)}) copy-start(bf16[1024,1024]{1,0:T(8,128)(2,1)} %param.13) | copy-start | bytes 6291460
  1.8 24.3 %collective-permute-start = (bf16[53,128,128]{2,1,0:T(8,128)(2,1)S(1)}, bf16[53,128,128]{2,1,0:T(8,128)(2,1)S(1)}, u32[]{:S(2)}, u32[]{:S(2)}) collective-permute-start(bf16[53,128,128]{2,1,0:T(8,128)(2,1)S(1)} %get-tuple-element.10.refs_0_.bundle), channel_id=1, source_target_pairs={{0,2},{2,0},{4,6},{6,4},{8,10},{10,8},{12,14},{14,12},{16,18},{18,... | collective-permute-start | bytes 5210120 | tf_op jit(solution)/shard_map/ppermute | solution.py:335
  2.3 6.7 %collective-permute-start.4 = (bf16[256,256]{1,0:T(8,128)(2,1)S(1)}, bf16[256,256]{1,0:T(8,128)(2,1)S(1)}, u32[]{:S(2)}, u32[]{:S(2)}) collective-permute-start(bf16[256,256]{1,0:T(8,128)(2,1)S(1)} %get-tuple-element.11.refs_2_), channel_id=1, source_target_pairs={{0,4},{2,6},{4,12},{6,14},{8,0},{10,2},{12,20},{14,22},{16,8},{18,... | collective-permute-start | bytes 393224 | tf_op jit(solution)/shard_map/ppermute | solution.py:349
  4.9 6.3 %collective-permute-start.1 = (bf16[256,256]{1,0:T(8,128)(2,1)S(1)}, bf16[256,256]{1,0:T(8,128)(2,1)S(1)}, u32[]{:S(2)}, u32[]{:S(2)}) collective-permute-start(bf16[256,256]{1,0:T(8,128)(2,1)S(1)} %get-tuple-element.12), channel_id=1, source_target_pairs={{0,10},{2,8},{4,2},{6,0},{8,18},{10,16},{12,6},{14,4},{16,26},{18,... | collective-permute-start | bytes 393224 | tf_op jit(solution)/shard_map/ppermute | solution.py:343
  5.0 8.5 %collective-permute-start.3 = (bf16[256,256]{1,0:T(8,128)(2,1)S(1)}, bf16[256,256]{1,0:T(8,128)(2,1)S(1)}, u32[]{:S(2)}, u32[]{:S(2)}) collective-permute-start(bf16[256,256]{1,0:T(8,128)(2,1)S(1)} %get-tuple-element.11.refs_2_), channel_id=1, source_target_pairs={{0,8},{2,10},{4,0},{6,2},{8,16},{10,18},{12,4},{14,6},{16,24},{18,... | collective-permute-start | bytes 393224 | tf_op jit(solution)/shard_map/ppermute | solution.py:347
  6.8 6.9 %collective-permute-start.2 = (bf16[256,256]{1,0:T(8,128)(2,1)S(1)}, bf16[256,256]{1,0:T(8,128)(2,1)S(1)}, u32[]{:S(2)}, u32[]{:S(2)}) collective-permute-start(bf16[256,256]{1,0:T(8,128)(2,1)S(1)} %get-tuple-element.12), channel_id=1, source_target_pairs={{0,6},{2,4},{4,14},{6,12},{8,2},{10,0},{12,22},{14,20},{16,10},{18... | collective-permute-start | bytes 393224 | tf_op jit(solution)/shard_map/ppermute | solution.py:345
  9.1 6.5 %collective-permute-start.8 = (bf16[256,256]{1,0:T(8,128)(2,1)S(1)}, bf16[256,256]{1,0:T(8,128)(2,1)S(1)}, u32[]{:S(2)}, u32[]{:S(2)}) collective-permute-start(bf16[256,256]{1,0:T(8,128)(2,1)S(1)} %collective-permute-done.4.refs_6_), channel_id=1, source_target_pairs={{0,4},{2,6},{4,12},{6,14},{8,0},{10,2},{12,20},{14,22},{16,8},{18,... | collective-permute-start | bytes 393224 | tf_op jit(solution)/shard_map/ppermute | solution.py:349
  11.2 6.0 %collective-permute-start.5 = (bf16[256,256]{1,0:T(8,128)(2,1)S(1)}, bf16[256,256]{1,0:T(8,128)(2,1)S(1)}, u32[]{:S(2)}, u32[]{:S(2)}) collective-permute-start(bf16[256,256]{1,0:T(8,128)(2,1)S(1)} %collective-permute-done.1.refs_3_), channel_id=1, source_target_pairs={{0,8},{2,10},{4,0},{6,2},{8,16},{10,18},{12,4},{14,6},{16,24},{18,... | collective-permute-start | bytes 393224 | tf_op jit(solution)/shard_map/ppermute | solution.py:343
  13.5 6.5 %collective-permute-start.7 = (bf16[256,256]{1,0:T(8,128)(2,1)S(1)}, bf16[256,256]{1,0:T(8,128)(2,1)S(1)}, u32[]{:S(2)}, u32[]{:S(2)}) collective-permute-start(bf16[256,256]{1,0:T(8,128)(2,1)S(1)} %collective-permute-done.3.refs_5_), channel_id=1, source_target_pairs={{0,8},{2,10},{4,0},{6,2},{8,16},{10,18},{12,4},{14,6},{16,24},{18,... | collective-permute-start | bytes 393224 | tf_op jit(solution)/shard_map/ppermute | solution.py:347
  13.7 6.4 %collective-permute-start.6 = (bf16[256,256]{1,0:T(8,128)(2,1)S(1)}, bf16[256,256]{1,0:T(8,128)(2,1)S(1)}, u32[]{:S(2)}, u32[]{:S(2)}) collective-permute-start(bf16[256,256]{1,0:T(8,128)(2,1)S(1)} %collective-permute-done.2.refs_4_), channel_id=1, source_target_pairs={{0,4},{2,6},{4,12},{6,14},{8,0},{10,2},{12,20},{14,22},{16,8},{18,... | collective-permute-start | bytes 393224 | tf_op jit(solution)/shard_map/ppermute | solution.py:345
  15.6 6.5 %collective-permute-start.12 = (bf16[256,256]{1,0:T(8,128)(2,1)S(1)}, bf16[256,256]{1,0:T(8,128)(2,1)S(1)}, u32[]{:S(2)}, u32[]{:S(2)}) collective-permute-start(bf16[256,256]{1,0:T(8,128)(2,1)S(1)} %collective-permute-done.8.refs_10_), channel_id=1, source_target_pairs={{0,4},{2,6},{4,12},{6,14},{8,0},{10,2},{12,20},{14,22},{16,8},{18,... | collective-permute-start | bytes 393224 | tf_op jit(solution)/shard_map/ppermute | solution.py:349
  17.2 6.4 %collective-permute-start.9 = (bf16[256,256]{1,0:T(8,128)(2,1)S(1)}, bf16[256,256]{1,0:T(8,128)(2,1)S(1)}, u32[]{:S(2)}, u32[]{:S(2)}) collective-permute-start(bf16[256,256]{1,0:T(8,128)(2,1)S(1)} %collective-permute-done.5.refs_7_), channel_id=1, source_target_pairs={{0,8},{2,10},{4,0},{6,2},{8,16},{10,18},{12,4},{14,6},{16,24},{18,... | collective-permute-start | bytes 393224 | tf_op jit(solution)/shard_map/ppermute | solution.py:343
  20.1 5.9 %collective-permute-start.11 = (bf16[256,256]{1,0:T(8,128)(2,1)S(1)}, bf16[256,256]{1,0:T(8,128)(2,1)S(1)}, u32[]{:S(2)}, u32[]{:S(2)}) collective-permute-start(bf16[256,256]{1,0:T(8,128)(2,1)S(1)} %collective-permute-done.7.refs_9_), channel_id=1, source_target_pairs={{0,8},{2,10},{4,0},{6,2},{8,16},{10,18},{12,4},{14,6},{16,24},{18,... | collective-permute-start | bytes 393224 | tf_op jit(solution)/shard_map/ppermute | solution.py:347
  20.1 6.0 %collective-permute-start.10 = (bf16[256,256]{1,0:T(8,128)(2,1)S(1)}, bf16[256,256]{1,0:T(8,128)(2,1)S(1)}, u32[]{:S(2)}, u32[]{:S(2)}) collective-permute-start(bf16[256,256]{1,0:T(8,128)(2,1)S(1)} %collective-permute-done.6.refs_8_), channel_id=1, source_target_pairs={{0,4},{2,6},{4,12},{6,14},{8,0},{10,2},{12,20},{14,22},{16,8},{18,... | collective-permute-start | bytes 393224 | tf_op jit(solution)/shard_map/ppermute | solution.py:345
  22.1 6.3 %collective-permute-start.14 = (bf16[256,256]{1,0:T(8,128)(2,1)S(1)}, bf16[256,256]{1,0:T(8,128)(2,1)S(1)}, u32[]{:S(2)}, u32[]{:S(2)}) collective-permute-start(bf16[256,256]{1,0:T(8,128)(2,1)S(1)} %collective-permute-done.12.refs_14_), channel_id=1, source_target_pairs={{0,4},{2,6},{4,12},{6,14},{8,0},{10,2},{12,20},{14,22},{16,8},{18,... | collective-permute-start | bytes 393224 | tf_op jit(solution)/shard_map/ppermute | solution.py:354
  23.7 5.0 %collective-permute-start.13 = (bf16[256,256]{1,0:T(8,128)(2,1)S(1)}, bf16[256,256]{1,0:T(8,128)(2,1)S(1)}, u32[]{:S(2)}, u32[]{:S(2)}) collective-permute-start(bf16[256,256]{1,0:T(8,128)(2,1)S(1)} %collective-permute-done.9.refs_11_), channel_id=1, source_target_pairs={{0,8},{2,10},{4,0},{6,2},{8,16},{10,18},{12,4},{14,6},{16,24},{18,... | collective-permute-start | bytes 393224 | tf_op jit(solution)/shard_map/ppermute | solution.py:353
  29.0 9.5 %copy-start.3 = (bf16[256,1024]{1,0:T(8,128)(2,1)S(1)}, bf16[256,1024]{1,0:T(8,128)(2,1)}, u32[]{:S(2)}) copy-start(bf16[256,1024]{1,0:T(8,128)(2,1)} %features.1) | copy-start | bytes 1572868
  29.1 9.0 %collective-permute-start.15 = (bf16[2,256,256]{2,1,0:T(8,128)(2,1)S(1)}, bf16[2,256,256]{2,1,0:T(8,128)(2,1)S(1)}, u32[]{:S(2)}, u32[]{:S(2)}) collective-permute-start(bf16[2,256,256]{2,1,0:T(8,128)(2,1)S(1)} %close.3), channel_id=1, source_target_pairs={{0,1},{1,0},{2,3},{3,2},{4,5},{5,4},{6,7},{7,6},{8,9},{9,8},{10,11... | collective-permute-start | bytes 786440 | tf_op jit(solution)/shard_map/ppermute | solution.py:362
  30.6 8.7 %copy-start.2 = (bf16[1024,1024]{1,0:T(8,128)(2,1)S(1)}, bf16[1024,1024]{1,0:T(8,128)(2,1)}, u32[]{:S(2)}) copy-start(bf16[1024,1024]{1,0:T(8,128)(2,1)} %w_out.5) | copy-start | bytes 6291460
  31.0 8.3 %copy-start.1 = (bf16[1024,1024]{1,0:T(8,128)(2,1)S(1)}, bf16[1024,1024]{1,0:T(8,128)(2,1)}, u32[]{:S(2)}) copy-start(bf16[1024,1024]{1,0:T(8,128)(2,1)} %w_in.5) | copy-start | bytes 6291460
  31.0 9.8 %collective-permute-start.18 = (bf16[2,256,256]{2,1,0:T(8,128)(2,1)S(1)}, bf16[2,256,256]{2,1,0:T(8,128)(2,1)S(1)}, u32[]{:S(2)}, u32[]{:S(2)}) collective-permute-start(bf16[2,256,256]{2,1,0:T(8,128)(2,1)S(1)} %close.2.refs_0_), channel_id=1, source_target_pairs={{0,1},{1,0},{2,3},{3,2},{4,5},{5,4},{6,7},{7,6},{8,9},{9,8},{10,11... | collective-permute-start | bytes 786440 | tf_op jit(solution)/shard_map/ppermute | solution.py:363
  38.0 1.7 %collective-permute-start.16 = (bf16[2,256,256]{2,1,0:T(8,128)(2,1)S(1)}, bf16[2,256,256]{2,1,0:T(8,128)(2,1)S(1)}, u32[]{:S(2)}, u32[]{:S(2)}) collective-permute-start(bf16[2,256,256]{2,1,0:T(8,128)(2,1)S(1)} %close.3), channel_id=1, source_target_pairs={{0,2},{2,0},{4,6},{6,4},{8,10},{10,8},{12,14},{14,12},{16,18},{18,... | collective-permute-start | bytes 786440 | tf_op jit(solution)/shard_map/ppermute | solution.py:365
  38.0 1.9 %collective-permute-start.17 = (bf16[2,256,256]{2,1,0:T(8,128)(2,1)S(1)}, bf16[2,256,256]{2,1,0:T(8,128)(2,1)S(1)}, u32[]{:S(2)}, u32[]{:S(2)}) collective-permute-start(bf16[2,256,256]{2,1,0:T(8,128)(2,1)S(1)} %collective-permute-done.15), channel_id=1, source_target_pairs={{0,2},{2,0},{4,6},{6,4},{8,10},{10,8},{12,14},{14,12},{16,18},{18,... | collective-permute-start | bytes 786440 | tf_op jit(solution)/shard_map/ppermute | solution.py:366

commit v7 on v6

--- a/solution.py
+++ b/solution.py
@@ -340,18 +340,18 @@
     steps = []
     for step in range(1, (chips - 1) // 2 + 1):
         found = []
+        forward[0] = lax.ppermute(forward[0], "dom", ahead)
+        found.append((forward[0], -step, 0))
+        backward[0] = lax.ppermute(backward[0], "dom", behind)
+        found.append((backward[0], step, 0))
         forward[1] = lax.ppermute(forward[1], "dom", swapped(ahead) if step == 1 else ahead)
         found.append((forward[1], -step, 1))
         backward[1] = lax.ppermute(backward[1], "dom", swapped(behind) if step == 1 else behind)
         found.append((backward[1], step, 1))
-        forward[0] = lax.ppermute(forward[0], "dom", ahead)
-        found.append((forward[0], -step, 0))
-        backward[0] = lax.ppermute(backward[0], "dom", behind)
-        found.append((backward[0], step, 0))
         steps.append(found)
     last = [
-        (lax.ppermute(forward[1], "dom", ahead), chips // 2, 1),
-        (lax.ppermute(backward[0], "dom", behind), chips // 2, 0),
+        (lax.ppermute(forward[0], "dom", ahead), chips // 2, 0),
+        (lax.ppermute(backward[1], "dom", behind), chips // 2, 1),
     ]
     early = [(mine, 0, 0)] + [piece for found in steps for piece in found]
     sums = absorb(bundles, shape, early, None, chips)

time: 42.2 us -> 42.3 us (level)
    ppermute x3, starting transfers between devices: 1.89 us -> 6.46 us  [on_device(): forward[0] = lax.ppermute(forward[0], 'dom', ahead)]
    ppermute x3, starting transfers between devices: 6.29 us -> 1.79 us  [on_device(): backward[0] = lax.ppermute(backward[0], 'dom', behind)]
    ppermute x3, waiting for transfers between devices: 6.57 us -> 2.3 us  [on_device(): forward[0] = lax.ppermute(forward[0], 'dom', ahead)]
    ppermute x3, waiting for transfers between devices: 2.31 us -> 6.57 us  [on_device(): backward[0] = lax.ppermute(backward[0], 'dom', behind)]
    ppermute x3, starting transfers between devices: 3.91 us -> 0.35 us  [on_device(): lax.ppermute(backward[1], 'dom', swapped(behind) if step == 1 else behind)]
    ppermute x3, starting transfers between devices: 0.45 us -> 4.01 us  [on_device(): lax.ppermute(forward[1], 'dom', swapped(ahead) if step == 1 else ahead)]
where the time goes in v7:
time: 42.3 us; the launch traced here: 42.2 us
  starting transfers between devices  17.8 us (42%)
  waiting for transfers between devices  16.2 us (38%)
  Pallas kernels  7.26 us (17%)
  matrix products  0.7 us (2%)
    ppermute x3, waiting for transfers between devices, on_device(): backward[0] = lax.ppermute(backward[0], 'dom', behind)  6.57 us
    ppermute x3, starting transfers between devices, on_device(): forward[0] = lax.ppermute(forward[0], 'dom', ahead)  6.46 us
    ppermute x1, waiting for transfers between devices, on_device(): passing = lax.ppermute(other, 'rep', facing)  6.42 us
    ppermute x3, starting transfers between devices, on_device(): lax.ppermute(forward[1], 'dom', swapped(ahead) if step == 1 else ahead)  4.01 us
    ppermute x3, waiting for transfers between devices, on_device(): forward[0] = lax.ppermute(forward[0], 'dom', ahead)  2.3 us
    pallas_call x1, Pallas kernels, absorb(): pl.pallas_call(functools.partial(absorb_body, origins, local, slots, chip...  2.26 us
    pallas_call x1, Pallas kernels, pack(): pl.pallas_call(functools.partial(pack_body, devices // 2, local), out_sha...  1.81 us
    ppermute x3, starting transfers between devices, on_device(): backward[0] = lax.ppermute(backward[0], 'dom', behind)  1.79 us
  transfers between devices with their start and end apart: 19, of which 10 were waited for; matrix products, arithmetic and copies ran while one was open for 2% of the time, Pallas kernels for 9%

profile of v7, /device:TPU:0, one launch (start us, length us, event | category | flops | bytes accessed | tf_op | source)
XLA Modules:
  0.0 42.2 jit_solution(16723834524290995588)
XLA Ops:
  0.0 0.0 copy-start
  0.0 1.8 %pack.1 = (bf16[256,256]{1,0:T(8,128)(2,1)S(1)}, bf16[256,256]{1,0:T(8,128)(2,1)S(1)}, bf16[53,128,128]{2,1,0:T(8,128)(2,1)S(1)}) custom-call(bf16[256,1024]{1,0:T(8,128)(2,1)} %features.1, bf16[2,128,1024]{2,1,0:T(8,128)(2,1)} %bitcast.4, bf16[48,128,128]{2,1,0:T(8,128)(2,1)} %bitcast.5, s32[2,2,12]{2,1,0:T(2,128)} %columns_in.1, s32[2,2]{1,0:T(2,128)} %counts_in.1, ...), custom_call_target="tpu_custom_call" | custom-call | tf_op jit(solution)/shard_map/pack/pallas_call | solution.py:136
  1.8 0.5 %collective-permute-start = (bf16[53,128,128]{2,1,0:T(8,128)(2,1)S(1)}, bf16[53,128,128]{2,1,0:T(8,128)(2,1)S(1)}, u32[]{:S(2)}, u32[]{:S(2)}) collective-permute-start(bf16[53,128,128]{2,1,0:T(8,128)(2,1)S(1)} %get-tuple-element.10.refs_0_.bundle), channel_id=1, source_target_pairs={{0,2},{2,0},{4,6},{6,4},{8,10},{10,8},{12,14},{14,12},{16,18},{18,... | collective-permute-start | bytes 5210120 | tf_op jit(solution)/shard_map/ppermute | solution.py:335
  2.3 2.6 %collective-permute-start.1 = (bf16[256,256]{1,0:T(8,128)(2,1)S(1)}, bf16[256,256]{1,0:T(8,128)(2,1)S(1)}, u32[]{:S(2)}, u32[]{:S(2)}) collective-permute-start(bf16[256,256]{1,0:T(8,128)(2,1)S(1)} %get-tuple-element.11.refs_2_), channel_id=1, source_target_pairs={{0,8},{2,10},{4,0},{6,2},{8,16},{10,18},{12,4},{14,6},{16,24},{18,... | collective-permute-start | bytes 393224 | tf_op jit(solution)/shard_map/ppermute | solution.py:343
  5.0 0.0 collective-permute-start.4
  5.0 1.7 %collective-permute-start.2 = (bf16[256,256]{1,0:T(8,128)(2,1)S(1)}, bf16[256,256]{1,0:T(8,128)(2,1)S(1)}, u32[]{:S(2)}, u32[]{:S(2)}) collective-permute-start(bf16[256,256]{1,0:T(8,128)(2,1)S(1)} %get-tuple-element.11.refs_2_), channel_id=1, source_target_pairs={{0,4},{2,6},{4,12},{6,14},{8,0},{10,2},{12,20},{14,22},{16,8},{18,... | collective-permute-start | bytes 393224 | tf_op jit(solution)/shard_map/ppermute | solution.py:345
  6.7 0.0 collective-permute-start.3
  6.7 2.3 %collective-permute-done.1.refs_3_ = bf16[256,256]{1,0:T(8,128)(2,1)S(1)} collective-permute-done((bf16[256,256]{1,0:T(8,128)(2,1)S(1)}, bf16[256,256]{1,0:T(8,128)(2,1)S(1)}, u32[]{:S(2)}, u32[]{:S(2)}) %collective-permute-start.1) | collective-permute-done | bytes 131104 | tf_op jit(solution)/shard_map/ppermute | solution.py:343
  9.0 2.2 %collective-permute-start.5 = (bf16[256,256]{1,0:T(8,128)(2,1)S(1)}, bf16[256,256]{1,0:T(8,128)(2,1)S(1)}, u32[]{:S(2)}, u32[]{:S(2)}) collective-permute-start(bf16[256,256]{1,0:T(8,128)(2,1)S(1)} %collective-permute-done.1.refs_3_), channel_id=1, source_target_pairs={{0,8},{2,10},{4,0},{6,2},{8,16},{10,18},{12,4},{14,6},{16,24},{18,... | collective-permute-start | bytes 393224 | tf_op jit(solution)/shard_map/ppermute | solution.py:343
  11.3 0.0 collective-permute-done.4.refs_6_
  11.3 0.0 collective-permute-start.8
  11.3 2.3 %collective-permute-done.2.refs_4_ = bf16[256,256]{1,0:T(8,128)(2,1)S(1)} collective-permute-done((bf16[256,256]{1,0:T(8,128)(2,1)S(1)}, bf16[256,256]{1,0:T(8,128)(2,1)S(1)}, u32[]{:S(2)}, u32[]{:S(2)}) %collective-permute-start.2) | collective-permute-done | bytes 131104 | tf_op jit(solution)/shard_map/ppermute | solution.py:345
  13.6 0.1 collective-permute-start.6
  13.6 0.0 collective-permute-done.3.refs_5_
  13.6 2.0 %collective-permute-start.7 = (bf16[256,256]{1,0:T(8,128)(2,1)S(1)}, bf16[256,256]{1,0:T(8,128)(2,1)S(1)}, u32[]{:S(2)}, u32[]{:S(2)}) collective-permute-start(bf16[256,256]{1,0:T(8,128)(2,1)S(1)} %collective-permute-done.3.refs_5_), channel_id=1, source_target_pairs={{0,8},{2,10},{4,0},{6,2},{8,16},{10,18},{12,4},{14,6},{16,24},{18,... | collective-permute-start | bytes 393224 | tf_op jit(solution)/shard_map/ppermute | solution.py:347
  15.6 0.0 collective-permute-done.5.refs_7_
  15.6 1.6 %collective-permute-start.9 = (bf16[256,256]{1,0:T(8,128)(2,1)S(1)}, bf16[256,256]{1,0:T(8,128)(2,1)S(1)}, u32[]{:S(2)}, u32[]{:S(2)}) collective-permute-start(bf16[256,256]{1,0:T(8,128)(2,1)S(1)} %collective-permute-done.5.refs_7_), channel_id=1, source_target_pairs={{0,8},{2,10},{4,0},{6,2},{8,16},{10,18},{12,4},{14,6},{16,24},{18,... | collective-permute-start | bytes 393224 | tf_op jit(solution)/shard_map/ppermute | solution.py:343
  17.2 0.1 collective-permute-done.8.refs_10_
  17.3 0.3 collective-permute-start.12
  17.6 2.5 %collective-permute-done.6.refs_8_ = bf16[256,256]{1,0:T(8,128)(2,1)S(1)} collective-permute-done((bf16[256,256]{1,0:T(8,128)(2,1)S(1)}, bf16[256,256]{1,0:T(8,128)(2,1)S(1)}, u32[]{:S(2)}, u32[]{:S(2)}) %collective-permute-start.6) | collective-permute-done | bytes 131104 | tf_op jit(solution)/shard_map/ppermute | solution.py:345
  20.1 0.0 collective-permute-start.10
  20.1 0.0 collective-permute-done.7.refs_9_
  20.1 2.0 %collective-permute-start.11 = (bf16[256,256]{1,0:T(8,128)(2,1)S(1)}, bf16[256,256]{1,0:T(8,128)(2,1)S(1)}, u32[]{:S(2)}, u32[]{:S(2)}) collective-permute-start(bf16[256,256]{1,0:T(8,128)(2,1)S(1)} %collective-permute-done.7.refs_9_), channel_id=1, source_target_pairs={{0,8},{2,10},{4,0},{6,2},{8,16},{10,18},{12,4},{14,6},{16,24},{18,... | collective-permute-start | bytes 393224 | tf_op jit(solution)/shard_map/ppermute | solution.py:347
  22.1 0.0 collective-permute-done.9.refs_11_
  22.1 1.6 %collective-permute-start.13 = (bf16[256,256]{1,0:T(8,128)(2,1)S(1)}, bf16[256,256]{1,0:T(8,128)(2,1)S(1)}, u32[]{:S(2)}, u32[]{:S(2)}) collective-permute-start(bf16[256,256]{1,0:T(8,128)(2,1)S(1)} %collective-permute-done.9.refs_11_), channel_id=1, source_target_pairs={{0,8},{2,10},{4,0},{6,2},{8,16},{10,18},{12,4},{14,6},{16,24},{18,... | collective-permute-start | bytes 393224 | tf_op jit(solution)/shard_map/ppermute | solution.py:353
  23.7 0.0 collective-permute-done.12.refs_14_
  23.7 0.4 %collective-permute-start.14 = (bf16[256,256]{1,0:T(8,128)(2,1)S(1)}, bf16[256,256]{1,0:T(8,128)(2,1)S(1)}, u32[]{:S(2)}, u32[]{:S(2)}) collective-permute-start(bf16[256,256]{1,0:T(8,128)(2,1)S(1)} %collective-permute-done.12.refs_14_), channel_id=1, source_target_pairs={{0,4},{2,6},{4,12},{6,14},{8,0},{10,2},{12,20},{14,22},{16,8},{18,... | collective-permute-start | bytes 393224 | tf_op jit(solution)/shard_map/ppermute | solution.py:354
  24.2 1.8 %collective-permute-done.10.refs_12_ = bf16[256,256]{1,0:T(8,128)(2,1)S(1)} collective-permute-done((bf16[256,256]{1,0:T(8,128)(2,1)S(1)}, bf16[256,256]{1,0:T(8,128)(2,1)S(1)}, u32[]{:S(2)}, u32[]{:S(2)}) %collective-permute-start.10) | collective-permute-done | bytes 131104 | tf_op jit(solution)/shard_map/ppermute | solution.py:345
  26.0 0.1 collective-permute-done.11.refs_13_
  26.0 0.0 collective-permute-done.refs_1_.bundle
  26.0 2.3 %absorb.1.sums = f32[2,2,256,256]{3,2,1,0:T(8,128)S(1)} custom-call(bf16[53,128,128]{2,1,0:T(8,128)(2,1)S(1)} %get-tuple-element.10.refs_0_.bundle, bf16[53,128,128]{2,1,0:T(8,128)(2,1)S(1)} %collective-permute-done.refs_1_.bundle, bf16[256,256]{1,0:T(8,128)(2,1)S(1)} %get-tuple-element.11.refs_2_, bf16[256,256]{1,0:T(8,128)(2,1)S(1)} %collective-permute-done.1.refs_3_, ...), custom_call_target="tpu_custom_call" | custom-call | flops 1744830464 | tf_op jit(solution)/shard_map/absorb/pallas_call | solution.py:211
  28.3 0.0 collective-permute-done.13.refs_0_
  28.3 0.4 collective-permute-done.14.refs_1_
  28.7 0.4 close.3
  29.1 0.0 copy-start.3
  29.1 1.6 %collective-permute-start.15 = (bf16[2,256,256]{2,1,0:T(8,128)(2,1)S(1)}, bf16[2,256,256]{2,1,0:T(8,128)(2,1)S(1)}, u32[]{:S(2)}, u32[]{:S(2)}) collective-permute-start(bf16[2,256,256]{2,1,0:T(8,128)(2,1)S(1)} %close.3), channel_id=1, source_target_pairs={{0,1},{1,0},{2,3},{3,2},{4,5},{5,4},{6,7},{7,6},{8,9},{9,8},{10,11... | collective-permute-start | bytes 786440 | tf_op jit(solution)/shard_map/ppermute | solution.py:362
  30.7 0.0 copy-start.2
  30.7 0.4 close.2.refs_0_
  31.1 0.0 copy-start.1
  31.1 0.6 %collective-permute-start.18 = (bf16[2,256,256]{2,1,0:T(8,128)(2,1)S(1)}, bf16[2,256,256]{2,1,0:T(8,128)(2,1)S(1)}, u32[]{:S(2)}, u32[]{:S(2)}) collective-permute-start(bf16[2,256,256]{2,1,0:T(8,128)(2,1)S(1)} %close.2.refs_0_), channel_id=1, source_target_pairs={{0,1},{1,0},{2,3},{3,2},{4,5},{5,4},{6,7},{7,6},{8,9},{9,8},{10,11... | collective-permute-start | bytes 786440 | tf_op jit(solution)/shard_map/ppermute | solution.py:363
  31.7 6.4 %collective-permute-done.15 = bf16[2,256,256]{2,1,0:T(8,128)(2,1)S(1)} collective-permute-done((bf16[2,256,256]{2,1,0:T(8,128)(2,1)S(1)}, bf16[2,256,256]{2,1,0:T(8,128)(2,1)S(1)}, u32[]{:S(2)}, u32[]{:S(2)}) %collective-permute-start.15) | collective-permute-done | bytes 262176 | tf_op jit(solution)/shard_map/ppermute | solution.py:362
  38.1 0.0 collective-permute-start.16
  38.1 0.5 %collective-permute-start.17 = (bf16[2,256,256]{2,1,0:T(8,128)(2,1)S(1)}, bf16[2,256,256]{2,1,0:T(8,128)(2,1)S(1)}, u32[]{:S(2)}, u32[]{:S(2)}) collective-permute-start(bf16[2,256,256]{2,1,0:T(8,128)(2,1)S(1)} %collective-permute-done.15), channel_id=1, source_target_pairs={{0,2},{2,0},{4,6},{6,4},{8,10},{10,8},{12,14},{14,12},{16,18},{18,... | collective-permute-start | bytes 786440 | tf_op jit(solution)/shard_map/ppermute | solution.py:366
  38.6 0.0 copy-done
  38.6 0.0 copy-done.3
  38.6 0.7 %fusion.base = f32[256,1024]{1,0:T(8,128)S(1)} fusion(bf16[256,1024]{1,0:T(8,128)(2,1)S(1)} %copy-done.3, bf16[1024,1024]{1,0:T(8,128)(2,1)S(1)} %copy-done), kind=kOutput, calls=%fused_computation | convolution fusion | flops 536870912 | bytes 3670016 | tf_op jit(solution)/shard_map/dot_general | solution.py:368
  39.3 0.0 copy-done.2
  39.3 0.0 copy-done.1
  39.3 0.5 %project.2.base = f32[256,1024]{1,0:T(8,128)S(1)} custom-call(f32[256,1024]{1,0:T(8,128)S(1)} %fusion.base, bf16[1024,1024]{1,0:T(8,128)(2,1)S(1)} %copy-done.1, bf16[1024,1024]{1,0:T(8,128)(2,1)S(1)} %copy-done.2, bf16[2,256,256]{2,1,0:T(8,128)(2,1)S(1)} %close.2.refs_0_), custom_call_target="tpu_custom_call" | custom-call | flops 268435456 | tf_op jit(solution)/shard_map/project/pallas_call | solution.py:279
  39.8 0.0 collective-permute-done.16.refs_0_
  39.8 0.2 collective-permute-done.17.refs_1_
  40.0 0.7 %project.3.base = f32[256,1024]{1,0:T(8,128)S(1)} custom-call(f32[256,1024]{1,0:T(8,128)S(1)} %project.2.base, bf16[1024,1024]{1,0:T(8,128)(2,1)S(1)} %copy-done.1, bf16[1024,1024]{1,0:T(8,128)(2,1)S(1)} %copy-done.2, bf16[2,256,256]{2,1,0:T(8,128)(2,1)S(1)} %collective-permute-done.16.refs_0_, bf16[2,256,256]{2,1,0:T(8,128)(2,1)S(1)} %collective-permute-done.17.refs_1_), custom_call_target="tpu_custom_call" | custom-call | flops 536870912 | tf_op jit(solution)/shard_map/project/pallas_call | solution.py:279
  40.7 0.2 collective-permute-done.18.part
  40.9 1.2 %finish.1 = bf16[256,1024]{1,0:T(8,128)(2,1)} custom-call(f32[256,1024]{1,0:T(8,128)S(1)} %project.3.base, bf16[1024,1024]{1,0:T(8,128)(2,1)S(1)} %copy-done.1, bf16[1024,1024]{1,0:T(8,128)(2,1)S(1)} %copy-done.2, bf16[2,256,256]{2,1,0:T(8,128)(2,1)S(1)} %collective-permute-done.18.part), custom_call_target="tpu_custom_call" | custom-call | flops 134217728 | tf_op jit(solution)/shard_map/finish/pallas_call | solution.py:313
Async XLA Ops:
  0.0 38.6 %copy-start = (bf16[1024,1024]{1,0:T(8,128)(2,1)S(1)}, bf16[1024,1024]{1,0:T(8,128)(2,1)}, u32[]{:S(2)}) copy-start(bf16[1024,1024]{1,0:T(8,128)(2,1)} %param.13) | copy-start | bytes 6291460
  1.8 24.2 %collective-permute-start = (bf16[53,128,128]{2,1,0:T(8,128)(2,1)S(1)}, bf16[53,128,128]{2,1,0:T(8,128)(2,1)S(1)}, u32[]{:S(2)}, u32[]{:S(2)}) collective-permute-start(bf16[53,128,128]{2,1,0:T(8,128)(2,1)S(1)} %get-tuple-element.10.refs_0_.bundle), channel_id=1, source_target_pairs={{0,2},{2,0},{4,6},{6,4},{8,10},{10,8},{12,14},{14,12},{16,18},{18,... | collective-permute-start | bytes 5210120 | tf_op jit(solution)/shard_map/ppermute | solution.py:335
  2.3 6.7 %collective-permute-start.1 = (bf16[256,256]{1,0:T(8,128)(2,1)S(1)}, bf16[256,256]{1,0:T(8,128)(2,1)S(1)}, u32[]{:S(2)}, u32[]{:S(2)}) collective-permute-start(bf16[256,256]{1,0:T(8,128)(2,1)S(1)} %get-tuple-element.11.refs_2_), channel_id=1, source_target_pairs={{0,8},{2,10},{4,0},{6,2},{8,16},{10,18},{12,4},{14,6},{16,24},{18,... | collective-permute-start | bytes 393224 | tf_op jit(solution)/shard_map/ppermute | solution.py:343
  5.0 6.3 %collective-permute-start.4 = (bf16[256,256]{1,0:T(8,128)(2,1)S(1)}, bf16[256,256]{1,0:T(8,128)(2,1)S(1)}, u32[]{:S(2)}, u32[]{:S(2)}) collective-permute-start(bf16[256,256]{1,0:T(8,128)(2,1)S(1)} %get-tuple-element.12), channel_id=1, source_target_pairs={{0,6},{2,4},{4,14},{6,12},{8,2},{10,0},{12,22},{14,20},{16,10},{18... | collective-permute-start | bytes 393224 | tf_op jit(solution)/shard_map/ppermute | solution.py:349
  5.0 8.6 %collective-permute-start.2 = (bf16[256,256]{1,0:T(8,128)(2,1)S(1)}, bf16[256,256]{1,0:T(8,128)(2,1)S(1)}, u32[]{:S(2)}, u32[]{:S(2)}) collective-permute-start(bf16[256,256]{1,0:T(8,128)(2,1)S(1)} %get-tuple-element.11.refs_2_), channel_id=1, source_target_pairs={{0,4},{2,6},{4,12},{6,14},{8,0},{10,2},{12,20},{14,22},{16,8},{18,... | collective-permute-start | bytes 393224 | tf_op jit(solution)/shard_map/ppermute | solution.py:345
  6.7 6.9 %collective-permute-start.3 = (bf16[256,256]{1,0:T(8,128)(2,1)S(1)}, bf16[256,256]{1,0:T(8,128)(2,1)S(1)}, u32[]{:S(2)}, u32[]{:S(2)}) collective-permute-start(bf16[256,256]{1,0:T(8,128)(2,1)S(1)} %get-tuple-element.12), channel_id=1, source_target_pairs={{0,10},{2,8},{4,2},{6,0},{8,18},{10,16},{12,6},{14,4},{16,26},{18,... | collective-permute-start | bytes 393224 | tf_op jit(solution)/shard_map/ppermute | solution.py:347
  9.0 6.6 %collective-permute-start.5 = (bf16[256,256]{1,0:T(8,128)(2,1)S(1)}, bf16[256,256]{1,0:T(8,128)(2,1)S(1)}, u32[]{:S(2)}, u32[]{:S(2)}) collective-permute-start(bf16[256,256]{1,0:T(8,128)(2,1)S(1)} %collective-permute-done.1.refs_3_), channel_id=1, source_target_pairs={{0,8},{2,10},{4,0},{6,2},{8,16},{10,18},{12,4},{14,6},{16,24},{18,... | collective-permute-start | bytes 393224 | tf_op jit(solution)/shard_map/ppermute | solution.py:343
  11.3 6.0 %collective-permute-start.8 = (bf16[256,256]{1,0:T(8,128)(2,1)S(1)}, bf16[256,256]{1,0:T(8,128)(2,1)S(1)}, u32[]{:S(2)}, u32[]{:S(2)}) collective-permute-start(bf16[256,256]{1,0:T(8,128)(2,1)S(1)} %collective-permute-done.4.refs_6_), channel_id=1, source_target_pairs={{0,4},{2,6},{4,12},{6,14},{8,0},{10,2},{12,20},{14,22},{16,8},{18,... | collective-permute-start | bytes 393224 | tf_op jit(solution)/shard_map/ppermute | solution.py:349
  13.6 6.5 %collective-permute-start.6 = (bf16[256,256]{1,0:T(8,128)(2,1)S(1)}, bf16[256,256]{1,0:T(8,128)(2,1)S(1)}, u32[]{:S(2)}, u32[]{:S(2)}) collective-permute-start(bf16[256,256]{1,0:T(8,128)(2,1)S(1)} %collective-permute-done.2.refs_4_), channel_id=1, source_target_pairs={{0,4},{2,6},{4,12},{6,14},{8,0},{10,2},{12,20},{14,22},{16,8},{18,... | collective-permute-start | bytes 393224 | tf_op jit(solution)/shard_map/ppermute | solution.py:345
  13.6 6.5 %collective-permute-start.7 = (bf16[256,256]{1,0:T(8,128)(2,1)S(1)}, bf16[256,256]{1,0:T(8,128)(2,1)S(1)}, u32[]{:S(2)}, u32[]{:S(2)}) collective-permute-start(bf16[256,256]{1,0:T(8,128)(2,1)S(1)} %collective-permute-done.3.refs_5_), channel_id=1, source_target_pairs={{0,8},{2,10},{4,0},{6,2},{8,16},{10,18},{12,4},{14,6},{16,24},{18,... | collective-permute-start | bytes 393224 | tf_op jit(solution)/shard_map/ppermute | solution.py:347
  15.6 6.5 %collective-permute-start.9 = (bf16[256,256]{1,0:T(8,128)(2,1)S(1)}, bf16[256,256]{1,0:T(8,128)(2,1)S(1)}, u32[]{:S(2)}, u32[]{:S(2)}) collective-permute-start(bf16[256,256]{1,0:T(8,128)(2,1)S(1)} %collective-permute-done.5.refs_7_), channel_id=1, source_target_pairs={{0,8},{2,10},{4,0},{6,2},{8,16},{10,18},{12,4},{14,6},{16,24},{18,... | collective-permute-start | bytes 393224 | tf_op jit(solution)/shard_map/ppermute | solution.py:343
  17.3 6.4 %collective-permute-start.12 = (bf16[256,256]{1,0:T(8,128)(2,1)S(1)}, bf16[256,256]{1,0:T(8,128)(2,1)S(1)}, u32[]{:S(2)}, u32[]{:S(2)}) collective-permute-start(bf16[256,256]{1,0:T(8,128)(2,1)S(1)} %collective-permute-done.8.refs_10_), channel_id=1, source_target_pairs={{0,4},{2,6},{4,12},{6,14},{8,0},{10,2},{12,20},{14,22},{16,8},{18,... | collective-permute-start | bytes 393224 | tf_op jit(solution)/shard_map/ppermute | solution.py:349
  20.1 5.9 %collective-permute-start.10 = (bf16[256,256]{1,0:T(8,128)(2,1)S(1)}, bf16[256,256]{1,0:T(8,128)(2,1)S(1)}, u32[]{:S(2)}, u32[]{:S(2)}) collective-permute-start(bf16[256,256]{1,0:T(8,128)(2,1)S(1)} %collective-permute-done.6.refs_8_), channel_id=1, source_target_pairs={{0,4},{2,6},{4,12},{6,14},{8,0},{10,2},{12,20},{14,22},{16,8},{18,... | collective-permute-start | bytes 393224 | tf_op jit(solution)/shard_map/ppermute | solution.py:345
  20.1 5.9 %collective-permute-start.11 = (bf16[256,256]{1,0:T(8,128)(2,1)S(1)}, bf16[256,256]{1,0:T(8,128)(2,1)S(1)}, u32[]{:S(2)}, u32[]{:S(2)}) collective-permute-start(bf16[256,256]{1,0:T(8,128)(2,1)S(1)} %collective-permute-done.7.refs_9_), channel_id=1, source_target_pairs={{0,8},{2,10},{4,0},{6,2},{8,16},{10,18},{12,4},{14,6},{16,24},{18,... | collective-permute-start | bytes 393224 | tf_op jit(solution)/shard_map/ppermute | solution.py:347
  22.1 6.2 %collective-permute-start.13 = (bf16[256,256]{1,0:T(8,128)(2,1)S(1)}, bf16[256,256]{1,0:T(8,128)(2,1)S(1)}, u32[]{:S(2)}, u32[]{:S(2)}) collective-permute-start(bf16[256,256]{1,0:T(8,128)(2,1)S(1)} %collective-permute-done.9.refs_11_), channel_id=1, source_target_pairs={{0,8},{2,10},{4,0},{6,2},{8,16},{10,18},{12,4},{14,6},{16,24},{18,... | collective-permute-start | bytes 393224 | tf_op jit(solution)/shard_map/ppermute | solution.py:353
  23.7 5.0 %collective-permute-start.14 = (bf16[256,256]{1,0:T(8,128)(2,1)S(1)}, bf16[256,256]{1,0:T(8,128)(2,1)S(1)}, u32[]{:S(2)}, u32[]{:S(2)}) collective-permute-start(bf16[256,256]{1,0:T(8,128)(2,1)S(1)} %collective-permute-done.12.refs_14_), channel_id=1, source_target_pairs={{0,4},{2,6},{4,12},{6,14},{8,0},{10,2},{12,20},{14,22},{16,8},{18,... | collective-permute-start | bytes 393224 | tf_op jit(solution)/shard_map/ppermute | solution.py:354
  29.1 9.5 %copy-start.3 = (bf16[256,1024]{1,0:T(8,128)(2,1)S(1)}, bf16[256,1024]{1,0:T(8,128)(2,1)}, u32[]{:S(2)}) copy-start(bf16[256,1024]{1,0:T(8,128)(2,1)} %features.1) | copy-start | bytes 1572868
  29.1 9.0 %collective-permute-start.15 = (bf16[2,256,256]{2,1,0:T(8,128)(2,1)S(1)}, bf16[2,256,256]{2,1,0:T(8,128)(2,1)S(1)}, u32[]{:S(2)}, u32[]{:S(2)}) collective-permute-start(bf16[2,256,256]{2,1,0:T(8,128)(2,1)S(1)} %close.3), channel_id=1, source_target_pairs={{0,1},{1,0},{2,3},{3,2},{4,5},{5,4},{6,7},{7,6},{8,9},{9,8},{10,11... | collective-permute-start | bytes 786440 | tf_op jit(solution)/shard_map/ppermute | solution.py:362
  30.7 8.7 %copy-start.2 = (bf16[1024,1024]{1,0:T(8,128)(2,1)S(1)}, bf16[1024,1024]{1,0:T(8,128)(2,1)}, u32[]{:S(2)}) copy-start(bf16[1024,1024]{1,0:T(8,128)(2,1)} %w_out.5) | copy-start | bytes 6291460
  31.1 8.3 %copy-start.1 = (bf16[1024,1024]{1,0:T(8,128)(2,1)S(1)}, bf16[1024,1024]{1,0:T(8,128)(2,1)}, u32[]{:S(2)}) copy-start(bf16[1024,1024]{1,0:T(8,128)(2,1)} %w_in.5) | copy-start | bytes 6291460
  31.1 9.8 %collective-permute-start.18 = (bf16[2,256,256]{2,1,0:T(8,128)(2,1)S(1)}, bf16[2,256,256]{2,1,0:T(8,128)(2,1)S(1)}, u32[]{:S(2)}, u32[]{:S(2)}) collective-permute-start(bf16[2,256,256]{2,1,0:T(8,128)(2,1)S(1)} %close.2.refs_0_), channel_id=1, source_target_pairs={{0,1},{1,0},{2,3},{3,2},{4,5},{5,4},{6,7},{7,6},{8,9},{9,8},{10,11... | collective-permute-start | bytes 786440 | tf_op jit(solution)/shard_map/ppermute | solution.py:363
  38.1 1.7 %collective-permute-start.16 = (bf16[2,256,256]{2,1,0:T(8,128)(2,1)S(1)}, bf16[2,256,256]{2,1,0:T(8,128)(2,1)S(1)}, u32[]{:S(2)}, u32[]{:S(2)}) collective-permute-start(bf16[2,256,256]{2,1,0:T(8,128)(2,1)S(1)} %close.3), channel_id=1, source_target_pairs={{0,2},{2,0},{4,6},{6,4},{8,10},{10,8},{12,14},{14,12},{16,18},{18,... | collective-permute-start | bytes 786440 | tf_op jit(solution)/shard_map/ppermute | solution.py:365
  38.1 1.9 %collective-permute-start.17 = (bf16[2,256,256]{2,1,0:T(8,128)(2,1)S(1)}, bf16[2,256,256]{2,1,0:T(8,128)(2,1)S(1)}, u32[]{:S(2)}, u32[]{:S(2)}) collective-permute-start(bf16[2,256,256]{2,1,0:T(8,128)(2,1)S(1)} %collective-permute-done.15), channel_id=1, source_target_pairs={{0,2},{2,0},{4,6},{6,4},{8,10},{10,8},{12,14},{14,12},{16,18},{18,... | collective-permute-start | bytes 786440 | tf_op jit(solution)/shard_map/ppermute | solution.py:366
